TPU v7x, 128 devices: a whole 4x4x4 slice. The times are simulated.
128 devices in a mesh: row: 8 (over z, x_hi), col: 16 (over x_lo, y, core).
Axes of the slice: x: 4 (x_hi: 2, x_lo: 2; x = x_hi * 2 + x_lo), y: 4, z: 4, core: 2. Of those that a mesh axis runs over, the one named last changes fastest.
Arguments:
- factor: float32 [16384, 16384], P(('row', 'col')), as said below
- damping: float32 [16384], P(('row', 'col')), may hold values from 0.1 to 1
- gradients: float32 [3072, 128], replicated, may hold values from -6 to 6
- inverses: float32 [5, 512, 512], replicated, as said below
Outputs:
- updated: float32 [8, 8, 256, 4, 16, 256], P(None, 'row', None, None, 'col')
- panel_tiles: float32 [8, 8, 256, 512], P(None, 'row', 'col')
- solution: float32 [3072, 128], replicated
Inputs may be any that keep to these rules, and one draw needn't show every extreme that they name: `factor`: symmetric. `inverses`: one matrix for each diagonal block after the first.
All inputs are finite; a program needn't handle non-finite values.
Results may differ from a plain program's by a relative error of at most 0.0001.
Values sent between devices are 32-bit elements; how exact they have to be, the bound alone decides.
No kernel may reach another device: no remote copies, remote signals or barrier semaphores. Data moves between devices by JAX's collectives and lax.ppermute only.
A program may use at most 128 MiB of HBM per device.

v0:
```python
import jax
import jax.numpy as jnp
from jax import lax
from jax.sharding import PartitionSpec as P


def spread_2(block, axis, source):
    block = jnp.where(lax.axis_index(axis) == source, block, jnp.zeros_like(block))
    return lax.psum(block, axis)


def right_solve(corner_factor, panel_rows):
    return jax.scipy.linalg.solve_triangular(corner_factor, panel_rows.T, lower=True).T


def exact_dot(left, right):
    return jnp.dot(left, right, precision=lax.Precision.HIGHEST, preferred_element_type=jnp.float32)


def locate(block_index, position, axis_count, tile_size, block_width):
    piece_width = min(tile_size, block_width)
    pieces = block_width // piece_width
    first_tile = block_index * block_width // tile_size
    offset = block_index * block_width % tile_size
    turn_index = (position - first_tile) % axis_count
    is_valid = turn_index < pieces
    local_start = (first_tile + turn_index) // axis_count * tile_size + offset
    return (local_start, turn_index * piece_width, is_valid)


def place(segment, place_at, block_width, axis_dim):
    extent = list(segment.shape)
    extent[axis_dim] = block_width + segment.shape[axis_dim]
    buffer = jnp.zeros(tuple(extent), segment.dtype)
    filled = lax.dynamic_update_slice_in_dim(buffer, segment, place_at, axis_dim)
    return lax.slice_in_dim(filled, 0, block_width, axis=axis_dim)


def body(factor, damping, gradients, inverses):
    row_count = lax.axis_size("row")
    col_count = lax.axis_size("col")
    part_rows, order_size = factor.shape
    panel_width = inverses.shape[1]
    tile_size = order_size // (row_count * row_count)
    col_tiles = order_size // (col_count * tile_size)
    local_cols = col_tiles * tile_size
    local_rows = row_count * tile_size
    piece_width = min(tile_size, panel_width)
    share_rows = tile_size // col_count
    lead_share = panel_width // col_count
    row_index = lax.axis_index("row")
    col_index = lax.axis_index("col")
    first_col = (row_index * col_count + col_index) * part_rows
    square = lax.dynamic_slice_in_dim(factor, first_col, part_rows, 1) + jnp.diag(damping)
    damped = lax.dynamic_update_slice_in_dim(factor, square, first_col, 1)
    arranged = damped.reshape(part_rows, col_tiles, col_count, tile_size).transpose(2, 0, 1, 3)
    arranged = arranged.reshape(col_count, part_rows, local_cols)
    carried = None
    spread = lax.all_to_all(arranged, "col", split_axis=0, concat_axis=1, tiled=True)
    landed = lax.all_to_all(spread, "row", split_axis=1, concat_axis=0, tiled=True)
    local_block = landed.reshape(local_rows, local_cols)
    row_start, row_place, row_valid = locate(0, row_index, row_count, tile_size, panel_width)
    col_start, col_place, col_valid = locate(0, col_index, col_count, tile_size, panel_width)
    col_piece = lax.dynamic_slice_in_dim(local_block, col_start, piece_width, 1) * col_valid.astype(
        jnp.float32
    )
    contrib = place(col_piece, col_place, panel_width, 1)
    corner_piece = lax.dynamic_slice_in_dim(contrib, row_start, piece_width, 0) * row_valid.astype(
        jnp.float32
    )
    corner = lax.psum(place(corner_piece, row_place, panel_width, 0), ("row", "col"))
    corner_factor = jnp.linalg.cholesky(corner)
    panel_rows = lax.psum(contrib, "col")
    factor_rows = right_solve(corner_factor, panel_rows)
    own_factor = lax.dynamic_slice_in_dim(
        factor_rows.reshape(row_count, tile_size, panel_width),
        col_index * share_rows,
        share_rows,
        1,
    )
    grouped = factor_rows.reshape(col_tiles, col_count // row_count, tile_size, panel_width)
    picked = lax.dynamic_index_in_dim(grouped, col_index // row_count, 1, keepdims=False)
    picked = picked.reshape(local_cols, panel_width)
    factor_cols = spread_2(picked, "row", col_index % row_count)
    outer_part = lax.dot_general(
        factor_rows,
        factor_cols,
        (((1,), (1,)), ((), ())),
        precision=lax.Precision.HIGHEST,
        preferred_element_type=jnp.float32,
    )
    trailing = local_block - outer_part
    block_count = gradients.shape[0] // panel_width
    first_block = jax.scipy.linalg.solve_triangular(
        corner_factor, gradients[:panel_width], lower=True
    )
    solved = [first_block]
    known_cols = jnp.zeros((local_cols, gradients.shape[1]), jnp.float32)
    lead_start = col_index * lead_share
    first_share = lax.dynamic_slice_in_dim(first_block, lead_start, lead_share, 0)
    for block_index in range(1, block_count):
        if block_index > 1:
            put_start, put_place, put_valid = locate(
                block_index - 1, col_index, col_count, tile_size, panel_width
            )
            segment = lax.dynamic_slice_in_dim(solved[-1], put_place, piece_width, 0)
            current = lax.dynamic_slice_in_dim(known_cols, put_start, piece_width, 0)
            known_cols = lax.dynamic_update_slice_in_dim(
                known_cols, jnp.where(put_valid, segment, current), put_start, 0
            )
        block_start, block_place, block_valid = locate(
            block_index, row_index, row_count, tile_size, panel_width
        )
        lead_rows = lax.dynamic_slice_in_dim(factor_rows, block_start, piece_width, 0)
        lead_part = lax.dynamic_slice_in_dim(lead_rows, lead_start, lead_share, 1)
        partial_value = exact_dot(lead_part, first_share)
        if block_index > 1:
            schur_rows = lax.dynamic_slice_in_dim(trailing, block_start, piece_width, 0)
            partial_value = partial_value + exact_dot(schur_rows, known_cols)
        partial_value = partial_value * block_valid.astype(jnp.float32)
        summed = lax.psum(place(partial_value, block_place, panel_width, 0), ("row", "col"))
        right_side = gradients[block_index * panel_width : (block_index + 1) * panel_width]
        solved.append(exact_dot(inverses[block_index - 1], right_side - summed))
    solution = jnp.concatenate(solved, axis=0)
    updated = trailing.reshape(row_count, 1, tile_size, col_tiles, 1, tile_size)
    panel_tiles = own_factor.reshape(row_count, 1, share_rows, panel_width)
    return (updated, panel_tiles, solution)


def solution(mesh):
    return jax.shard_map(
        body,
        mesh=mesh,
        in_specs=(P(("row", "col"), None), P(("row", "col")), P(), P()),
        out_specs=(P(None, "row", None, None, "col", None), P(None, "row", "col", None), P()),
        check_vma=False,
    )
```

profile of v0, /device:TPU:1, one launch (start us, length us, event | category | flops | bytes accessed | tf_op | source)
XLA Modules:
  0.0 1456.4 jit_solution(4369769002759106836)
XLA Ops:
  7.2 7.6 copy.88
  16.3 9.2 copy.41
  25.5 10.0 copy.27
  35.5 100.9 %all_to_all.21 = f32[16,128,1024]{1,2,0:T(8,128)} all-to-all(f32[16,128,1024]{1,2,0:T(8,128)} %bitcast.143), channel_id=1, replica_groups=mesh['row'=8,'col'=16] {'col'}, dimensions={0} | all-to-all | bytes 16777216 | tf_op jit(solution)/shard_map/all_to_all | solution.py:59
  136.5 9.2 copy.28
  145.7 10.8 copy.29
  156.5 7.2 all-to-all-start.1
  163.9 94.4 %all-to-all-done.1 = f32[1,2048,1024]{2,0,1:T(1,128)} async-done(((f32[1,2048,1024]{2,0,1:T(1,128)}), f32[1,2048,1024]{2,0,1:T(1,128)}, u32[]{:S(2)}, u32[]{:S(2)}) %all-to-all-start.1) | async-done | bytes 8388640 | tf_op jit(solution)/shard_map/all_to_all | solution.py:60
  258.3 4.4 constant_dynamic-slice_fusion.2
  262.7 4.6 copy.40
  273.2 145.4 %all-reduce.10.cloned.1.call-done = f32[512,512]{0,1:T(8,128)} async-done(((f32[512,512]{0,1:T(8,128)}), f32[512,512]{0,1:T(8,128)}) %all-reduce.10.cloned.1.call-update) | async-done | bytes 1048592 | tf_op jit(solution)/shard_map/psum | solution.py:71
  421.6 11.7 cholesky.85
  433.5 9.8 custom-call.34
  444.0 11.7 cholesky.180
  455.7 10.2 custom-call.35
  466.6 11.7 cholesky.201
  478.3 9.8 custom-call.36
  488.7 11.7 cholesky.218
  505.3 10.4 while.1
  515.7 40.1 %custom-call.37 = f32[4,128,128]{1,2,0:T(8,128)S(1)} custom-call(f32[4,128,128]{2,1,0:T(8,128)} %get-tuple-element.10), custom_call_target="InvertDiagBlocksLowerTriangular" | custom-call | tf_op jit(solution)/shard_map/jit(_solve_triangular)/triangular_solve | solution.py:13
  573.1 4.4 pad_maximum_fusion
  577.4 6.6 reshape.97
  586.5 8.8 fusion.9
  600.7 6.1 copy.43
  608.1 119.9 %all-reduce.16.cloned.1.call-done = f32[512,128]{1,0:T(8,128)} async-done(((f32[512,128]{1,0:T(8,128)}), f32[512,128]{1,0:T(8,128)}) %all-reduce.16.cloned.1.call-update) | async-done | bytes 262160 | tf_op jit(solution)/shard_map/psum | solution.py:121
  731.4 102.9 %all-reduce.14.cloned.1.call-done = f32[1024,512]{0,1:T(8,128)} async-done(((f32[1024,512]{0,1:T(8,128)}), f32[1024,512]{0,1:T(8,128)}) %all-reduce.14.cloned.1.call-update) | async-done | bytes 2097168 | tf_op jit(solution)/shard_map/psum | solution.py:9
  834.3 20.1 %bitcast_subtract_fusion = f32[2048,1024]{1,0:T(8,128)S(1)} fusion(f32[1,2048,1024]{2,0,1:T(1,128)} %all-to-all-done.1, f32[1024,512]{0,1:T(8,128)} %all-reduce.14.cloned.1.call-done, f32[128,2048]{1,0:T(8,128)} %copy-done.2, f32[128,2048]{1,0:T(8,128)} %copy-done.1, f32[128,2048]{1,0:T(8,128)S(1)} %fusion.83, f32[128,2048]{1,0:T(8,128)S(1)} %fusion.23), kind=kOutput, calls=%fused_computation.2 | convolution fusion | flops 12890144768 | bytes 23068672 | tf_op jit(solution)/shard_map/dot_general | solution.py:85
  860.7 141.0 %all-reduce.18.cloned.1.call-done = f32[512,128]{1,0:T(8,128)} async-done(((f32[512,128]{1,0:T(8,128)}), f32[512,128]{1,0:T(8,128)}) %all-reduce.18.cloned.1.call-update) | async-done | bytes 262160 | tf_op jit(solution)/shard_map/psum | solution.py:121
  1009.7 139.1 %all-reduce.20.cloned.1.call-done = f32[512,128]{1,0:T(8,128)} async-done(((f32[512,128]{1,0:T(8,128)}), f32[512,128]{1,0:T(8,128)}) %all-reduce.20.cloned.1.call-update) | async-done | bytes 262160 | tf_op jit(solution)/shard_map/psum | solution.py:121
  1156.5 139.3 %all-reduce.22.cloned.1.call-done = f32[512,128]{1,0:T(8,128)} async-done(((f32[512,128]{1,0:T(8,128)}), f32[512,128]{1,0:T(8,128)}) %all-reduce.22.cloned.1.call-update) | async-done | bytes 262160 | tf_op jit(solution)/shard_map/psum | solution.py:121
  1305.8 13.5 reshape.120
  1319.3 123.6 %all-reduce.24.cloned.1.call-done = f32[512,128]{1,0:T(8,128)} async-done(((f32[512,128]{1,0:T(8,128)}), f32[512,128]{1,0:T(8,128)}) %all-reduce.24.cloned.1.call-update) | async-done | bytes 262160 | tf_op jit(solution)/shard_map/psum | solution.py:121
  (133 shorter events, 92.5 us)
Async XLA Ops:
  7.2 7.6 copy-start.8
  156.5 101.7 %all-to-all-start.1 = ((f32[1,2048,1024]{2,0,1:T(1,128)}), f32[1,2048,1024]{2,0,1:T(1,128)}, u32[]{:S(2)}, u32[]{:S(2)}) async-start(f32[1,2048,1024]{2,0,1:T(1,128)} %copy.29), calls=%async_computation.1 | async-start | bytes 16777216 | tf_op jit(solution)/shard_map/all_to_all | solution.py:60
  163.7 254.8 %all-reduce.10.cloned.1.call-start = ((), (), s32[]{:S(2)}) async-start(), calls=%async_computation.2 | async-start | bytes 2097152 | tf_op jit(solution)/shard_map/psum | solution.py:71
  272.2 289.7 %all-reduce.12.cloned.1.call-start = ((), (), s32[]{:S(2)}) async-start(), calls=%async_computation.3 | async-start | bytes 8388608 | tf_op jit(solution)/shard_map/psum | solution.py:73
  272.9 455.0 %all-reduce.16.cloned.1.call-start = ((), (), s32[]{:S(2)}) async-start(), calls=%async_computation.5 | async-start | bytes 524288 | tf_op jit(solution)/shard_map/psum | solution.py:121
  559.7 1.5 copy-start.4
  561.2 0.6 copy-start.6
  561.9 5.7 copy-start.3
  569.9 7.5 copy-start.1
  573.0 4.4 copy-start.2
  586.1 248.2 %all-reduce.14.cloned.1.call-start = ((), (), s32[]{:S(2)}) async-start(), calls=%async_computation.4 | async-start | bytes 4194304 | tf_op jit(solution)/shard_map/psum | solution.py:9
  595.3 2.5 copy-start.5
  595.4 2.6 copy-start.7
  597.2 404.5 %all-reduce.18.cloned.1.call-start = ((), (), s32[]{:S(2)}) async-start(), calls=%async_computation.6 | async-start | bytes 524288 | tf_op jit(solution)/shard_map/psum | solution.py:121
  854.4 3.2 copy-start
  859.4 289.4 %all-reduce.20.cloned.1.call-start = ((), (), s32[]{:S(2)}) async-start(), calls=%async_computation.7 | async-start | bytes 524288 | tf_op jit(solution)/shard_map/psum | solution.py:121
  1008.1 287.7 %all-reduce.22.cloned.1.call-start = ((), (), s32[]{:S(2)}) async-start(), calls=%async_computation.8 | async-start | bytes 524288 | tf_op jit(solution)/shard_map/psum | solution.py:121
  1155.2 287.8 %all-reduce.24.cloned.1.call-start = ((), (), s32[]{:S(2)}) async-start(), calls=%async_computation.9 | async-start | bytes 524288 | tf_op jit(solution)/shard_map/psum | solution.py:121
Sparse Core Ops, SparseCore 0:
  272.3 146.2 all-reduce.9
  421.7 128.5 all-reduce.11
  586.2 141.7 all-reduce.15
  730.3 103.9 all-reduce.13
  859.5 142.1 all-reduce.17
  1008.2 140.4 all-reduce.19
  1155.3 140.4 all-reduce.21
  1302.3 140.5 all-reduce.23
where the time goes:
time: 1460 us
  waiting for transfers between devices  1010 us (69%)
  other arithmetic  136 us (9%)
  local copies, waits for them, and re-layouts  118 us (8%)
  blocking collectives  101 us (7%)
  matrix products  69.3 us (5%)
  between operations  18.1 us (1%)
    psum x5, waiting for transfers between devices, body(): lax.psum(place(partial_value, block_place, panel_width, 0), ('row', 'col'))  663 us
    psum x1, waiting for transfers between devices, body(): lax.psum(place(corner_piece, row_place, panel_width, 0), ('row', 'col'))  145 us
    psum x1, waiting for transfers between devices, spread_2(): return lax.psum(block, axis)  103 us
    all_to_all x1, blocking collectives, body(): lax.all_to_all(arranged, 'col', split_axis=0, concat_axis=1, tiled=True)  101 us
    all_to_all x1, waiting for transfers between devices, body(): lax.all_to_all(spread, 'row', split_axis=1, concat_axis=0, tiled=True)  94.4 us
    another operation x14, other arithmetic, body(): corner_factor = jnp.linalg.cholesky(corner)  78.7 us
    another operation x4, other arithmetic, right_solve(): jax.scipy.linalg.solve_triangular(corner_factor, panel_rows.T, lower=True)  44.6 us
    unnamed x28, local copies, waits for them, and re-layouts  38.7 us
  transfers between devices with their start and end apart: 9, of which 8 were waited for; matrix products, arithmetic and copies ran while one was open for 13% of the time, Pallas kernels for 0%

commit v1 on v0

v1 whole, which is shorter than its diff:
```python
import functools

import jax
import jax.numpy as jnp
from jax import lax
from jax.experimental import pallas as pl
from jax.experimental.pallas import tpu as pltpu
from jax.sharding import Mesh
from jax.sharding import PartitionSpec as P


INTERPRET = False
CHUNKS = 2
FIRST_STEPS = 1
ALL = ("z", "xh", "xl", "y", "core")
VMEM = pl.BlockSpec(memory_space=pltpu.VMEM)
SMEM = pl.BlockSpec(memory_space=pltpu.SMEM)
ANY = pl.BlockSpec(memory_space=pl.ANY)
F32 = jnp.float32


def shape(*dims):
    return jax.ShapeDtypeStruct(dims, F32)


def dot(left, right, dims):
    return lax.dot_general(
        left, right, (dims, ((), ())), precision=lax.Precision.HIGHEST, preferred_element_type=F32
    )


def halves(value):
    high = value.astype(jnp.bfloat16)
    return high, (value - high.astype(F32)).astype(jnp.bfloat16)


def dot3(left, right, dims):
    one = lambda a, b: lax.dot_general(a, b, (dims, ((), ())), preferred_element_type=F32)
    return one(left[0], right[0]) + (one(left[0], right[1]) + one(left[1], right[0]))


NN = ((1,), (0,))
NT = ((1,), (1,))
TN = ((0,), (0,))


def device_of(z, xh, xl, y, core):
    return (((z * 2 + xh) * 2 + xl) * 4 + y) * 2 + core


def every():
    return [
        (z, xh, xl, y, core)
        for z in range(4)
        for xh in range(2)
        for xl in range(2)
        for y in range(4)
        for core in range(2)
    ]


def swap(value, dz=0, dx=0, dy=0, dcore=0, only=None):
    pairs = []
    for z, xh, xl, y, core in every():
        if only is None or only(z, xh * 2 + xl, y, core):
            to = (z ^ dz, xh ^ (dx >> 1), xl ^ (dx & 1), y ^ dy, core ^ dcore)
            pairs.append((device_of(z, xh, xl, y, core), device_of(*to)))
    return lax.ppermute(value, ALL, pairs)


def factor_block(block):
    size = block.shape[0]
    lane = lax.broadcasted_iota(jnp.int32, (8, size), 1)
    sub = lax.broadcasted_iota(jnp.int32, (8, size), 0)
    left = [block[8 * i : 8 * i + 8, :] for i in range(size // 8)]
    right = [jnp.where(lane == sub + 8 * i, 1.0, 0.0).astype(F32) for i in range(size // 8)]
    for k in range(size - 1):
        b, s = divmod(k, 8)
        inverse = 1.0 / left[b][s : s + 1, k : k + 1]
        left_row = jnp.broadcast_to(left[b][s : s + 1, :] * inverse, (8, size))
        right_row = jnp.broadcast_to(right[b][s : s + 1, :] * inverse, (8, size))
        for i in range(b if s < 7 else b + 1, size // 8):
            col = jnp.broadcast_to(left[i][:, k : k + 1], (8, size))
            if i == b:
                col = jnp.where(sub > s, col, 0.0)
            left[i] = left[i] - col * left_row
            right[i] = right[i] - col * right_row
    rows = []
    for i in range(size // 8):
        pivot = jnp.sum(jnp.where(lane == sub + 8 * i, left[i], 0.0), axis=1, keepdims=True)
        rows.append(right[i] * (1.0 / jnp.sqrt(pivot)))
    return jnp.concatenate(rows, axis=0)


def eliminate(w_ref, x_ref, low_step, high_step):
    n = x_ref.shape[0]
    nb = n // 4

    def step(j, carry):
        at = pl.multiple_of(j * nb, nb)
        xj = factor_block(w_ref[pl.ds(at, nb), pl.ds(at, nb)])
        low = dot(w_ref[:, pl.ds(at, nb)], xj, NT)
        rows = lax.broadcasted_iota(jnp.int32, (n, nb), 0)
        low = jnp.where(rows >= at + nb, low, 0.0)
        w_ref[...] = w_ref[...] - dot(low, low, NT)
        xr = dot(xj, x_ref[pl.ds(at, nb), :], NN)
        x_ref[pl.ds(at, nb), :] = xr
        x_ref[...] = x_ref[...] - dot(low, xr, NN)
        return carry

    lax.fori_loop(low_step, high_step, step, 0)


def corner_kernel(spot_ref, *refs):
    pieces = refs[:4]
    x_ref, w_ref = refs[-2:]
    n = x_ref.shape[0]
    part = pieces[0].shape[1]
    z = spot_ref[0]
    core = spot_ref[4]
    for q in range(4):
        for i in range(4):
            side = core if i < 2 else 1 - core
            row = pl.multiple_of((i % 2) * (n // 2) + side * (n // 4) + (z ^ q) * part, part)
            w_ref[pl.ds(row, part), :] = pieces[q][i]
    ri = lax.broadcasted_iota(jnp.int32, (n, n), 0)
    ci = lax.broadcasted_iota(jnp.int32, (n, n), 1)
    x_ref[...] = jnp.where(ri == ci, 1.0, 0.0).astype(F32)
    eliminate(w_ref, x_ref, 0, FIRST_STEPS)


def corner_end_kernel(x_in, w_in, x_ref, square_ref, w_ref):
    x_ref[...] = x_in[...]
    w_ref[...] = w_in[...]
    eliminate(w_ref, x_ref, FIRST_STEPS, 4)
    x = x_ref[...]
    square_ref[...] = dot(x, x, TN)


def inverse_factor(spot, pieces):
    n = pieces[0].shape[2]
    square = shape(n, n)
    state = pl.pallas_call(
        corner_kernel,
        out_shape=[square, square],
        in_specs=[SMEM] + [VMEM] * 4,
        out_specs=[VMEM, VMEM],
        interpret=INTERPRET,
        name="inverse_start",
    )(spot, *pieces)
    return pl.pallas_call(
        corner_end_kernel,
        out_shape=[square, square],
        in_specs=[VMEM, VMEM],
        out_specs=[VMEM, VMEM],
        scratch_shapes=[pltpu.VMEM((n, n), F32)],
        interpret=INTERPRET,
        name="inverse_end",
    )(*state)


def corner_lines(panel):
    source = lambda zz, xx, yy, cc: zz == 0 and xx == 0 and yy < 2
    return [swap(panel, dy=d, only=source) for d in (1, 2, 3)]


def corner_both(panel, got, y):
    upper = jnp.where(y == 0, panel, jnp.where(y == 1, got[0], jnp.where(y == 2, got[1], got[2])))
    lower = jnp.where(y == 1, panel, jnp.where(y == 0, got[0], jnp.where(y == 3, got[1], got[2])))
    return jnp.stack([upper, lower])


def spread_corner(own, other, z, x):
    whole = jnp.concatenate([own, other], axis=0)
    part = whole.shape[1] // 4
    pieces = [whole[:, d * part : (d + 1) * part] for d in range(4)]
    first = lambda zz, xx, yy, cc: zz == 0 and xx == 0
    got = [swap(pieces[d], dz=d, only=first) for d in (1, 2, 3)]
    value = jnp.where(z == 0, pieces[0], got[0] + got[1] + got[2])
    second = lambda zz, xx, yy, cc: xx == 0
    got = [swap(value, dx=d, only=second) for d in (1, 2, 3)]
    value = jnp.where(x == 0, value, got[0] + got[1] + got[2])
    return [value] + [swap(value, dz=d) for d in (1, 2, 3)]


def pack_first_kernel(spot_ref, factor_ref, damping_ref, out_ref, hold, *, chunk, width):
    rows = hold.shape[0]
    part = damping_ref.shape[1]
    z, xh, xl, y, core = (spot_ref[i] for i in range(5))
    hold[...] = factor_ref[...]
    device = (((z * 2 + xh) * 2 + xl) * 4 + y) * 2 + core
    at = pl.multiple_of(device * part, part)
    lane = lax.broadcasted_iota(jnp.int32, (rows, part), 1)
    sub = lax.broadcasted_iota(jnp.int32, (rows, part), 0)
    add = jnp.where(lane == sub + chunk * rows, jnp.broadcast_to(damping_ref[...], (rows, part)), 0.0)
    hold[:, pl.ds(at, part)] = hold[:, pl.ds(at, part)] + add
    for m in range(8):
        for side in range(2):
            for b in range(4):
                col = (b * 2 + side) * 8 + m
                out_ref[m, :, (side * 4 + b) * width : (side * 4 + b + 1) * width] = hold[
                    :, col * width : (col + 1) * width
                ]


def pack_first(spot, factor, damping, chunk):
    part, order = factor.shape
    rows = part // CHUNKS
    width = order // 64
    return pl.pallas_call(
        functools.partial(pack_first_kernel, chunk=chunk, width=width),
        out_shape=shape(8, rows, 8 * width),
        grid=(1,),
        in_specs=[SMEM, pl.BlockSpec((rows, order), lambda i: (chunk, 0)), VMEM],
        out_specs=VMEM,
        scratch_shapes=[pltpu.VMEM((rows, order), F32)],
        interpret=INTERPRET,
        name="pack_first",
    )(spot, factor, damping)


def pack_second_kernel(spot_ref, in_ref, *refs):
    outs = refs[-4:]
    rows = in_ref.shape[1]
    half = in_ref.shape[2] // 2
    xh, xl = spot_ref[1], spot_ref[2]
    for n in range(4):
        col = pl.multiple_of((xl ^ (n & 1)) * half, half)
        for y1 in range(2):
            for k in range(2):
                m = y1 * 4 + (xh ^ (n >> 1)) * 2 + k
                at = (y1 * 2 + k) * rows
                outs[n][at : at + rows, :] = in_ref[m, :, pl.ds(col, half)]


def pack_third_kernel(spot_ref, *refs):
    ins, outs = refs[:4], refs[-4:]
    half = ins[0].shape[0] // 2
    z, xl = spot_ref[0], spot_ref[2]
    flip = (xl ^ (z >> 1)) == 1
    for q in range(4):
        row = pl.multiple_of(((z & 1) ^ (q & 1)) * half, half)
        for n1 in range(2):
            same = ins[n1 * 2 + (q >> 1)][pl.ds(row, half), :]
            changed = ins[n1 * 2 + 1 - (q >> 1)][pl.ds(row, half), :]
            outs[q][n1 * half : (n1 + 1) * half, :] = jnp.where(flip, changed, same)


def repack(kernel, spot, arrays, out, after=()):
    return pl.pallas_call(
        kernel,
        out_shape=[out] * 4,
        in_specs=[SMEM] + [VMEM] * len(arrays) + [ANY] * len(after),
        out_specs=[VMEM] * 4,
        interpret=INTERPRET,
    )(spot, *arrays, *after)


def send_chunk(spot, factor, damping, chunk, after):
    first = pack_first(spot, factor, damping, chunk)
    first = lax.all_to_all(first, ("y", "core"), 0, 0, tiled=True)
    _, rows, cols = first.shape
    out = shape(4 * rows, cols // 2)
    second = repack(pack_second_kernel, spot, [first], out, after)
    second = [second[n] if n == 0 else swap(second[n], dx=n) for n in range(4)]
    third = repack(pack_third_kernel, spot, second, out)
    return [third[q] if q == 0 else swap(third[q], dz=q) for q in range(4)]


def panel_kernel(spot_ref, x_ref, rows_ref, cols_ref, row_ref, col_ref, tile_ref):
    part = rows_ref.shape[0] // 16
    xl, y, core = spot_ref[2], spot_ref[3], spot_ref[4]
    x = halves(x_ref[...])
    row_ref[...] = dot3(halves(rows_ref[...]), x, NT)
    col_ref[...] = dot3(halves(cols_ref[...]), x, NT)
    share = part // 8
    column = (xl * 4 + y) * 2 + core
    for a in range(8):
        at = pl.multiple_of(a * 2 * part + column * share, share)
        tile_ref[a * share : (a + 1) * share, :] = row_ref[pl.ds(at, share), :]


def panel_solve(spot, x, rows_in, cols_in):
    width = x.shape[0]
    return pl.pallas_call(
        panel_kernel,
        out_shape=[shape(*rows_in.shape), shape(*cols_in.shape), shape(rows_in.shape[0] // 16, width)],
        in_specs=[SMEM, VMEM, VMEM, VMEM],
        out_specs=[VMEM] * 3,
        interpret=INTERPRET,
        name="panel_solve",
    )(spot, x, rows_in, cols_in)


def share_rows(panel):
    pairs = []
    for z, xh, xl, y, core in every():
        to = (xl * 2 + (y >> 1), y & 1, z >> 1, (z & 1) * 2 + xh, core)
        pairs.append((device_of(z, xh, xl, y, core), device_of(*to)))
    return lax.ppermute(panel, ALL, pairs)


def share_cols(panel):
    pairs = []
    for z, xh, xl, y, core in every():
        to = (z, core, xh, xl * 2 + (y >> 1), y & 1)
        pairs.append((device_of(z, xh, xl, y, core), device_of(*to)))
    return lax.ppermute(panel, ALL, pairs)


def update_kernel(spot_ref, *refs):
    blocks = refs[:4]
    row_ref, col_ref = refs[4:6]
    out_ref, high_ref, low_ref, hold = refs[-4:]
    count, _, rows, width = row_ref.shape
    xh = spot_ref[1]
    step = pl.program_id(0)
    half = 2 * rows

    @pl.when(step == 0)
    def _():
        high_ref[...], low_ref[...] = halves(col_ref[...])

    for q in range(4):

        @pl.when(step == q)
        def _():
            for n in range(2):
                at = pl.multiple_of((xh ^ n) * half, half)
                hold[pl.ds(at, half), :] = blocks[q][n * half : (n + 1) * half, :]

    left = halves(row_ref[...].reshape(count * rows, width))
    hold[...] = hold[...] - dot3(left, (high_ref[...], low_ref[...]), NT)
    lanes = out_ref.shape[3]
    groups = hold.shape[1] // lanes
    for i in range(count):
        for g in range(groups):
            out_ref.at[i, 0][pl.ds(g, rows, stride=groups), :] = hold[
                i * rows : (i + 1) * rows, g * lanes : (g + 1) * lanes
            ]


def update(spot, blocks, row_factor, col_factor, out, chunk):
    height, local_cols = blocks[0].shape
    rows = height // 4
    width = row_factor.shape[1]
    lanes = local_cols // 8
    first = out is None
    full = lambda a: pl.BlockSpec(a.shape, lambda i, s: (0, 0))
    place = lambda i, s: (s[0] ^ i, chunk, 0, 0)
    operands = [*blocks, row_factor.reshape(16, CHUNKS, rows, width), col_factor]
    return pl.pallas_call(
        update_kernel,
        out_shape=shape(16, CHUNKS, rows * 8, lanes),
        grid_spec=pltpu.PrefetchScalarGridSpec(
            num_scalar_prefetch=1,
            grid=(4,),
            in_specs=[full(b) for b in blocks]
            + [pl.BlockSpec((4, 1, rows, width), place), full(col_factor)]
            + ([] if first else [ANY]),
            out_specs=pl.BlockSpec((4, 1, rows * 8, lanes), place),
            scratch_shapes=[
                pltpu.VMEM(col_factor.shape, jnp.bfloat16),
                pltpu.VMEM(col_factor.shape, jnp.bfloat16),
                pltpu.VMEM((height, local_cols), F32),
            ],
        ),
        input_output_aliases={} if first else {7: 0},
        interpret=INTERPRET,
        name="update",
    )(spot, *operands, *([] if first else [out]))


def on_line(z, x, y, core):
    return z == 0 and x == 2


def place_panels_kernel(spot_ref, own_ref, other_ref, out_ref):
    part = own_ref.shape[1] // 2
    y, core = spot_ref[3], spot_ref[4]
    for ref, side in ((own_ref, core), (other_ref, 1 - core)):
        for m in range(4):
            line = y ^ m
            for slot, tile in ((0, 4 + line), (1, line + 8 * (1 - line // 2))):
                at = (tile * 2 + side) * part
                out_ref[:, pl.ds(pl.multiple_of(at, part), part)] = ref[
                    m, slot * part : (slot + 1) * part, :
                ].T


def place_panels(spot, own, other):
    _, rows, width = own.shape
    return pl.pallas_call(
        place_panels_kernel,
        out_shape=shape(width, 12 * rows),
        in_specs=[SMEM, VMEM, VMEM],
        out_specs=VMEM,
        interpret=INTERPRET,
        name="place_panels",
    )(spot, own, other)


def dot_e(left, right, dims):
    return dot3(halves(left), halves(right), dims)


def solve_kernel(spot_ref, *refs, block, last, panel):
    refs = list(refs)
    y, core = spot_ref[3], spot_ref[4]
    take = lambda: refs.pop(0)
    grads_ref = take()
    known = []
    if block == 0:
        x = take()[...]
        solved = dot_e(x, grads_ref[0:panel, :], NN)
        v = dot_e(x, solved, TN)
    else:
        shares = [take()[...] for _ in range(4)]
        inverse_ref = take()
        lead = 2 * (block % 2)
        near = y == lead
        twin = y == lead + 1
        far = y == (lead ^ 2)
        upper = jnp.where(near, shares[0], jnp.where(twin, shares[1], jnp.where(far, shares[2], shares[3])))
        lower = jnp.where(twin, shares[0], jnp.where(near, shares[1], jnp.where(far, shares[3], shares[2])))
        right = jnp.concatenate([upper, lower], axis=0)
        solved = dot_e(inverse_ref[0], right, NN)
        if last:
            refs[0][...] = solved
            return
        square_ref, panel_ref, v_ref = take(), take(), take()
        known = [take()[...] for _ in range(block - 1)] + [solved]
        v = v_ref[...] - dot_e(square_ref[...], dot_e(panel_ref[...], solved, NN), NN)
    own_ref, other_ref = take(), take()
    solved_ref, v_out, share_ref = refs
    tile = panel // 2
    part = tile // 2
    slot = (block + 1) // 2
    rest = []
    for ref in (own_ref, other_ref):
        total = dot_e(ref[:, :panel], v, NN)
        for j, value in enumerate(known):
            total = total + dot_e(ref[:, (j + 1) * panel : (j + 2) * panel], value, NN)
        rest.append(total)
    start = (slot * 4 + y) * tile
    for value, side in ((rest[0], core), (rest[1], 1 - core)):
        at = pl.multiple_of(side * part, part)
        row = pl.multiple_of(start + at, part)
        share_ref[pl.ds(at, part), :] = grads_ref[pl.ds(row, part), :] - value
    solved_ref[...] = solved
    v_out[...] = v


def forward_solve(spot, x, square, grads, inverses, panels, own, other):
    panel = x.shape[0]
    count = grads.shape[1]
    blocks = grads.shape[0] // panel
    solved, v, share = [], None, None
    for block in range(blocks):
        last = block == blocks - 1
        operands, specs = [spot, grads], [SMEM, VMEM]
        if block == 0:
            operands += [x]
            specs += [VMEM]
        else:
            got = [share] + [swap(share, dy=m, only=on_line) for m in (1, 2, 3)]
            operands += [*got, inverses]
            specs += [VMEM] * 4
            specs += [pl.BlockSpec((1, panel, panel), lambda i, b=block: (b - 1, 0, 0))]
            if not last:
                operands += [square, panels, v, *solved[1:]]
                specs += [VMEM, pl.BlockSpec((panel, panel), lambda i, b=block: (0, b))]
                specs += [VMEM] * block
        if not last:
            slot = (block + 1) // 2
            operands += [own[slot], other[slot]]
            specs += [VMEM, VMEM]
        outs = [shape(panel, count)]
        if not last:
            outs += [shape(panel, count), shape(panel // 2, count)]
        run = pl.pallas_call(
            functools.partial(solve_kernel, block=block, last=last, panel=panel),
            out_shape=outs,
            grid=(1,),
            in_specs=specs,
            out_specs=[VMEM] * len(outs),
            interpret=INTERPRET,
            name="solve",
        )
        result = run(*operands)
        solved.append(result[0])
        if not last:
            v, share = result[1], result[2]
    return solved


def spread_solution(spot, solved, z, x, y, core):
    whole = jnp.concatenate(solved, axis=0)
    rows = whole.shape[0]
    own = lax.dynamic_slice_in_dim(whole, (y * 2 + core) * (rows // 8), rows // 8, 0)
    got = [swap(own, dx=d, only=on_line) for d in (1, 2, 3)]
    own = jnp.where(x == 2, own, got[0] + got[1] + got[2])
    source = lambda zz, xx, yy, cc: zz == 0
    got = [swap(own, dz=d, only=source) for d in (1, 2, 3)]
    own = jnp.where(z == 0, own, got[0] + got[1] + got[2])
    lines = jnp.stack([own] + [swap(own, dy=d) for d in (1, 2, 3)])
    other = swap(lines, dcore=1)
    return pl.pallas_call(
        place_rows_kernel,
        out_shape=shape(*whole.shape),
        in_specs=[SMEM, VMEM, VMEM],
        out_specs=VMEM,
        interpret=INTERPRET,
        name="place_rows",
    )(spot, lines, other)


def place_rows_kernel(spot_ref, own_ref, other_ref, out_ref):
    rows = own_ref.shape[1]
    y, core = spot_ref[3], spot_ref[4]
    for ref, side in ((own_ref, core), (other_ref, 1 - core)):
        for m in range(4):
            at = ((y ^ m) * 2 + side) * rows
            out_ref[pl.ds(pl.multiple_of(at, rows), rows), :] = ref[m]


def program(factor, damping, gradients, inverses):
    part, order = factor.shape
    panel_width = inverses.shape[1]
    z, xh, xl = lax.axis_index("z"), lax.axis_index("xh"), lax.axis_index("xl")
    y, core = lax.axis_index("y"), lax.axis_index("core")
    x = xh * 2 + xl
    spot = jnp.stack([z, xh, xl, y, core]).astype(jnp.int32)
    device = device_of(z, xh, xl, y, core)
    panel = factor[:, :panel_width]
    row = lax.broadcasted_iota(jnp.int32, panel.shape, 0) + device * part
    col = lax.broadcasted_iota(jnp.int32, panel.shape, 1)
    panel = panel + jnp.where(row == col, damping[:, None], 0.0)

    from_first = lambda zz, xx, yy, cc: zz == 0 and xx == 0
    from_second = lambda zz, xx, yy, cc: zz == 0 and xx == 1
    lead = [swap(panel, dx=2, only=from_first), swap(panel, dx=3, only=from_second), panel]
    got = corner_lines(panel)
    rows_share = share_rows(panel)
    cols_share = share_cols(panel)
    corner_own = corner_both(panel, got, y)
    corner_other = swap(corner_own, dcore=1, only=from_first)
    ends = jnp.where(y < 2, lead[2], lead[0])
    ends = jnp.concatenate([lead[1], ends], axis=0)
    lines = jnp.stack([ends] + [swap(ends, dy=m, only=on_line) for m in (1, 2, 3)])
    lines_other = swap(lines, dcore=1, only=on_line)
    pieces = spread_corner(corner_own, corner_other, z, x)
    rows_in = lax.all_gather(rows_share, ("xl", "y", "core"), tiled=True)
    cols_in = lax.all_gather(cols_share, ("z", "xh"), tiled=True)
    second = swap(factor[:, panel_width : 3 * panel_width], dx=3, only=from_second)
    lower = [
        lead[0],
        jnp.concatenate([lead[1], second], axis=1),
        factor[:, : 5 * panel_width],
    ]
    lower_other = [swap(value, dcore=1, only=on_line) for value in lower]

    stages = [send_chunk(spot, factor, damping[None, :], chunk, ()) for chunk in range(CHUNKS)]

    x_inverse, inverse = inverse_factor(spot, pieces)
    panels = place_panels(spot, lines, lines_other)
    row_factor, col_factor, tiles = panel_solve(spot, x_inverse, rows_in, cols_in)

    solved = forward_solve(spot, x_inverse, inverse, gradients, inverses, panels, lower, lower_other)
    solution_rows = spread_solution(spot, solved, z, x, y, core)

    out = None
    for chunk in range(CHUNKS):
        out = update(spot, stages[chunk], row_factor, col_factor, out, chunk)
    tile = order // 64
    updated = out.reshape(8, 1, tile, 4, 1, tile)
    panel_tiles = tiles.reshape(8, 1, part // 8, panel_width)
    return (updated, panel_tiles, solution_rows)


def solution(mesh):
    split = Mesh(mesh.devices.reshape(4, 2, 2, 4, 2), ALL)
    row, col = ("z", "xh"), ("xl", "y", "core")
    return jax.shard_map(
        program,
        mesh=split,
        in_specs=(P(row + col, None), P(row + col), P(), P()),
        out_specs=(P(None, row, None, None, col, None), P(None, row, col, None), P()),
        check_vma=False,
    )
```

time: 1460 us -> 597 us (0.41)
  waiting for transfers between devices: 1010 us -> 142 us
  starting transfers between devices: 8.32 us -> 241 us
  Pallas kernels: 0 us -> 167 us
  other arithmetic: 136 us -> 7.93 us
  local copies, waits for them, and re-layouts: 118 us -> 16.8 us
  blocking collectives: 101 us -> 0 us
  matrix products: 69.3 us -> 0 us
    psum x8 -> x0, waiting for transfers between devices: 911 us -> none  [the longest x5 663 us: body(): lax.psum(place(partial_value, block_place, panel_width, 0), ('row', 'col'))]
    ppermute x0 -> x62, starting transfers between devices: none -> 228 us  [the longest x60 222 us: swap(): return lax.ppermute(value, ALL, pairs)]
    pallas_call x0 -> x19, Pallas kernels: none -> 167 us  [the longest x1 45.2 us: inverse_factor(): pl.pallas_call(corner_end_kernel, out_shape=[square, square], in_specs=[V...]
    ppermute x0 -> x62, waiting for transfers between devices: none -> 142 us  [the longest x60 139 us: swap(): return lax.ppermute(value, ALL, pairs)]
    another operation x19 -> x5, other arithmetic: 123 us -> 2.51 us  [the longest x2 1.17 us: corner_both(): return jnp.stack([upper, lower])]
    all_to_all x1 -> x0, blocking collectives: 101 us -> none  [body(): lax.all_to_all(arranged, 'col', split_axis=0, concat_axis=1, tiled=True)]
    all_to_all x1 -> x2, waiting for transfers between devices: 94.4 us -> 0.01 us  [send_chunk(): first = lax.all_to_all(first, ('y', 'core'), 0, 0, tiled=True)]
    dot_general x15 -> x0, matrix products: 51 us -> none  [the longest x14 31 us: exact_dot(): jnp.dot(left, right, precision=lax.Precision.HIGHEST, preferred_element_t...]
  transfers between devices with their start and end apart: 9 -> 66, of which waited for: 8 -> 13; matrix products, arithmetic and copies ran while one was open for 13% -> 3% of each run, Pallas kernels for 0% -> 27%
where the time goes in v1:
time: 597 us; the launch traced here: 590 us
  starting transfers between devices  241 us (40%)
  Pallas kernels  167 us (28%)
  waiting for transfers between devices  142 us (24%)
  local copies, waits for them, and re-layouts  16.8 us (3%)
  between operations  15.2 us (3%)
  other arithmetic  7.93 us (1%)
    ppermute x60, starting transfers between devices, swap(): return lax.ppermute(value, ALL, pairs)  222 us
    ppermute x60, waiting for transfers between devices, swap(): return lax.ppermute(value, ALL, pairs)  139 us
    pallas_call x1, Pallas kernels, inverse_factor(): pl.pallas_call(corner_end_kernel, out_shape=[square, square], in_specs=[V...  45.2 us
    pallas_call x6, Pallas kernels, forward_solve(): result = run(*operands)  39.7 us
    pallas_call x2, Pallas kernels, update(): pl.pallas_call(update_kernel, out_shape=shape(16, CHUNKS, rows * 8, lanes...  20 us
    pallas_call x4, Pallas kernels, repack(): pl.pallas_call(kernel, out_shape=[out] * 4, in_specs=[SMEM] + [VMEM] * le...  18.3 us
    pallas_call x1, Pallas kernels, inverse_factor(): pl.pallas_call(corner_kernel, out_shape=[square, square], in_specs=[SMEM]...  15.8 us
    all_to_all x2, starting transfers between devices, send_chunk(): first = lax.all_to_all(first, ('y', 'core'), 0, 0, tiled=True)  12.7 us
  transfers between devices with their start and end apart: 66, of which 13 were waited for; matrix products, arithmetic and copies ran while one was open for 3% of the time, Pallas kernels for 27%

profile of v1, /device:TPU:1, one launch (start us, length us, event | category | flops | bytes accessed | tf_op | source)
XLA Modules:
  0.0 590.4 jit_solution(1600022015512009179)
XLA Ops:
  8.3 6.0 %collective-permute-start.20 = (f32[128,512]{1,0:T(8,128)S(1)}, f32[128,512]{1,0:T(8,128)S(1)}, u32[]{:S(2)}, u32[]{:S(2)}) collective-permute-start(f32[128,512]{1,0:T(8,128)S(1)} %select_add_fusion), channel_id=1, source_target_pairs={{0,0},{1,16},{2,1},{3,17},{4,2},{5,18},{6,3},{7,19},{8,4},{9,20},{... | collective-permute-start | bytes 786440 | tf_op jit(solution)/shard_map/ppermute | solution.py:308
  19.0 4.8 pack_first.3
  23.9 8.2 %all-to-all-start.1 = ((f32[8,64,2048]{2,1,0:T(8,128)}), f32[8,64,2048]{2,1,0:T(8,128)}, u32[]{:S(2)}, u32[]{:S(2)}) async-start(f32[8,64,2048]{2,1,0:T(8,128)} %pack_first.3), calls=%async_computation.1 | async-start | bytes 8388608 | tf_op jit(solution)/shard_map/all_to_all | solution.py:261
  32.7 8.7 %collective-permute-start.27 = (f32[128,512]{1,0:T(8,128)S(1)}, f32[128,512]{1,0:T(8,128)}, u32[]{:S(2)}, u32[]{:S(2)}) collective-permute-start(f32[128,512]{1,0:T(8,128)S(1)} %select_add_fusion), channel_id=1, source_target_pairs={{0,16},{1,17},{2,18},{3,19},{4,20},{5,21},{6,22},{7,23}} | collective-permute-start | bytes 786440 | tf_op jit(solution)/shard_map/ppermute | solution.py:68
  41.5 7.0 %collective-permute-start.8 = (f32[128,512]{1,0:T(8,128)S(1)}, f32[128,512]{1,0:T(8,128)S(1)}, u32[]{:S(2)}, u32[]{:S(2)}) collective-permute-start(f32[128,512]{1,0:T(8,128)S(1)} %select_add_fusion), channel_id=1, source_target_pairs={{0,6},{1,7},{2,4},{3,5}} | collective-permute-start | bytes 786440 | tf_op jit(solution)/shard_map/ppermute | solution.py:68
  53.7 35.1 %collective-permute-done.8 = f32[128,512]{1,0:T(8,128)S(1)} collective-permute-done((f32[128,512]{1,0:T(8,128)S(1)}, f32[128,512]{1,0:T(8,128)S(1)}, u32[]{:S(2)}, u32[]{:S(2)}) %collective-permute-start.8) | collective-permute-done | bytes 262176 | tf_op jit(solution)/shard_map/ppermute | solution.py:68
  88.7 5.6 collective-permute-done.7
  94.4 5.6 collective-permute-done.6
  117.8 4.9 pack_first.2
  131.1 44.5 %collective-permute-start.14 = (f32[4,32,512]{2,1,0:T(8,128)}, f32[4,32,512]{2,1,0:T(8,128)}, u32[]{:S(2)}, u32[]{:S(2)}) collective-permute-start(f32[4,32,512]{2,1,0:T(8,128)} %slice_select_fusion), channel_id=1, source_target_pairs={{0,16},{1,17},{2,18},{3,19},{4,20},{5,21},{6,22},{7,23},{32,48},{3... | collective-permute-start | bytes 786440 | tf_op jit(solution)/shard_map/ppermute | solution.py:68
  188.2 14.6 %collective-permute-done.18.refs_3_ = f32[4,32,512]{2,1,0:T(8,128)S(1)} collective-permute-done((f32[4,32,512]{2,1,0:T(8,128)S(1)}, f32[4,32,512]{2,1,0:T(8,128)S(1)}, u32[]{:S(2)}, u32[]{:S(2)}) %collective-permute-start.18) | collective-permute-done | bytes 262176 | tf_op jit(solution)/shard_map/ppermute | solution.py:68
  209.9 15.8 %inverse_start.1 = (f32[512,512]{1,0:T(8,128)}, f32[512,512]{1,0:T(8,128)}) custom-call(s32[5]{0:T(128)} %stack.62.spot_ref, f32[4,32,512]{2,1,0:T(8,128)} %copy-done.11, f32[4,32,512]{2,1,0:T(8,128)} %collective-permute-done.16.refs_1_, f32[4,32,512]{2,1,0:T(8,128)} %copy-done.19, f32[4,32,512]{2,1,0:T(8,128)} %copy-done.18), custom_call_target="tpu_custom_call" | custom-call | tf_op jit(solution)/shard_map/inverse_start/pallas_call | solution.py:143
  225.6 45.2 %inverse_end.1 = (f32[512,512]{1,0:T(8,128)}, f32[512,512]{1,0:T(8,128)}) custom-call(f32[512,512]{1,0:T(8,128)} %get-tuple-element.48.x_in, f32[512,512]{1,0:T(8,128)} %get-tuple-element.49.w_in), custom_call_target="tpu_custom_call" | custom-call | tf_op jit(solution)/shard_map/inverse_end/pallas_call | solution.py:151
  278.4 6.1 %place_panels.1.refs_7_ = f32[512,3072]{1,0:T(8,128)} custom-call(s32[5]{0:T(128)} %stack.62.spot_ref, f32[4,256,512]{2,1,0:T(8,128)} %copy-done.1, f32[4,256,512]{2,1,0:T(8,128)} %collective-permute-done.36.other_ref), custom_call_target="tpu_custom_call" | custom-call | tf_op jit(solution)/shard_map/place_panels/pallas_call | solution.py:393
  285.1 7.3 %solve.7 = (f32[512,128]{1,0:T(8,128)}, f32[512,128]{1,0:T(8,128)}, f32[256,128]{1,0:T(8,128)}) custom-call(s32[5]{0:T(128)} %stack.62.spot_ref, f32[3072,128]{1,0:T(8,128)} %refs_0_.11, f32[256,128]{1,0:T(8,128)} %get-tuple-element.63.refs_1_, f32[256,128]{1,0:T(8,128)} %copy-done.29, f32[256,128]{1,0:T(8,128)} %collective-permute-done.30.refs_3_, ...), custom_call_target="tpu_custom_call" | custom-call | tf_op jit(solution)/shard_map/solve/pallas_call | solution.py:490
  295.2 7.6 %solve.8 = (f32[512,128]{1,0:T(8,128)}, f32[512,128]{1,0:T(8,128)}, f32[256,128]{1,0:T(8,128)}) custom-call(s32[5]{0:T(128)} %stack.62.spot_ref, f32[3072,128]{1,0:T(8,128)} %refs_0_.11, f32[256,128]{1,0:T(8,128)} %get-tuple-element.67.refs_1_, f32[256,128]{1,0:T(8,128)} %copy-done.32, f32[256,128]{1,0:T(8,128)} %copy-done.30, f32[256,128]{1,0:T(8,128)} %copy-done.27, ...), custom_call_target="tpu_custom_call" | custom-call | tf_op jit(solution)/shard_map/solve/pallas_call | solution.py:490
  305.7 8.3 %solve.9 = (f32[512,128]{1,0:T(8,128)}, f32[512,128]{1,0:T(8,128)}, f32[256,128]{1,0:T(8,128)}) custom-call(s32[5]{0:T(128)} %stack.62.spot_ref, f32[3072,128]{1,0:T(8,128)} %refs_0_.11, f32[256,128]{1,0:T(8,128)} %get-tuple-element.70.refs_1_, f32[256,128]{1,0:T(8,128)} %copy-done.22, f32[256,128]{1,0:T(8,128)} %copy-done.21, f32[256,128]{1,0:T(8,128)} %copy-done.20, ...), custom_call_target="tpu_custom_call" | custom-call | tf_op jit(solution)/shard_map/solve/pallas_call | solution.py:490
  317.3 8.6 %solve.10 = (f32[512,128]{1,0:T(8,128)}, f32[512,128]{1,0:T(8,128)}, f32[256,128]{1,0:T(8,128)}) custom-call(s32[5]{0:T(128)} %stack.62.spot_ref, f32[3072,128]{1,0:T(8,128)} %refs_0_.11, f32[256,128]{1,0:T(8,128)} %get-tuple-element.73.refs_1_, f32[256,128]{1,0:T(8,128)} %copy-done.26, f32[256,128]{1,0:T(8,128)} %copy-done.25, f32[256,128]{1,0:T(8,128)} %copy-done.23, ...), custom_call_target="tpu_custom_call" | custom-call | tf_op jit(solution)/shard_map/solve/pallas_call | solution.py:490
  345.0 45.2 %collective-permute-start.22 = (f32[256,1024]{1,0:T(8,128)}, f32[256,1024]{1,0:T(8,128)S(1)}, u32[]{:S(2)}, u32[]{:S(2)}) collective-permute-start(f32[256,1024]{1,0:T(8,128)} %get-tuple-element.55), channel_id=1, source_target_pairs={{0,16},{1,17},{2,18},{3,19},{4,20},{5,21},{6,22},{7,23},{8,24},{9,... | collective-permute-start | bytes 3145736 | tf_op jit(solution)/shard_map/ppermute | solution.py:68
  399.4 15.7 %collective-permute-start.60 = (f32[384,128]{1,0:T(8,128)S(1)}, f32[384,128]{1,0:T(8,128)S(1)}, u32[]{:S(2)}, u32[]{:S(2)}) collective-permute-start(f32[384,128]{1,0:T(8,128)S(1)} %add_select_fusion.1), channel_id=1, source_target_pairs={{0,6},{1,7},{2,4},{3,5},{4,2},{5,3},{6,0},{7,1},{8,14},{9,15},{10,... | collective-permute-start | bytes 589832 | tf_op jit(solution)/shard_map/ppermute | solution.py:68
  415.1 8.9 %collective-permute-start.59 = (f32[384,128]{1,0:T(8,128)S(1)}, f32[384,128]{1,0:T(8,128)}, u32[]{:S(2)}, u32[]{:S(2)}) collective-permute-start(f32[384,128]{1,0:T(8,128)S(1)} %add_select_fusion.1), channel_id=1, source_target_pairs={{0,4},{1,5},{2,6},{3,7},{4,0},{5,1},{6,2},{7,3},{8,12},{9,13},{10,... | collective-permute-start | bytes 589832 | tf_op jit(solution)/shard_map/ppermute | solution.py:68
  431.0 5.5 collective-permute-done.22.refs_2_
  443.7 12.6 %collective-permute-start.24 = (f32[256,1024]{1,0:T(8,128)}, f32[256,1024]{1,0:T(8,128)S(1)}, u32[]{:S(2)}, u32[]{:S(2)}) collective-permute-start(f32[256,1024]{1,0:T(8,128)} %get-tuple-element.58), channel_id=1, source_target_pairs={{0,32},{1,33},{2,34},{3,35},{4,36},{5,37},{6,38},{7,39},{8,40},{9,... | collective-permute-start | bytes 3145736 | tf_op jit(solution)/shard_map/ppermute | solution.py:68
  458.4 11.9 %collective-permute-start.25 = (f32[256,1024]{1,0:T(8,128)}, f32[256,1024]{1,0:T(8,128)}, u32[]{:S(2)}, u32[]{:S(2)}) collective-permute-start(f32[256,1024]{1,0:T(8,128)} %get-tuple-element.59), channel_id=1, source_target_pairs={{0,64},{1,65},{2,66},{3,67},{4,68},{5,69},{6,70},{7,71},{8,72},{9,... | collective-permute-start | bytes 3145736 | tf_op jit(solution)/shard_map/ppermute | solution.py:68
  470.3 11.3 %collective-permute-done.1.refs_2_ = f32[256,1024]{1,0:T(8,128)} collective-permute-done((f32[256,1024]{1,0:T(8,128)}, f32[256,1024]{1,0:T(8,128)}, u32[]{:S(2)}, u32[]{:S(2)}) %collective-permute-start.1) | collective-permute-done | bytes 1048608 | tf_op jit(solution)/shard_map/ppermute | solution.py:68
  481.6 7.0 %collective-permute-start.26 = (f32[256,1024]{1,0:T(8,128)}, f32[256,1024]{1,0:T(8,128)}, u32[]{:S(2)}, u32[]{:S(2)}) collective-permute-start(f32[256,1024]{1,0:T(8,128)} %get-tuple-element.60), channel_id=1, source_target_pairs={{0,96},{1,97},{2,98},{3,99},{4,100},{5,101},{6,102},{7,103},{8,104... | collective-permute-start | bytes 3145736 | tf_op jit(solution)/shard_map/ppermute | solution.py:68
  500.8 9.6 %panel_solve.1 = (f32[2048,512]{1,0:T(8,128)}, f32[1024,512]{1,0:T(8,128)}, f32[128,512]{1,0:T(8,128)}) custom-call(s32[5]{0:T(128)} %stack.62.spot_ref, f32[512,512]{1,0:T(8,128)} %get-tuple-element.50.x_ref.refs_1_, f32[2048,512]{1,0:T(8,128)} %all-gather.3.cloned.1.call-done.rows_ref, f32[1024,512]{1,0:T(8,128)} %all-gather.5.cloned.1.call-done.cols_ref), custom_call_target="tpu_custom_call" | custom-call | tf_op jit(solution)/shard_map/panel_solve/pallas_call | solution.py:285
  510.4 18.5 %collective-permute-done.26.refs_3_ = f32[256,1024]{1,0:T(8,128)} collective-permute-done((f32[256,1024]{1,0:T(8,128)}, f32[256,1024]{1,0:T(8,128)}, u32[]{:S(2)}, u32[]{:S(2)}) %collective-permute-start.26) | collective-permute-done | bytes 1048608 | tf_op jit(solution)/shard_map/ppermute | solution.py:68
  528.9 10.0 %update.2.refs_6_ = f32[16,2,512,128]{3,2,1,0:T(8,128)} custom-call(s32[5]{0:T(128)} %stack.62.spot_ref, f32[256,1024]{1,0:T(8,128)} %get-tuple-element.57.refs_0_, f32[256,1024]{1,0:T(8,128)} %copy-done.13, f32[256,1024]{1,0:T(8,128)} %collective-permute-done.25.refs_2_, f32[256,1024]{1,0:T(8,128)} %collective-permute-done.26.refs_3_, ...), custom_call_target="tpu_custom_call" | custom-call | tf_op jit(solution)/shard_map/update/pallas_call | solution.py:352
  538.9 11.5 %collective-permute-done.4.refs_2_ = f32[256,1024]{1,0:T(8,128)S(1)} collective-permute-done((f32[256,1024]{1,0:T(8,128)}, f32[256,1024]{1,0:T(8,128)S(1)}, u32[]{:S(2)}, u32[]{:S(2)}) %collective-permute-start.4) | collective-permute-done | bytes 1048608 | tf_op jit(solution)/shard_map/ppermute | solution.py:68
  550.4 23.0 %collective-permute-done.5.refs_3_ = f32[256,1024]{1,0:T(8,128)} collective-permute-done((f32[256,1024]{1,0:T(8,128)}, f32[256,1024]{1,0:T(8,128)}, u32[]{:S(2)}, u32[]{:S(2)}) %collective-permute-start.5) | collective-permute-done | bytes 1048608 | tf_op jit(solution)/shard_map/ppermute | solution.py:68
  573.4 10.0 %update.3 = f32[16,2,512,128]{3,2,1,0:T(8,128)} custom-call(s32[5]{0:T(128)} %stack.62.spot_ref, f32[256,1024]{1,0:T(8,128)} %get-tuple-element.44.refs_0_, f32[256,1024]{1,0:T(8,128)} %copy-done.9, f32[256,1024]{1,0:T(8,128)} %copy-done.10, f32[256,1024]{1,0:T(8,128)} %collective-permute-done.5.refs_3_, ...), custom_call_target="tpu_custom_call", output_to_operand_aliasing={{}: (7, {})} | custom-call | tf_op jit(solution)/shard_map/update/pallas_call | solution.py:352
  (216 shorter events, 130.6 us)
Async XLA Ops:
  7.2 493.6 %all-gather.5.cloned.1.call-start = ((), (), s32[]{:S(2)}) async-start(), calls=%async_computation.3 | async-start | bytes 2359296 | tf_op jit(solution)/shard_map/all_gather | solution.py:554
  23.9 98.8 %all-to-all-start.1 = ((f32[8,64,2048]{2,1,0:T(8,128)}), f32[8,64,2048]{2,1,0:T(8,128)}, u32[]{:S(2)}, u32[]{:S(2)}) async-start(f32[8,64,2048]{2,1,0:T(8,128)} %pack_first.3), calls=%async_computation.1 | async-start | bytes 8388608 | tf_op jit(solution)/shard_map/all_to_all | solution.py:261
  32.0 468.7 %all-gather.3.cloned.1.call-start = ((), (), s32[]{:S(2)}) async-start(), calls=%async_computation.2 | async-start | bytes 4456448 | tf_op jit(solution)/shard_map/all_gather | solution.py:553
  41.5 47.3 %collective-permute-start.8 = (f32[128,512]{1,0:T(8,128)S(1)}, f32[128,512]{1,0:T(8,128)S(1)}, u32[]{:S(2)}, u32[]{:S(2)}) collective-permute-start(f32[128,512]{1,0:T(8,128)S(1)} %select_add_fusion), channel_id=1, source_target_pairs={{0,6},{1,7},{2,4},{3,5}} | collective-permute-start | bytes 786440 | tf_op jit(solution)/shard_map/ppermute | solution.py:68
  48.5 45.9 %collective-permute-start.7 = (f32[128,512]{1,0:T(8,128)S(1)}, f32[128,512]{1,0:T(8,128)S(1)}, u32[]{:S(2)}, u32[]{:S(2)}) collective-permute-start(f32[128,512]{1,0:T(8,128)S(1)} %select_add_fusion), channel_id=1, source_target_pairs={{0,4},{1,5},{2,6},{3,7}} | collective-permute-start | bytes 786440 | tf_op jit(solution)/shard_map/ppermute | solution.py:68
  49.8 50.2 %collective-permute-start.6 = (f32[128,512]{1,0:T(8,128)S(1)}, f32[128,512]{1,0:T(8,128)S(1)}, u32[]{:S(2)}, u32[]{:S(2)}) collective-permute-start(f32[128,512]{1,0:T(8,128)S(1)} %select_add_fusion), channel_id=1, source_target_pairs={{0,2},{1,3},{2,0},{3,1}} | collective-permute-start | bytes 786440 | tf_op jit(solution)/shard_map/ppermute | solution.py:68
  53.0 48.1 %collective-permute-start.32 = (f32[128,512]{1,0:T(8,128)S(1)}, f32[128,512]{1,0:T(8,128)S(1)}, u32[]{:S(2)}, u32[]{:S(2)}) collective-permute-start(f32[128,512]{1,0:T(8,128)S(1)} %select_add_fusion), channel_id=1, source_target_pairs={{8,16},{9,17},{10,18},{11,19},{12,20},{13,21},{14,22},{15,23}} | collective-permute-start | bytes 786440 | tf_op jit(solution)/shard_map/ppermute | solution.py:68
  106.1 171.4 %collective-permute-start.36 = (f32[4,256,512]{2,1,0:T(8,128)S(1)}, f32[4,256,512]{2,1,0:T(8,128)}, u32[]{:S(2)}, u32[]{:S(2)}) collective-permute-start(f32[4,256,512]{2,1,0:T(8,128)S(1)} %pad_maximum_fusion.own_ref), channel_id=1, source_target_pairs={{16,17},{17,16},{18,19},{19,18},{20,21},{21,20},{22,23},{23,22}} | collective-permute-start | bytes 6291464 | tf_op jit(solution)/shard_map/ppermute | solution.py:68
  116.4 63.3 %collective-permute-start.37 = (f32[128,1024]{1,0:T(8,128)}, f32[128,1024]{1,0:T(8,128)}, u32[]{:S(2)}, u32[]{:S(2)}) collective-permute-start(f32[128,1024]{1,0:T(8,128)} %slice.26), channel_id=1, source_target_pairs={{8,16},{9,17},{10,18},{11,19},{12,20},{13,21},{14,22},{15,23}} | collective-permute-start | bytes 1572872 | tf_op jit(solution)/shard_map/ppermute | solution.py:68
  122.7 302.6 %all-to-all-start = ((f32[8,64,2048]{2,1,0:T(8,128)}), f32[8,64,2048]{2,1,0:T(8,128)}, u32[]{:S(2)}, u32[]{:S(2)}) async-start(f32[8,64,2048]{2,1,0:T(8,128)} %pack_first.2), calls=%async_computation | async-start | bytes 8388608 | tf_op jit(solution)/shard_map/all_to_all | solution.py:261
  129.1 56.1 %collective-permute-start.15 = (f32[4,32,512]{2,1,0:T(8,128)}, f32[4,32,512]{2,1,0:T(8,128)}, u32[]{:S(2)}, u32[]{:S(2)}) collective-permute-start(f32[4,32,512]{2,1,0:T(8,128)} %slice_select_fusion), channel_id=1, source_target_pairs={{0,24},{1,25},{2,26},{3,27},{4,28},{5,29},{6,30},{7,31},{32,56},{3... | collective-permute-start | bytes 786440 | tf_op jit(solution)/shard_map/ppermute | solution.py:68
  131.1 55.7 %collective-permute-start.14 = (f32[4,32,512]{2,1,0:T(8,128)}, f32[4,32,512]{2,1,0:T(8,128)}, u32[]{:S(2)}, u32[]{:S(2)}) collective-permute-start(f32[4,32,512]{2,1,0:T(8,128)} %slice_select_fusion), channel_id=1, source_target_pairs={{0,16},{1,17},{2,18},{3,19},{4,20},{5,21},{6,22},{7,23},{32,48},{3... | collective-permute-start | bytes 786440 | tf_op jit(solution)/shard_map/ppermute | solution.py:68
  179.7 125.2 %collective-permute-start.45 = (f32[128,2560]{1,0:T(8,128)S(1)}, f32[128,2560]{1,0:T(8,128)}, u32[]{:S(2)}, u32[]{:S(2)}) collective-permute-start(f32[128,2560]{1,0:T(8,128)S(1)} %slice.27.refs_11_.refs_12_), channel_id=1, source_target_pairs={{16,17},{17,16},{18,19},{19,18},{20,21},{21,20},{22,23},{23,22}} | collective-permute-start | bytes 3932168 | tf_op jit(solution)/shard_map/ppermute | solution.py:68
  185.1 99.3 %collective-permute-start.38 = (f32[128,1536]{1,0:T(8,128)}, f32[128,1536]{1,0:T(8,128)}, u32[]{:S(2)}, u32[]{:S(2)}) collective-permute-start(f32[128,1536]{1,0:T(8,128)} %constant_dynamic-update-slice_fusion.refs_9_.refs_10_), channel_id=1, source_target_pairs={{16,17},{17,16},{18,19},{19,18},{20,21},{21,20},{22,23},{23,22}} | collective-permute-start | bytes 2359304 | tf_op jit(solution)/shard_map/ppermute | solution.py:68
  203.5 67.4 %collective-permute-start.28 = (f32[128,512]{1,0:T(8,128)}, f32[128,512]{1,0:T(8,128)}, u32[]{:S(2)}, u32[]{:S(2)}) collective-permute-start(f32[128,512]{1,0:T(8,128)} %collective-permute-done.27.refs_2_), channel_id=1, source_target_pairs={{16,17},{17,16},{18,19},{19,18},{20,21},{21,20},{22,23},{23,22}} | collective-permute-start | bytes 786440 | tf_op jit(solution)/shard_map/ppermute | solution.py:68
  334.5 55.7 %collective-permute-start.54 = (f32[384,128]{1,0:T(8,128)S(1)}, f32[384,128]{1,0:T(8,128)S(1)}, u32[]{:S(2)}, u32[]{:S(2)}) collective-permute-start(f32[384,128]{1,0:T(8,128)S(1)} %constant_dynamic-slice_fusion), channel_id=1, source_target_pairs={{16,8},{17,9},{18,10},{19,11},{20,12},{21,13},{22,14},{23,15}} | collective-permute-start | bytes 589832 | tf_op jit(solution)/shard_map/ppermute | solution.py:68
  335.2 55.2 %collective-permute-start.53 = (f32[384,128]{1,0:T(8,128)S(1)}, f32[384,128]{1,0:T(8,128)}, u32[]{:S(2)}, u32[]{:S(2)}) collective-permute-start(f32[384,128]{1,0:T(8,128)S(1)} %constant_dynamic-slice_fusion), channel_id=1, source_target_pairs={{16,0},{17,1},{18,2},{19,3},{20,4},{21,5},{22,6},{23,7}} | collective-permute-start | bytes 589832 | tf_op jit(solution)/shard_map/ppermute | solution.py:68
  336.5 53.9 %collective-permute-start.52 = (f32[384,128]{1,0:T(8,128)S(1)}, f32[384,128]{1,0:T(8,128)}, u32[]{:S(2)}, u32[]{:S(2)}) collective-permute-start(f32[384,128]{1,0:T(8,128)S(1)} %constant_dynamic-slice_fusion), channel_id=1, source_target_pairs={{16,24},{17,25},{18,26},{19,27},{20,28},{21,29},{22,30},{23,31}} | collective-permute-start | bytes 589832 | tf_op jit(solution)/shard_map/ppermute | solution.py:68
  342.3 87.5 %collective-permute-start.21 = (f32[256,1024]{1,0:T(8,128)}, f32[256,1024]{1,0:T(8,128)S(1)}, u32[]{:S(2)}, u32[]{:S(2)}) collective-permute-start(f32[256,1024]{1,0:T(8,128)} %get-tuple-element.54), channel_id=1, source_target_pairs={{0,8},{1,9},{2,10},{3,11},{4,12},{5,13},{6,14},{7,15},{8,0},{9,1},... | collective-permute-start | bytes 3145736 | tf_op jit(solution)/shard_map/ppermute | solution.py:68
  345.0 91.5 %collective-permute-start.22 = (f32[256,1024]{1,0:T(8,128)}, f32[256,1024]{1,0:T(8,128)S(1)}, u32[]{:S(2)}, u32[]{:S(2)}) collective-permute-start(f32[256,1024]{1,0:T(8,128)} %get-tuple-element.55), channel_id=1, source_target_pairs={{0,16},{1,17},{2,18},{3,19},{4,20},{5,21},{6,22},{7,23},{8,24},{9,... | collective-permute-start | bytes 3145736 | tf_op jit(solution)/shard_map/ppermute | solution.py:68
  390.2 46.3 %collective-permute-start.23 = (f32[256,1024]{1,0:T(8,128)}, f32[256,1024]{1,0:T(8,128)S(1)}, u32[]{:S(2)}, u32[]{:S(2)}) collective-permute-start(f32[256,1024]{1,0:T(8,128)} %get-tuple-element.56), channel_id=1, source_target_pairs={{0,24},{1,25},{2,26},{3,27},{4,28},{5,29},{6,30},{7,31},{8,16},{9,... | collective-permute-start | bytes 3145736 | tf_op jit(solution)/shard_map/ppermute | solution.py:68
  415.1 28.6 %collective-permute-start.59 = (f32[384,128]{1,0:T(8,128)S(1)}, f32[384,128]{1,0:T(8,128)}, u32[]{:S(2)}, u32[]{:S(2)}) collective-permute-start(f32[384,128]{1,0:T(8,128)S(1)} %add_select_fusion.1), channel_id=1, source_target_pairs={{0,4},{1,5},{2,6},{3,7},{4,0},{5,1},{6,2},{7,3},{8,12},{9,13},{10,... | collective-permute-start | bytes 589832 | tf_op jit(solution)/shard_map/ppermute | solution.py:68
  424.0 32.3 %collective-permute-start.58 = (f32[384,128]{1,0:T(8,128)S(1)}, f32[384,128]{1,0:T(8,128)}, u32[]{:S(2)}, u32[]{:S(2)}) collective-permute-start(f32[384,128]{1,0:T(8,128)S(1)} %add_select_fusion.1), channel_id=1, source_target_pairs={{0,2},{1,3},{2,0},{3,1},{4,6},{5,7},{6,4},{7,5},{8,10},{9,11},{10,... | collective-permute-start | bytes 589832 | tf_op jit(solution)/shard_map/ppermute | solution.py:68
  436.5 45.1 %collective-permute-start.1 = (f32[256,1024]{1,0:T(8,128)}, f32[256,1024]{1,0:T(8,128)}, u32[]{:S(2)}, u32[]{:S(2)}) collective-permute-start(f32[256,1024]{1,0:T(8,128)} %get-tuple-element.42), channel_id=1, source_target_pairs={{0,16},{1,17},{2,18},{3,19},{4,20},{5,21},{6,22},{7,23},{8,24},{9,... | collective-permute-start | bytes 3145736 | tf_op jit(solution)/shard_map/ppermute | solution.py:68
  436.5 52.1 %collective-permute-start.2 = (f32[256,1024]{1,0:T(8,128)}, f32[256,1024]{1,0:T(8,128)}, u32[]{:S(2)}, u32[]{:S(2)}) collective-permute-start(f32[256,1024]{1,0:T(8,128)} %get-tuple-element.43), channel_id=1, source_target_pairs={{0,24},{1,25},{2,26},{3,27},{4,28},{5,29},{6,30},{7,31},{8,16},{9,... | collective-permute-start | bytes 3145736 | tf_op jit(solution)/shard_map/ppermute | solution.py:68
  443.7 54.0 %collective-permute-start.24 = (f32[256,1024]{1,0:T(8,128)}, f32[256,1024]{1,0:T(8,128)S(1)}, u32[]{:S(2)}, u32[]{:S(2)}) collective-permute-start(f32[256,1024]{1,0:T(8,128)} %get-tuple-element.58), channel_id=1, source_target_pairs={{0,32},{1,33},{2,34},{3,35},{4,36},{5,37},{6,38},{7,39},{8,40},{9,... | collective-permute-start | bytes 3145736 | tf_op jit(solution)/shard_map/ppermute | solution.py:68
  457.4 37.4 %collective-permute-start.61 = (f32[4,384,128]{2,1,0:T(8,128)S(1)}, f32[4,384,128]{2,1,0:T(8,128)}, u32[]{:S(2)}, u32[]{:S(2)}) collective-permute-start(f32[4,384,128]{2,1,0:T(8,128)S(1)} %pad_maximum_fusion.2.own_ref), channel_id=1, source_target_pairs={{0,1},{1,0},{2,3},{3,2},{4,5},{5,4},{6,7},{7,6},{8,9},{9,8},{10,11... | collective-permute-start | bytes 2359304 | tf_op jit(solution)/shard_map/ppermute | solution.py:68
  458.4 52.0 %collective-permute-start.25 = (f32[256,1024]{1,0:T(8,128)}, f32[256,1024]{1,0:T(8,128)}, u32[]{:S(2)}, u32[]{:S(2)}) collective-permute-start(f32[256,1024]{1,0:T(8,128)} %get-tuple-element.59), channel_id=1, source_target_pairs={{0,64},{1,65},{2,66},{3,67},{4,68},{5,69},{6,70},{7,71},{8,72},{9,... | collective-permute-start | bytes 3145736 | tf_op jit(solution)/shard_map/ppermute | solution.py:68
  481.6 47.3 %collective-permute-start.26 = (f32[256,1024]{1,0:T(8,128)}, f32[256,1024]{1,0:T(8,128)}, u32[]{:S(2)}, u32[]{:S(2)}) collective-permute-start(f32[256,1024]{1,0:T(8,128)} %get-tuple-element.60), channel_id=1, source_target_pairs={{0,96},{1,97},{2,98},{3,99},{4,100},{5,101},{6,102},{7,103},{8,104... | collective-permute-start | bytes 3145736 | tf_op jit(solution)/shard_map/ppermute | solution.py:68
  493.3 45.6 %collective-permute-start.3 = (f32[256,1024]{1,0:T(8,128)}, f32[256,1024]{1,0:T(8,128)S(1)}, u32[]{:S(2)}, u32[]{:S(2)}) collective-permute-start(f32[256,1024]{1,0:T(8,128)} %get-tuple-element.45), channel_id=1, source_target_pairs={{0,32},{1,33},{2,34},{3,35},{4,36},{5,37},{6,38},{7,39},{8,40},{9,... | collective-permute-start | bytes 3145736 | tf_op jit(solution)/shard_map/ppermute | solution.py:68
  494.8 55.6 %collective-permute-start.4 = (f32[256,1024]{1,0:T(8,128)}, f32[256,1024]{1,0:T(8,128)S(1)}, u32[]{:S(2)}, u32[]{:S(2)}) collective-permute-start(f32[256,1024]{1,0:T(8,128)} %get-tuple-element.46), channel_id=1, source_target_pairs={{0,64},{1,65},{2,66},{3,67},{4,68},{5,69},{6,70},{7,71},{8,72},{9,... | collective-permute-start | bytes 3145736 | tf_op jit(solution)/shard_map/ppermute | solution.py:68
  497.7 75.7 %collective-permute-start.5 = (f32[256,1024]{1,0:T(8,128)}, f32[256,1024]{1,0:T(8,128)}, u32[]{:S(2)}, u32[]{:S(2)}) collective-permute-start(f32[256,1024]{1,0:T(8,128)} %get-tuple-element.47), channel_id=1, source_target_pairs={{0,96},{1,97},{2,98},{3,99},{4,100},{5,101},{6,102},{7,103},{8,104... | collective-permute-start | bytes 3145736 | tf_op jit(solution)/shard_map/ppermute | solution.py:68
  (69 other events, 655.5 us)
Sparse Core Ops, SparseCore 0:
  18.5 66.2 all-gather.4
  86.5 44.6 all-gather.2

commit v2 on v1

--- a/solution.py
+++ b/solution.py
@@ -10,8 +10,6 @@
 
 
 INTERPRET = False
-CHUNKS = 2
-FIRST_STEPS = 1
 ALL = ("z", "xh", "xl", "y", "core")
 VMEM = pl.BlockSpec(memory_space=pltpu.VMEM)
 SMEM = pl.BlockSpec(memory_space=pltpu.SMEM)
@@ -92,9 +90,22 @@
     return jnp.concatenate(rows, axis=0)
 
 
-def eliminate(w_ref, x_ref, low_step, high_step):
+def corner_kernel(spot_ref, *refs):
+    pieces = refs[:4]
+    x_ref, square_ref, w_ref = refs[-3:]
     n = x_ref.shape[0]
     nb = n // 4
+    part = pieces[0].shape[1]
+    z = spot_ref[0]
+    core = spot_ref[4]
+    for q in range(4):
+        for i in range(4):
+            side = core if i < 2 else 1 - core
+            row = pl.multiple_of((i % 2) * (n // 2) + side * (n // 4) + (z ^ q) * part, part)
+            w_ref[pl.ds(row, part), :] = pieces[q][i]
+    ri = lax.broadcasted_iota(jnp.int32, (n, n), 0)
+    ci = lax.broadcasted_iota(jnp.int32, (n, n), 1)
+    x_ref[...] = jnp.where(ri == ci, 1.0, 0.0).astype(F32)
 
     def step(j, carry):
         at = pl.multiple_of(j * nb, nb)
@@ -108,55 +119,22 @@
         x_ref[...] = x_ref[...] - dot(low, xr, NN)
         return carry
 
-    lax.fori_loop(low_step, high_step, step, 0)
-
-
-def corner_kernel(spot_ref, *refs):
-    pieces = refs[:4]
-    x_ref, w_ref = refs[-2:]
-    n = x_ref.shape[0]
-    part = pieces[0].shape[1]
-    z = spot_ref[0]
-    core = spot_ref[4]
-    for q in range(4):
-        for i in range(4):
-            side = core if i < 2 else 1 - core
-            row = pl.multiple_of((i % 2) * (n // 2) + side * (n // 4) + (z ^ q) * part, part)
-            w_ref[pl.ds(row, part), :] = pieces[q][i]
-    ri = lax.broadcasted_iota(jnp.int32, (n, n), 0)
-    ci = lax.broadcasted_iota(jnp.int32, (n, n), 1)
-    x_ref[...] = jnp.where(ri == ci, 1.0, 0.0).astype(F32)
-    eliminate(w_ref, x_ref, 0, FIRST_STEPS)
-
-
-def corner_end_kernel(x_in, w_in, x_ref, square_ref, w_ref):
-    x_ref[...] = x_in[...]
-    w_ref[...] = w_in[...]
-    eliminate(w_ref, x_ref, FIRST_STEPS, 4)
+    lax.fori_loop(0, 4, step, 0)
     x = x_ref[...]
     square_ref[...] = dot(x, x, TN)
 
 
 def inverse_factor(spot, pieces):
     n = pieces[0].shape[2]
-    square = shape(n, n)
-    state = pl.pallas_call(
+    return pl.pallas_call(
         corner_kernel,
-        out_shape=[square, square],
+        out_shape=[shape(n, n), shape(n, n)],
         in_specs=[SMEM] + [VMEM] * 4,
         out_specs=[VMEM, VMEM],
-        interpret=INTERPRET,
-        name="inverse_start",
+        scratch_shapes=[pltpu.VMEM((n, n), F32)],
+        interpret=INTERPRET,
+        name="inverse_factor",
     )(spot, *pieces)
-    return pl.pallas_call(
-        corner_end_kernel,
-        out_shape=[square, square],
-        in_specs=[VMEM, VMEM],
-        out_specs=[VMEM, VMEM],
-        scratch_shapes=[pltpu.VMEM((n, n), F32)],
-        interpret=INTERPRET,
-        name="inverse_end",
-    )(*state)
 
 
 def corner_lines(panel):
@@ -183,88 +161,42 @@
     return [value] + [swap(value, dz=d) for d in (1, 2, 3)]
 
 
-def pack_first_kernel(spot_ref, factor_ref, damping_ref, out_ref, hold, *, chunk, width):
+def pack_kernel(spot_ref, factor_ref, damping_ref, out_ref, hold):
     rows = hold.shape[0]
     part = damping_ref.shape[1]
+    count, _, cols = out_ref.shape
+    width = cols // 4
     z, xh, xl, y, core = (spot_ref[i] for i in range(5))
     hold[...] = factor_ref[...]
     device = (((z * 2 + xh) * 2 + xl) * 4 + y) * 2 + core
     at = pl.multiple_of(device * part, part)
     lane = lax.broadcasted_iota(jnp.int32, (rows, part), 1)
     sub = lax.broadcasted_iota(jnp.int32, (rows, part), 0)
-    add = jnp.where(lane == sub + chunk * rows, jnp.broadcast_to(damping_ref[...], (rows, part)), 0.0)
+    damping = jnp.broadcast_to(damping_ref[...], (rows, part))
+    add = jnp.where(lane == sub + pl.program_id(0) * rows, damping, 0.0)
     hold[:, pl.ds(at, part)] = hold[:, pl.ds(at, part)] + add
-    for m in range(8):
-        for side in range(2):
-            for b in range(4):
-                col = (b * 2 + side) * 8 + m
-                out_ref[m, :, (side * 4 + b) * width : (side * 4 + b + 1) * width] = hold[
-                    :, col * width : (col + 1) * width
-                ]
-
-
-def pack_first(spot, factor, damping, chunk):
+    for m in range(count):
+        for b in range(4):
+            col = b * count + m
+            out_ref[m, :, b * width : (b + 1) * width] = hold[:, col * width : (col + 1) * width]
+
+
+def send_tiles(spot, factor, damping):
     part, order = factor.shape
-    rows = part // CHUNKS
-    width = order // 64
-    return pl.pallas_call(
-        functools.partial(pack_first_kernel, chunk=chunk, width=width),
-        out_shape=shape(8, rows, 8 * width),
-        grid=(1,),
-        in_specs=[SMEM, pl.BlockSpec((rows, order), lambda i: (chunk, 0)), VMEM],
-        out_specs=VMEM,
+    rows = part // 4
+    cols = order // 16
+    packed = pl.pallas_call(
+        pack_kernel,
+        out_shape=shape(16, part, cols),
+        grid=(4,),
+        in_specs=[SMEM, pl.BlockSpec((rows, order), lambda i: (i, 0)), VMEM],
+        out_specs=pl.BlockSpec((16, rows, cols), lambda i: (0, i, 0)),
         scratch_shapes=[pltpu.VMEM((rows, order), F32)],
         interpret=INTERPRET,
-        name="pack_first",
+        name="pack_tiles",
     )(spot, factor, damping)
-
-
-def pack_second_kernel(spot_ref, in_ref, *refs):
-    outs = refs[-4:]
-    rows = in_ref.shape[1]
-    half = in_ref.shape[2] // 2
-    xh, xl = spot_ref[1], spot_ref[2]
-    for n in range(4):
-        col = pl.multiple_of((xl ^ (n & 1)) * half, half)
-        for y1 in range(2):
-            for k in range(2):
-                m = y1 * 4 + (xh ^ (n >> 1)) * 2 + k
-                at = (y1 * 2 + k) * rows
-                outs[n][at : at + rows, :] = in_ref[m, :, pl.ds(col, half)]
-
-
-def pack_third_kernel(spot_ref, *refs):
-    ins, outs = refs[:4], refs[-4:]
-    half = ins[0].shape[0] // 2
-    z, xl = spot_ref[0], spot_ref[2]
-    flip = (xl ^ (z >> 1)) == 1
-    for q in range(4):
-        row = pl.multiple_of(((z & 1) ^ (q & 1)) * half, half)
-        for n1 in range(2):
-            same = ins[n1 * 2 + (q >> 1)][pl.ds(row, half), :]
-            changed = ins[n1 * 2 + 1 - (q >> 1)][pl.ds(row, half), :]
-            outs[q][n1 * half : (n1 + 1) * half, :] = jnp.where(flip, changed, same)
-
-
-def repack(kernel, spot, arrays, out, after=()):
-    return pl.pallas_call(
-        kernel,
-        out_shape=[out] * 4,
-        in_specs=[SMEM] + [VMEM] * len(arrays) + [ANY] * len(after),
-        out_specs=[VMEM] * 4,
-        interpret=INTERPRET,
-    )(spot, *arrays, *after)
-
-
-def send_chunk(spot, factor, damping, chunk, after):
-    first = pack_first(spot, factor, damping, chunk)
-    first = lax.all_to_all(first, ("y", "core"), 0, 0, tiled=True)
-    _, rows, cols = first.shape
-    out = shape(4 * rows, cols // 2)
-    second = repack(pack_second_kernel, spot, [first], out, after)
-    second = [second[n] if n == 0 else swap(second[n], dx=n) for n in range(4)]
-    third = repack(pack_third_kernel, spot, second, out)
-    return [third[q] if q == 0 else swap(third[q], dz=q) for q in range(4)]
+    packed = lax.all_to_all(packed, ("xl", "y", "core"), 0, 0, tiled=True)
+    return lax.all_to_all(packed.reshape(8, 2 * part, cols), ("z", "xh"), 0, 0, tiled=True)
 
 
 def panel_kernel(spot_ref, x_ref, rows_ref, cols_ref, row_ref, col_ref, tile_ref):
@@ -308,67 +240,42 @@
     return lax.ppermute(panel, ALL, pairs)
 
 
-def update_kernel(spot_ref, *refs):
-    blocks = refs[:4]
-    row_ref, col_ref = refs[4:6]
-    out_ref, high_ref, low_ref, hold = refs[-4:]
-    count, _, rows, width = row_ref.shape
-    xh = spot_ref[1]
-    step = pl.program_id(0)
-    half = 2 * rows
-
-    @pl.when(step == 0)
+def update_kernel(block_ref, row_ref, col_ref, out_ref, high_ref, low_ref, hold):
+    @pl.when(pl.program_id(0) == 0)
     def _():
         high_ref[...], low_ref[...] = halves(col_ref[...])
 
-    for q in range(4):
-
-        @pl.when(step == q)
-        def _():
-            for n in range(2):
-                at = pl.multiple_of((xh ^ n) * half, half)
-                hold[pl.ds(at, half), :] = blocks[q][n * half : (n + 1) * half, :]
-
-    left = halves(row_ref[...].reshape(count * rows, width))
-    hold[...] = hold[...] - dot3(left, (high_ref[...], low_ref[...]), NT)
-    lanes = out_ref.shape[3]
-    groups = hold.shape[1] // lanes
-    for i in range(count):
-        for g in range(groups):
-            out_ref.at[i, 0][pl.ds(g, rows, stride=groups), :] = hold[
-                i * rows : (i + 1) * rows, g * lanes : (g + 1) * lanes
-            ]
-
-
-def update(spot, blocks, row_factor, col_factor, out, chunk):
-    height, local_cols = blocks[0].shape
-    rows = height // 4
+    left = halves(row_ref[...])
+    hold[...] = block_ref[0] - dot3(left, (high_ref[...], low_ref[...]), NT)
+    rows, cols = hold.shape
+    lanes = out_ref.shape[1]
+    groups = cols // lanes
+    for g in range(groups):
+        out_ref[pl.ds(g, rows, stride=groups), :] = hold[:, g * lanes : (g + 1) * lanes]
+
+
+def update(blocks, row_factor, col_factor):
+    count, rows, cols = blocks.shape
     width = row_factor.shape[1]
-    lanes = local_cols // 8
-    first = out is None
-    full = lambda a: pl.BlockSpec(a.shape, lambda i, s: (0, 0))
-    place = lambda i, s: (s[0] ^ i, chunk, 0, 0)
-    operands = [*blocks, row_factor.reshape(16, CHUNKS, rows, width), col_factor]
+    lanes = cols // 8
     return pl.pallas_call(
         update_kernel,
-        out_shape=shape(16, CHUNKS, rows * 8, lanes),
-        grid_spec=pltpu.PrefetchScalarGridSpec(
-            num_scalar_prefetch=1,
-            grid=(4,),
-            in_specs=[full(b) for b in blocks]
-            + [pl.BlockSpec((4, 1, rows, width), place), full(col_factor)]
-            + ([] if first else [ANY]),
-            out_specs=pl.BlockSpec((4, 1, rows * 8, lanes), place),
-            scratch_shapes=[
-                pltpu.VMEM(col_factor.shape, jnp.bfloat16),
-                pltpu.VMEM(col_factor.shape, jnp.bfloat16),
-                pltpu.VMEM((height, local_cols), F32),
-            ],
-        ),
-        input_output_aliases={} if first else {7: 0},
+        out_shape=shape(count * rows * 8, lanes),
+        grid=(count,),
+        in_specs=[
+            pl.BlockSpec((1, rows, cols), lambda i: (i, 0, 0)),
+            pl.BlockSpec((rows, width), lambda i: (i, 0)),
+            pl.BlockSpec(col_factor.shape, lambda i: (0, 0)),
+        ],
+        out_specs=pl.BlockSpec((rows * 8, lanes), lambda i: (i, 0)),
+        scratch_shapes=[
+            pltpu.VMEM(col_factor.shape, jnp.bfloat16),
+            pltpu.VMEM(col_factor.shape, jnp.bfloat16),
+            pltpu.VMEM((rows, cols), F32),
+        ],
         interpret=INTERPRET,
         name="update",
-    )(spot, *operands, *([] if first else [out]))
+    )(blocks, row_factor, col_factor)
 
 
 def on_line(z, x, y, core):
@@ -539,28 +446,28 @@
 
     from_first = lambda zz, xx, yy, cc: zz == 0 and xx == 0
     from_second = lambda zz, xx, yy, cc: zz == 0 and xx == 1
+    got = corner_lines(panel)
     lead = [swap(panel, dx=2, only=from_first), swap(panel, dx=3, only=from_second), panel]
-    got = corner_lines(panel)
+    second = swap(factor[:, panel_width : 3 * panel_width], dx=3, only=from_second)
+    corner_own = corner_both(panel, got, y)
+    corner_other = swap(corner_own, dcore=1, only=from_first)
     rows_share = share_rows(panel)
     cols_share = share_cols(panel)
-    corner_own = corner_both(panel, got, y)
-    corner_other = swap(corner_own, dcore=1, only=from_first)
+    pieces = spread_corner(corner_own, corner_other, z, x)
+    rows_in = lax.all_gather(rows_share, ("xl", "y", "core"), tiled=True)
+    cols_in = lax.all_gather(cols_share, ("z", "xh"), tiled=True)
+    blocks = send_tiles(spot, factor, damping[None, :])
+
     ends = jnp.where(y < 2, lead[2], lead[0])
     ends = jnp.concatenate([lead[1], ends], axis=0)
     lines = jnp.stack([ends] + [swap(ends, dy=m, only=on_line) for m in (1, 2, 3)])
-    lines_other = swap(lines, dcore=1, only=on_line)
-    pieces = spread_corner(corner_own, corner_other, z, x)
-    rows_in = lax.all_gather(rows_share, ("xl", "y", "core"), tiled=True)
-    cols_in = lax.all_gather(cols_share, ("z", "xh"), tiled=True)
-    second = swap(factor[:, panel_width : 3 * panel_width], dx=3, only=from_second)
     lower = [
         lead[0],
         jnp.concatenate([lead[1], second], axis=1),
         factor[:, : 5 * panel_width],
     ]
     lower_other = [swap(value, dcore=1, only=on_line) for value in lower]
-
-    stages = [send_chunk(spot, factor, damping[None, :], chunk, ()) for chunk in range(CHUNKS)]
+    lines_other = swap(lines, dcore=1, only=on_line)
 
     x_inverse, inverse = inverse_factor(spot, pieces)
     panels = place_panels(spot, lines, lines_other)
@@ -569,9 +476,7 @@
     solved = forward_solve(spot, x_inverse, inverse, gradients, inverses, panels, lower, lower_other)
     solution_rows = spread_solution(spot, solved, z, x, y, core)
 
-    out = None
-    for chunk in range(CHUNKS):
-        out = update(spot, stages[chunk], row_factor, col_factor, out, chunk)
+    out = update(blocks, row_factor, col_factor)
     tile = order // 64
     updated = out.reshape(8, 1, tile, 4, 1, tile)
     panel_tiles = tiles.reshape(8, 1, part // 8, panel_width)

time: 597 us -> 635 us (1.064)
  waiting for transfers between devices: 142 us -> 307 us
  starting transfers between devices: 241 us -> 149 us
  Pallas kernels: 167 us -> 138 us
    ppermute x60 -> x48, starting transfers between devices: 222 us -> 106 us  [swap(): return lax.ppermute(value, ALL, pairs)]
    ppermute x1, waiting for transfers between devices: 3.29 us -> 115 us  [share_cols(): return lax.ppermute(panel, ALL, pairs)]
    ppermute x60 -> x48, waiting for transfers between devices: 139 us -> 192 us  [swap(): return lax.ppermute(value, ALL, pairs)]
    pallas_call x10 -> x3, Pallas kernels: 109 us -> 79.9 us  [the longest x1 58.3 us: inverse_factor(): pl.pallas_call(corner_kernel, out_shape=[shape(n, n), shape(n, n)], in_sp...]
    all_to_all x2, starting transfers between devices: 12.7 us -> 38.2 us  [the longest x1 31.2 us: send_tiles(): lax.all_to_all(packed.reshape(8, 2 * part, cols), ('z', 'xh'), 0, 0, tile...]
  transfers between devices with their start and end apart: 66 -> 54, of which waited for: 13 -> 12; matrix products, arithmetic and copies ran while one was open for 3% -> 2% of each run, Pallas kernels for 27% -> 18%
where the time goes in v2:
time: 635 us; the launch traced here: 633 us
  waiting for transfers between devices  307 us (48%)
  starting transfers between devices  149 us (23%)
  Pallas kernels  138 us (22%)
  local copies, waits for them, and re-layouts  17.6 us (3%)
  between operations  14.9 us (2%)
    ppermute x48, waiting for transfers between devices, swap(): return lax.ppermute(value, ALL, pairs)  192 us
    ppermute x1, waiting for transfers between devices, share_cols(): return lax.ppermute(panel, ALL, pairs)  115 us
    ppermute x48, starting transfers between devices, swap(): return lax.ppermute(value, ALL, pairs)  106 us
    pallas_call x1, Pallas kernels, inverse_factor(): pl.pallas_call(corner_kernel, out_shape=[shape(n, n), shape(n, n)], in_sp...  58.3 us
    pallas_call x6, Pallas kernels, forward_solve(): result = run(*operands)  39.8 us
    all_to_all x1, starting transfers between devices, send_tiles(): lax.all_to_all(packed.reshape(8, 2 * part, cols), ('z', 'xh'), 0, 0, tile...  31.2 us
    pallas_call x1, Pallas kernels, update(): pl.pallas_call(update_kernel, out_shape=shape(count * rows * 8, lanes), g...  14.3 us
  transfers between devices with their start and end apart: 54, of which 12 were waited for; matrix products, arithmetic and copies ran while one was open for 2% of the time, Pallas kernels for 18%

profile of v2, /device:TPU:1, one launch (start us, length us, event | category | flops | bytes accessed | tf_op | source)
XLA Modules:
  0.0 632.7 jit_solution(3339167085735974387)
XLA Ops:
  7.9 7.4 %pack_tiles.1 = f32[16,128,1024]{2,1,0:T(8,128)} custom-call(s32[5]{0:T(128)} %stack.62.spot_ref, f32[128,16384]{1,0:T(8,128)} %factor_ref.1, f32[1,128]{1,0:T(1,128)} %bitcast.32), custom_call_target="tpu_custom_call" | custom-call | tf_op jit(solution)/shard_map/pack_tiles/pallas_call | solution.py:188
  15.3 7.0 %all-to-all-start = ((f32[16,128,1024]{2,1,0:T(8,128)}), f32[16,128,1024]{2,1,0:T(8,128)}, u32[]{:S(2)}, u32[]{:S(2)}) async-start(f32[16,128,1024]{2,1,0:T(8,128)} %pack_tiles.1), calls=%async_computation | async-start | bytes 16777216 | tf_op jit(solution)/shard_map/all_to_all | solution.py:198
  23.4 4.4 collective-permute-start.14
  27.8 114.6 %collective-permute-done.14 = f32[128,512]{1,0:T(8,128)S(1)} collective-permute-done((f32[128,512]{1,0:T(8,128)S(1)}, f32[128,512]{1,0:T(8,128)S(1)}, u32[]{:S(2)}, u32[]{:S(2)}) %collective-permute-start.14) | collective-permute-done | bytes 262176 | tf_op jit(solution)/shard_map/ppermute | solution.py:240
  144.6 31.2 %all-to-all-start.1 = ((f32[8,256,1024]{2,1,0:T(8,128)}), f32[8,256,1024]{2,1,0:T(8,128)}, u32[]{:S(2)}, u32[]{:S(2)}) async-start(f32[8,256,1024]{2,1,0:T(8,128)} %bitcast.6), calls=%async_computation.1 | async-start | bytes 16777216 | tf_op jit(solution)/shard_map/all_to_all | solution.py:199
  175.8 5.6 collective-permute-start.15
  182.7 3.6 collective-permute-start.1
  188.9 93.6 %collective-permute-done.15.refs_2_ = f32[128,512]{1,0:T(8,128)} collective-permute-done((f32[128,512]{1,0:T(8,128)S(1)}, f32[128,512]{1,0:T(8,128)}, u32[]{:S(2)}, u32[]{:S(2)}) %collective-permute-start.15) | collective-permute-done | bytes 262176 | tf_op jit(solution)/shard_map/ppermute | solution.py:66
  288.0 2.1 collective-permute-start.24
  292.4 2.0 collective-permute-start.6
  294.4 2.0 collective-permute-start.4
  299.8 4.0 collective-permute-done.4
  307.6 42.0 %collective-permute-start.8 = (f32[4,32,512]{2,1,0:T(8,128)}, f32[4,32,512]{2,1,0:T(8,128)}, u32[]{:S(2)}, u32[]{:S(2)}) collective-permute-start(f32[4,32,512]{2,1,0:T(8,128)} %slice_select_fusion), channel_id=1, source_target_pairs={{0,16},{1,17},{2,18},{3,19},{4,20},{5,21},{6,22},{7,23},{32,48},{3... | collective-permute-start | bytes 786440 | tf_op jit(solution)/shard_map/ppermute | solution.py:66
  349.6 2.4 collective-permute-start.7
  361.9 14.6 %collective-permute-done.12.refs_3_ = f32[4,32,512]{2,1,0:T(8,128)S(1)} collective-permute-done((f32[4,32,512]{2,1,0:T(8,128)S(1)}, f32[4,32,512]{2,1,0:T(8,128)S(1)}, u32[]{:S(2)}, u32[]{:S(2)}) %collective-permute-start.12) | collective-permute-done | bytes 262176 | tf_op jit(solution)/shard_map/ppermute | solution.py:66
  378.6 5.0 collective-permute-done.10.refs_1_
  383.6 58.3 %inverse_factor.1 = (f32[512,512]{1,0:T(8,128)}, f32[512,512]{1,0:T(8,128)}) custom-call(s32[5]{0:T(128)} %stack.62.spot_ref, f32[4,32,512]{2,1,0:T(8,128)} %copy-done.6, f32[4,32,512]{2,1,0:T(8,128)} %collective-permute-done.10.refs_1_, f32[4,32,512]{2,1,0:T(8,128)} %copy-done.13, f32[4,32,512]{2,1,0:T(8,128)} %copy-done.12), custom_call_target="tpu_custom_call" | custom-call | tf_op jit(solution)/shard_map/inverse_factor/pallas_call | solution.py:129
  441.9 4.6 solve.6
  449.4 6.1 place_panels.1.refs_7_
  456.2 7.3 %solve.7 = (f32[512,128]{1,0:T(8,128)}, f32[512,128]{1,0:T(8,128)}, f32[256,128]{1,0:T(8,128)}) custom-call(s32[5]{0:T(128)} %stack.62.spot_ref, f32[3072,128]{1,0:T(8,128)} %refs_0_.11, f32[256,128]{1,0:T(8,128)} %get-tuple-element.27.refs_1_, f32[256,128]{1,0:T(8,128)} %copy-done.23, f32[256,128]{1,0:T(8,128)} %collective-permute-done.18.refs_3_, ...), custom_call_target="tpu_custom_call" | custom-call | tf_op jit(solution)/shard_map/solve/pallas_call | solution.py:397
  466.3 7.7 %solve.8 = (f32[512,128]{1,0:T(8,128)}, f32[512,128]{1,0:T(8,128)}, f32[256,128]{1,0:T(8,128)}) custom-call(s32[5]{0:T(128)} %stack.62.spot_ref, f32[3072,128]{1,0:T(8,128)} %refs_0_.11, f32[256,128]{1,0:T(8,128)} %get-tuple-element.31.refs_1_, f32[256,128]{1,0:T(8,128)} %copy-done.26, f32[256,128]{1,0:T(8,128)} %copy-done.24, f32[256,128]{1,0:T(8,128)} %copy-done.21, ...), custom_call_target="tpu_custom_call" | custom-call | tf_op jit(solution)/shard_map/solve/pallas_call | solution.py:397
  476.8 8.3 %solve.9 = (f32[512,128]{1,0:T(8,128)}, f32[512,128]{1,0:T(8,128)}, f32[256,128]{1,0:T(8,128)}) custom-call(s32[5]{0:T(128)} %stack.62.spot_ref, f32[3072,128]{1,0:T(8,128)} %refs_0_.11, f32[256,128]{1,0:T(8,128)} %get-tuple-element.34.refs_1_, f32[256,128]{1,0:T(8,128)} %copy-done.16, f32[256,128]{1,0:T(8,128)} %copy-done.15, f32[256,128]{1,0:T(8,128)} %copy-done.14, ...), custom_call_target="tpu_custom_call" | custom-call | tf_op jit(solution)/shard_map/solve/pallas_call | solution.py:397
  488.3 8.6 %solve.10 = (f32[512,128]{1,0:T(8,128)}, f32[512,128]{1,0:T(8,128)}, f32[256,128]{1,0:T(8,128)}) custom-call(s32[5]{0:T(128)} %stack.62.spot_ref, f32[3072,128]{1,0:T(8,128)} %refs_0_.11, f32[256,128]{1,0:T(8,128)} %get-tuple-element.37.refs_1_, f32[256,128]{1,0:T(8,128)} %copy-done.20, f32[256,128]{1,0:T(8,128)} %copy-done.19, f32[256,128]{1,0:T(8,128)} %copy-done.17, ...), custom_call_target="tpu_custom_call" | custom-call | tf_op jit(solution)/shard_map/solve/pallas_call | solution.py:397
  501.3 3.2 solve.11
  508.2 65.1 %collective-permute-done.41 = f32[384,128]{1,0:T(8,128)S(1)} collective-permute-done((f32[384,128]{1,0:T(8,128)S(1)}, f32[384,128]{1,0:T(8,128)S(1)}, u32[]{:S(2)}, u32[]{:S(2)}) %collective-permute-start.41) | collective-permute-done | bytes 196640 | tf_op jit(solution)/shard_map/ppermute | solution.py:66
  578.5 2.1 collective-permute-done.43
  581.3 3.3 collective-permute-start.47
  584.6 4.0 collective-permute-done.48
  589.4 7.1 %collective-permute-start.49 = (f32[4,384,128]{2,1,0:T(8,128)S(1)}, f32[4,384,128]{2,1,0:T(8,128)S(1)}, u32[]{:S(2)}, u32[]{:S(2)}) collective-permute-start(f32[4,384,128]{2,1,0:T(8,128)S(1)} %pad_maximum_fusion.2.own_ref), channel_id=1, source_target_pairs={{0,1},{1,0},{2,3},{3,2},{4,5},{5,4},{6,7},{7,6},{8,9},{9,8},{10,11... | collective-permute-start | bytes 2359304 | tf_op jit(solution)/shard_map/ppermute | solution.py:66
  599.3 2.6 place_rows.1
  601.9 9.7 %panel_solve.1 = (f32[2048,512]{1,0:T(8,128)}, f32[1024,512]{1,0:T(8,128)}, f32[128,512]{1,0:T(8,128)}) custom-call(s32[5]{0:T(128)} %stack.62.spot_ref, f32[512,512]{1,0:T(8,128)} %get-tuple-element.22.x_ref.refs_1_, f32[2048,512]{1,0:T(8,128)} %all-gather.3.cloned.1.call-done.rows_ref, f32[1024,512]{1,0:T(8,128)} %all-gather.5.cloned.1.call-done.cols_ref), custom_call_target="tpu_custom_call" | custom-call | tf_op jit(solution)/shard_map/panel_solve/pallas_call | solution.py:217
  611.6 14.3 %update.1 = f32[16384,128]{1,0:T(8,128)} custom-call(f32[8,256,1024]{2,1,0:T(8,128)} %all-to-all-done.1.block_ref, f32[2048,512]{1,0:T(8,128)} %get-tuple-element.23.row_ref, f32[1024,512]{1,0:T(8,128)} %get-tuple-element.24.col_ref), custom_call_target="tpu_custom_call" | custom-call | tf_op jit(solution)/shard_map/update/pallas_call | solution.py:261
  (173 shorter events, 64.2 us)
Async XLA Ops:
  15.3 129.3 %all-to-all-start = ((f32[16,128,1024]{2,1,0:T(8,128)}), f32[16,128,1024]{2,1,0:T(8,128)}, u32[]{:S(2)}, u32[]{:S(2)}) async-start(f32[16,128,1024]{2,1,0:T(8,128)} %pack_tiles.1), calls=%async_computation | async-start | bytes 16777216 | tf_op jit(solution)/shard_map/all_to_all | solution.py:198
  22.3 579.6 %all-gather.5.cloned.1.call-start = ((), (), s32[]{:S(2)}) async-start(), calls=%async_computation.3 | async-start | bytes 2359296 | tf_op jit(solution)/shard_map/all_gather | solution.py:458
  23.4 119.0 %collective-permute-start.14 = (f32[128,512]{1,0:T(8,128)S(1)}, f32[128,512]{1,0:T(8,128)S(1)}, u32[]{:S(2)}, u32[]{:S(2)}) collective-permute-start(f32[128,512]{1,0:T(8,128)S(1)} %select_add_fusion), channel_id=1, source_target_pairs={{0,0},{1,16},{2,1},{3,17},{4,2},{5,18},{6,3},{7,19},{8,4},{9,20},{... | collective-permute-start | bytes 786440 | tf_op jit(solution)/shard_map/ppermute | solution.py:240
  143.1 458.8 %all-gather.3.cloned.1.call-start = ((), (), s32[]{:S(2)}) async-start(), calls=%async_computation.2 | async-start | bytes 4456448 | tf_op jit(solution)/shard_map/all_gather | solution.py:457
  144.6 467.0 %all-to-all-start.1 = ((f32[8,256,1024]{2,1,0:T(8,128)}), f32[8,256,1024]{2,1,0:T(8,128)}, u32[]{:S(2)}, u32[]{:S(2)}) async-start(f32[8,256,1024]{2,1,0:T(8,128)} %bitcast.6), calls=%async_computation.1 | async-start | bytes 16777216 | tf_op jit(solution)/shard_map/all_to_all | solution.py:199
  175.8 106.6 %collective-permute-start.15 = (f32[128,512]{1,0:T(8,128)S(1)}, f32[128,512]{1,0:T(8,128)}, u32[]{:S(2)}, u32[]{:S(2)}) collective-permute-start(f32[128,512]{1,0:T(8,128)S(1)} %select_add_fusion), channel_id=1, source_target_pairs={{0,16},{1,17},{2,18},{3,19},{4,20},{5,21},{6,22},{7,23}} | collective-permute-start | bytes 786440 | tf_op jit(solution)/shard_map/ppermute | solution.py:66
  181.4 101.1 %collective-permute-start.2 = (f32[128,512]{1,0:T(8,128)S(1)}, f32[128,512]{1,0:T(8,128)S(1)}, u32[]{:S(2)}, u32[]{:S(2)}) collective-permute-start(f32[128,512]{1,0:T(8,128)S(1)} %select_add_fusion), channel_id=1, source_target_pairs={{0,6},{1,7},{2,4},{3,5}} | collective-permute-start | bytes 786440 | tf_op jit(solution)/shard_map/ppermute | solution.py:66
  182.7 99.8 %collective-permute-start.1 = (f32[128,512]{1,0:T(8,128)S(1)}, f32[128,512]{1,0:T(8,128)S(1)}, u32[]{:S(2)}, u32[]{:S(2)}) collective-permute-start(f32[128,512]{1,0:T(8,128)S(1)} %select_add_fusion), channel_id=1, source_target_pairs={{0,4},{1,5},{2,6},{3,7}} | collective-permute-start | bytes 786440 | tf_op jit(solution)/shard_map/ppermute | solution.py:66
  186.3 96.2 %collective-permute-start = (f32[128,512]{1,0:T(8,128)S(1)}, f32[128,512]{1,0:T(8,128)S(1)}, u32[]{:S(2)}, u32[]{:S(2)}) collective-permute-start(f32[128,512]{1,0:T(8,128)S(1)} %select_add_fusion), channel_id=1, source_target_pairs={{0,2},{1,3},{2,0},{3,1}} | collective-permute-start | bytes 786440 | tf_op jit(solution)/shard_map/ppermute | solution.py:66
  188.2 95.4 %collective-permute-start.20 = (f32[128,512]{1,0:T(8,128)S(1)}, f32[128,512]{1,0:T(8,128)S(1)}, u32[]{:S(2)}, u32[]{:S(2)}) collective-permute-start(f32[128,512]{1,0:T(8,128)S(1)} %select_add_fusion), channel_id=1, source_target_pairs={{8,16},{9,17},{10,18},{11,19},{12,20},{13,21},{14,22},{15,23}} | collective-permute-start | bytes 786440 | tf_op jit(solution)/shard_map/ppermute | solution.py:66
  288.0 160.4 %collective-permute-start.24 = (f32[4,256,512]{2,1,0:T(8,128)S(1)}, f32[4,256,512]{2,1,0:T(8,128)}, u32[]{:S(2)}, u32[]{:S(2)}) collective-permute-start(f32[4,256,512]{2,1,0:T(8,128)S(1)} %pad_maximum_fusion.own_ref), channel_id=1, source_target_pairs={{16,17},{17,16},{18,19},{19,18},{20,21},{21,20},{22,23},{23,22}} | collective-permute-start | bytes 6291464 | tf_op jit(solution)/shard_map/ppermute | solution.py:66
  291.1 8.6 %collective-permute-start.5 = (f32[4,32,512]{2,1,0:T(8,128)}, f32[4,32,512]{2,1,0:T(8,128)S(1)}, u32[]{:S(2)}, u32[]{:S(2)}) collective-permute-start(f32[4,32,512]{2,1,0:T(8,128)} %get-tuple-element.44), channel_id=1, source_target_pairs={{0,64},{1,65},{2,66},{3,67},{4,68},{5,69},{6,70},{7,71}} | collective-permute-start | bytes 786440 | tf_op jit(solution)/shard_map/ppermute | solution.py:66
  292.4 7.4 %collective-permute-start.6 = (f32[4,32,512]{2,1,0:T(8,128)}, f32[4,32,512]{2,1,0:T(8,128)}, u32[]{:S(2)}, u32[]{:S(2)}) collective-permute-start(f32[4,32,512]{2,1,0:T(8,128)} %get-tuple-element.45), channel_id=1, source_target_pairs={{0,96},{1,97},{2,98},{3,99},{4,100},{5,101},{6,102},{7,103}} | collective-permute-start | bytes 786440 | tf_op jit(solution)/shard_map/ppermute | solution.py:66
  294.4 9.3 %collective-permute-start.4 = (f32[4,32,512]{2,1,0:T(8,128)}, f32[4,32,512]{2,1,0:T(8,128)}, u32[]{:S(2)}, u32[]{:S(2)}) collective-permute-start(f32[4,32,512]{2,1,0:T(8,128)} %get-tuple-element.46), channel_id=1, source_target_pairs={{0,32},{1,33},{2,34},{3,35},{4,36},{5,37},{6,38},{7,39}} | collective-permute-start | bytes 786440 | tf_op jit(solution)/shard_map/ppermute | solution.py:66
  298.3 55.1 %collective-permute-start.25 = (f32[128,1024]{1,0:T(8,128)}, f32[128,1024]{1,0:T(8,128)}, u32[]{:S(2)}, u32[]{:S(2)}) collective-permute-start(f32[128,1024]{1,0:T(8,128)} %slice.26), channel_id=1, source_target_pairs={{8,16},{9,17},{10,18},{11,19},{12,20},{13,21},{14,22},{15,23}} | collective-permute-start | bytes 1572872 | tf_op jit(solution)/shard_map/ppermute | solution.py:66
  305.6 53.3 %collective-permute-start.9 = (f32[4,32,512]{2,1,0:T(8,128)}, f32[4,32,512]{2,1,0:T(8,128)}, u32[]{:S(2)}, u32[]{:S(2)}) collective-permute-start(f32[4,32,512]{2,1,0:T(8,128)} %slice_select_fusion), channel_id=1, source_target_pairs={{0,24},{1,25},{2,26},{3,27},{4,28},{5,29},{6,30},{7,31},{32,56},{3... | collective-permute-start | bytes 786440 | tf_op jit(solution)/shard_map/ppermute | solution.py:66
  307.6 52.8 %collective-permute-start.8 = (f32[4,32,512]{2,1,0:T(8,128)}, f32[4,32,512]{2,1,0:T(8,128)}, u32[]{:S(2)}, u32[]{:S(2)}) collective-permute-start(f32[4,32,512]{2,1,0:T(8,128)} %slice_select_fusion), channel_id=1, source_target_pairs={{0,16},{1,17},{2,18},{3,19},{4,20},{5,21},{6,22},{7,23},{32,48},{3... | collective-permute-start | bytes 786440 | tf_op jit(solution)/shard_map/ppermute | solution.py:66
  349.6 10.9 %collective-permute-start.7 = (f32[4,32,512]{2,1,0:T(8,128)}, f32[4,32,512]{2,1,0:T(8,128)}, u32[]{:S(2)}, u32[]{:S(2)}) collective-permute-start(f32[4,32,512]{2,1,0:T(8,128)} %slice_select_fusion), channel_id=1, source_target_pairs={{0,8},{1,9},{2,10},{3,11},{4,12},{5,13},{6,14},{7,15},{32,40},{33,... | collective-permute-start | bytes 786440 | tf_op jit(solution)/shard_map/ppermute | solution.py:66
  353.4 122.6 %collective-permute-start.33 = (f32[128,2560]{1,0:T(8,128)S(1)}, f32[128,2560]{1,0:T(8,128)}, u32[]{:S(2)}, u32[]{:S(2)}) collective-permute-start(f32[128,2560]{1,0:T(8,128)S(1)} %slice.27.refs_11_.refs_12_), channel_id=1, source_target_pairs={{16,17},{17,16},{18,19},{19,18},{20,21},{21,20},{22,23},{23,22}} | collective-permute-start | bytes 3932168 | tf_op jit(solution)/shard_map/ppermute | solution.py:66
  358.8 96.6 %collective-permute-start.26 = (f32[128,1536]{1,0:T(8,128)}, f32[128,1536]{1,0:T(8,128)}, u32[]{:S(2)}, u32[]{:S(2)}) collective-permute-start(f32[128,1536]{1,0:T(8,128)} %constant_dynamic-update-slice_fusion.refs_9_.refs_10_), channel_id=1, source_target_pairs={{16,17},{17,16},{18,19},{19,18},{20,21},{21,20},{22,23},{23,22}} | collective-permute-start | bytes 2359304 | tf_op jit(solution)/shard_map/ppermute | solution.py:66
  361.7 14.7 %collective-permute-start.12 = (f32[4,32,512]{2,1,0:T(8,128)S(1)}, f32[4,32,512]{2,1,0:T(8,128)S(1)}, u32[]{:S(2)}, u32[]{:S(2)}) collective-permute-start(f32[4,32,512]{2,1,0:T(8,128)S(1)} %add_select_fusion.refs_0_), channel_id=1, source_target_pairs={{0,96},{1,97},{2,98},{3,99},{4,100},{5,101},{6,102},{7,103},{8,104... | collective-permute-start | bytes 786440 | tf_op jit(solution)/shard_map/ppermute | solution.py:66
  361.8 14.7 %collective-permute-start.11 = (f32[4,32,512]{2,1,0:T(8,128)S(1)}, f32[4,32,512]{2,1,0:T(8,128)S(1)}, u32[]{:S(2)}, u32[]{:S(2)}) collective-permute-start(f32[4,32,512]{2,1,0:T(8,128)S(1)} %add_select_fusion.refs_0_), channel_id=1, source_target_pairs={{0,64},{1,65},{2,66},{3,67},{4,68},{5,69},{6,70},{7,71},{8,72},{9,... | collective-permute-start | bytes 786440 | tf_op jit(solution)/shard_map/ppermute | solution.py:66
  376.5 7.1 %collective-permute-start.10 = (f32[4,32,512]{2,1,0:T(8,128)S(1)}, f32[4,32,512]{2,1,0:T(8,128)}, u32[]{:S(2)}, u32[]{:S(2)}) collective-permute-start(f32[4,32,512]{2,1,0:T(8,128)S(1)} %add_select_fusion.refs_0_), channel_id=1, source_target_pairs={{0,32},{1,33},{2,34},{3,35},{4,36},{5,37},{6,38},{7,39},{8,40},{9,... | collective-permute-start | bytes 786440 | tf_op jit(solution)/shard_map/ppermute | solution.py:66
  377.2 64.7 %collective-permute-start.16 = (f32[128,512]{1,0:T(8,128)}, f32[128,512]{1,0:T(8,128)}, u32[]{:S(2)}, u32[]{:S(2)}) collective-permute-start(f32[128,512]{1,0:T(8,128)} %collective-permute-done.15.refs_2_), channel_id=1, source_target_pairs={{16,17},{17,16},{18,19},{19,18},{20,21},{21,20},{22,23},{23,22}} | collective-permute-start | bytes 786440 | tf_op jit(solution)/shard_map/ppermute | solution.py:66
  446.5 9.0 %collective-permute-start.19 = (f32[256,128]{1,0:T(8,128)}, f32[256,128]{1,0:T(8,128)S(1)}, u32[]{:S(2)}, u32[]{:S(2)}) collective-permute-start(f32[256,128]{1,0:T(8,128)} %get-tuple-element.27.refs_1_), channel_id=1, source_target_pairs={{16,22},{17,23},{18,20},{19,21},{20,18},{21,19},{22,16},{23,17}} | collective-permute-start | bytes 393224 | tf_op jit(solution)/shard_map/ppermute | solution.py:66
  447.2 8.3 %collective-permute-start.18 = (f32[256,128]{1,0:T(8,128)}, f32[256,128]{1,0:T(8,128)}, u32[]{:S(2)}, u32[]{:S(2)}) collective-permute-start(f32[256,128]{1,0:T(8,128)} %get-tuple-element.27.refs_1_), channel_id=1, source_target_pairs={{16,20},{17,21},{18,22},{19,23},{20,16},{21,17},{22,18},{23,19}} | collective-permute-start | bytes 393224 | tf_op jit(solution)/shard_map/ppermute | solution.py:66
  448.5 7.0 %collective-permute-start.17 = (f32[256,128]{1,0:T(8,128)}, f32[256,128]{1,0:T(8,128)S(1)}, u32[]{:S(2)}, u32[]{:S(2)}) collective-permute-start(f32[256,128]{1,0:T(8,128)} %get-tuple-element.27.refs_1_), channel_id=1, source_target_pairs={{16,18},{17,19},{18,16},{19,17},{20,22},{21,23},{22,20},{23,21}} | collective-permute-start | bytes 393224 | tf_op jit(solution)/shard_map/ppermute | solution.py:66
  506.2 67.1 %collective-permute-start.41 = (f32[384,128]{1,0:T(8,128)S(1)}, f32[384,128]{1,0:T(8,128)S(1)}, u32[]{:S(2)}, u32[]{:S(2)}) collective-permute-start(f32[384,128]{1,0:T(8,128)S(1)} %constant_dynamic-slice_fusion), channel_id=1, source_target_pairs={{16,0},{17,1},{18,2},{19,3},{20,4},{21,5},{22,6},{23,7}} | collective-permute-start | bytes 589832 | tf_op jit(solution)/shard_map/ppermute | solution.py:66
  507.5 65.8 %collective-permute-start.40 = (f32[384,128]{1,0:T(8,128)S(1)}, f32[384,128]{1,0:T(8,128)S(1)}, u32[]{:S(2)}, u32[]{:S(2)}) collective-permute-start(f32[384,128]{1,0:T(8,128)S(1)} %constant_dynamic-slice_fusion), channel_id=1, source_target_pairs={{16,24},{17,25},{18,26},{19,27},{20,28},{21,29},{22,30},{23,31}} | collective-permute-start | bytes 589832 | tf_op jit(solution)/shard_map/ppermute | solution.py:66
  580.7 7.9 %collective-permute-start.48 = (f32[384,128]{1,0:T(8,128)S(1)}, f32[384,128]{1,0:T(8,128)S(1)}, u32[]{:S(2)}, u32[]{:S(2)}) collective-permute-start(f32[384,128]{1,0:T(8,128)S(1)} %add_select_fusion.1), channel_id=1, source_target_pairs={{0,6},{1,7},{2,4},{3,5},{4,2},{5,3},{6,0},{7,1},{8,14},{9,15},{10,... | collective-permute-start | bytes 589832 | tf_op jit(solution)/shard_map/ppermute | solution.py:66
  581.3 7.3 %collective-permute-start.47 = (f32[384,128]{1,0:T(8,128)S(1)}, f32[384,128]{1,0:T(8,128)S(1)}, u32[]{:S(2)}, u32[]{:S(2)}) collective-permute-start(f32[384,128]{1,0:T(8,128)S(1)} %add_select_fusion.1), channel_id=1, source_target_pairs={{0,4},{1,5},{2,6},{3,7},{4,0},{5,1},{6,2},{7,3},{8,12},{9,13},{10,... | collective-permute-start | bytes 589832 | tf_op jit(solution)/shard_map/ppermute | solution.py:66
  589.4 9.0 %collective-permute-start.49 = (f32[4,384,128]{2,1,0:T(8,128)S(1)}, f32[4,384,128]{2,1,0:T(8,128)S(1)}, u32[]{:S(2)}, u32[]{:S(2)}) collective-permute-start(f32[4,384,128]{2,1,0:T(8,128)S(1)} %pad_maximum_fusion.2.own_ref), channel_id=1, source_target_pairs={{0,1},{1,0},{2,3},{3,2},{4,5},{5,4},{6,7},{7,6},{8,9},{9,8},{10,11... | collective-permute-start | bytes 2359304 | tf_op jit(solution)/shard_map/ppermute | solution.py:66
  (51 other events, 238.0 us)
Sparse Core Ops, SparseCore 0:
  143.3 142.3 all-gather.4
  287.3 36.8 all-gather.2

commit v3 on v2

--- a/solution.py
+++ b/solution.py
@@ -137,27 +137,21 @@
     )(spot, *pieces)
 
 
-def corner_lines(panel):
+def spread_corner(panel, z, x, y):
+    part = panel.shape[0] // 4
+    pieces = [panel[d * part : (d + 1) * part] for d in range(4)]
     source = lambda zz, xx, yy, cc: zz == 0 and xx == 0 and yy < 2
-    return [swap(panel, dy=d, only=source) for d in (1, 2, 3)]
-
-
-def corner_both(panel, got, y):
-    upper = jnp.where(y == 0, panel, jnp.where(y == 1, got[0], jnp.where(y == 2, got[1], got[2])))
-    lower = jnp.where(y == 1, panel, jnp.where(y == 0, got[0], jnp.where(y == 3, got[1], got[2])))
-    return jnp.stack([upper, lower])
-
-
-def spread_corner(own, other, z, x):
-    whole = jnp.concatenate([own, other], axis=0)
-    part = whole.shape[1] // 4
-    pieces = [whole[:, d * part : (d + 1) * part] for d in range(4)]
-    first = lambda zz, xx, yy, cc: zz == 0 and xx == 0
-    got = [swap(pieces[d], dz=d, only=first) for d in (1, 2, 3)]
+    got = [swap(pieces[d], dz=d, only=source) for d in (1, 2, 3)]
     value = jnp.where(z == 0, pieces[0], got[0] + got[1] + got[2])
-    second = lambda zz, xx, yy, cc: xx == 0
-    got = [swap(value, dx=d, only=second) for d in (1, 2, 3)]
+    source = lambda zz, xx, yy, cc: xx == 0 and yy < 2
+    got = [swap(value, dx=d, only=source) for d in (1, 2, 3)]
     value = jnp.where(x == 0, value, got[0] + got[1] + got[2])
+    source = lambda zz, xx, yy, cc: yy < 2
+    got = [swap(value, dy=d, only=source) for d in (1, 2, 3)]
+    upper = jnp.where(y == 0, value, jnp.where(y == 1, got[0], jnp.where(y == 2, got[1], got[2])))
+    lower = jnp.where(y == 1, value, jnp.where(y == 0, got[0], jnp.where(y == 3, got[1], got[2])))
+    both = jnp.stack([upper, lower])
+    value = jnp.concatenate([both, swap(both, dcore=1)], axis=0)
     return [value] + [swap(value, dz=d) for d in (1, 2, 3)]
 
 
@@ -240,7 +234,9 @@
     return lax.ppermute(panel, ALL, pairs)
 
 
-def update_kernel(block_ref, row_ref, col_ref, out_ref, high_ref, low_ref, hold):
+def update_kernel(block_ref, row_ref, col_ref, *refs):
+    out_ref, high_ref, low_ref, hold = refs[-4:]
+
     @pl.when(pl.program_id(0) == 0)
     def _():
         high_ref[...], low_ref[...] = halves(col_ref[...])
@@ -254,28 +250,32 @@
         out_ref[pl.ds(g, rows, stride=groups), :] = hold[:, g * lanes : (g + 1) * lanes]
 
 
-def update(blocks, row_factor, col_factor):
+def update(blocks, row_factor, col_factor, out):
     count, rows, cols = blocks.shape
+    half = count // 2
+    first = 0 if out is None else half
     width = row_factor.shape[1]
     lanes = cols // 8
     return pl.pallas_call(
         update_kernel,
         out_shape=shape(count * rows * 8, lanes),
-        grid=(count,),
+        grid=(half,),
         in_specs=[
-            pl.BlockSpec((1, rows, cols), lambda i: (i, 0, 0)),
-            pl.BlockSpec((rows, width), lambda i: (i, 0)),
+            pl.BlockSpec((1, rows, cols), lambda i: (i + first, 0, 0)),
+            pl.BlockSpec((rows, width), lambda i: (i + first, 0)),
             pl.BlockSpec(col_factor.shape, lambda i: (0, 0)),
-        ],
-        out_specs=pl.BlockSpec((rows * 8, lanes), lambda i: (i, 0)),
+        ]
+        + ([] if out is None else [ANY]),
+        out_specs=pl.BlockSpec((rows * 8, lanes), lambda i: (i + first, 0)),
         scratch_shapes=[
             pltpu.VMEM(col_factor.shape, jnp.bfloat16),
             pltpu.VMEM(col_factor.shape, jnp.bfloat16),
             pltpu.VMEM((rows, cols), F32),
         ],
+        input_output_aliases={} if out is None else {3: 0},
         interpret=INTERPRET,
         name="update",
-    )(blocks, row_factor, col_factor)
+    )(blocks, row_factor, col_factor, *([] if out is None else [out]))
 
 
 def on_line(z, x, y, core):
@@ -446,28 +446,25 @@
 
     from_first = lambda zz, xx, yy, cc: zz == 0 and xx == 0
     from_second = lambda zz, xx, yy, cc: zz == 0 and xx == 1
-    got = corner_lines(panel)
     lead = [swap(panel, dx=2, only=from_first), swap(panel, dx=3, only=from_second), panel]
-    second = swap(factor[:, panel_width : 3 * panel_width], dx=3, only=from_second)
-    corner_own = corner_both(panel, got, y)
-    corner_other = swap(corner_own, dcore=1, only=from_first)
-    rows_share = share_rows(panel)
-    cols_share = share_cols(panel)
-    pieces = spread_corner(corner_own, corner_other, z, x)
-    rows_in = lax.all_gather(rows_share, ("xl", "y", "core"), tiled=True)
-    cols_in = lax.all_gather(cols_share, ("z", "xh"), tiled=True)
-    blocks = send_tiles(spot, factor, damping[None, :])
-
+    pieces = spread_corner(panel, z, x, y)
     ends = jnp.where(y < 2, lead[2], lead[0])
     ends = jnp.concatenate([lead[1], ends], axis=0)
     lines = jnp.stack([ends] + [swap(ends, dy=m, only=on_line) for m in (1, 2, 3)])
+    cols_share = share_cols(panel)
+    rows_share = share_rows(panel)
+    second = swap(factor[:, panel_width : 3 * panel_width], dx=3, only=from_second)
+    cols_in = lax.all_gather(cols_share, ("z", "xh"), tiled=True)
+    rows_in = lax.all_gather(rows_share, ("xl", "y", "core"), tiled=True)
+    blocks = send_tiles(spot, factor, damping[None, :])
+
     lower = [
         lead[0],
         jnp.concatenate([lead[1], second], axis=1),
         factor[:, : 5 * panel_width],
     ]
+    lines_other = swap(lines, dcore=1, only=on_line)
     lower_other = [swap(value, dcore=1, only=on_line) for value in lower]
-    lines_other = swap(lines, dcore=1, only=on_line)
 
     x_inverse, inverse = inverse_factor(spot, pieces)
     panels = place_panels(spot, lines, lines_other)
@@ -476,7 +473,8 @@
     solved = forward_solve(spot, x_inverse, inverse, gradients, inverses, panels, lower, lower_other)
     solution_rows = spread_solution(spot, solved, z, x, y, core)
 
-    out = update(blocks, row_factor, col_factor)
+    out = update(blocks, row_factor, col_factor, None)
+    out = update(blocks, row_factor, col_factor, out)
     tile = order // 64
     updated = out.reshape(8, 1, tile, 4, 1, tile)
     panel_tiles = tiles.reshape(8, 1, part // 8, panel_width)

time: 635 us -> 644 us (1.014)
    pallas_call x1 -> x2, Pallas kernels: 14.3 us -> 17.1 us  [update(): pl.pallas_call(update_kernel, out_shape=shape(count * rows * 8, lanes), g...]
  transfers between devices with their start and end apart: 54 -> 54, of which waited for: 12 -> 13; matrix products, arithmetic and copies ran while one was open for 2% -> 2% of each run, Pallas kernels for 18% -> 18%
where the time goes in v3:
time: 644 us; the launch traced here: 638 us
  waiting for transfers between devices  310 us (48%)
  starting transfers between devices  151 us (23%)
  Pallas kernels  141 us (22%)
  local copies, waits for them, and re-layouts  16.8 us (3%)
  between operations  15.2 us (2%)
    ppermute x48, waiting for transfers between devices, swap(): return lax.ppermute(value, ALL, pairs)  196 us
    ppermute x1, waiting for transfers between devices, share_cols(): return lax.ppermute(panel, ALL, pairs)  115 us
    ppermute x48, starting transfers between devices, swap(): return lax.ppermute(value, ALL, pairs)  108 us
    pallas_call x1, Pallas kernels, inverse_factor(): pl.pallas_call(corner_kernel, out_shape=[shape(n, n), shape(n, n)], in_sp...  58.3 us
    pallas_call x6, Pallas kernels, forward_solve(): result = run(*operands)  39.8 us
    all_to_all x1, starting transfers between devices, send_tiles(): lax.all_to_all(packed.reshape(8, 2 * part, cols), ('z', 'xh'), 0, 0, tile...  31.2 us
    pallas_call x2, Pallas kernels, update(): pl.pallas_call(update_kernel, out_shape=shape(count * rows * 8, lanes), g...  17.1 us
  transfers between devices with their start and end apart: 54, of which 13 were waited for; matrix products, arithmetic and copies ran while one was open for 2% of the time, Pallas kernels for 18%

profile of v3, /device:TPU:1, one launch (start us, length us, event | category | flops | bytes accessed | tf_op | source)
XLA Modules:
  0.0 637.9 jit_solution(12693455181305873372)
XLA Ops:
  7.9 7.4 %pack_tiles.1 = f32[16,128,1024]{2,1,0:T(8,128)} custom-call(s32[5]{0:T(128)} %stack.62.spot_ref, f32[128,16384]{1,0:T(8,128)} %factor_ref.1, f32[1,128]{1,0:T(1,128)} %bitcast.32), custom_call_target="tpu_custom_call" | custom-call | tf_op jit(solution)/shard_map/pack_tiles/pallas_call | solution.py:182
  15.3 7.0 %all-to-all-start = ((f32[16,128,1024]{2,1,0:T(8,128)}), f32[16,128,1024]{2,1,0:T(8,128)}, u32[]{:S(2)}, u32[]{:S(2)}) async-start(f32[16,128,1024]{2,1,0:T(8,128)} %pack_tiles.1), calls=%async_computation | async-start | bytes 16777216 | tf_op jit(solution)/shard_map/all_to_all | solution.py:192
  23.4 4.4 collective-permute-start.14
  27.8 114.6 %collective-permute-done.14 = f32[128,512]{1,0:T(8,128)S(1)} collective-permute-done((f32[128,512]{1,0:T(8,128)S(1)}, f32[128,512]{1,0:T(8,128)S(1)}, u32[]{:S(2)}, u32[]{:S(2)}) %collective-permute-start.14) | collective-permute-done | bytes 262176 | tf_op jit(solution)/shard_map/ppermute | solution.py:234
  144.6 31.2 %all-to-all-start.1 = ((f32[8,256,1024]{2,1,0:T(8,128)}), f32[8,256,1024]{2,1,0:T(8,128)}, u32[]{:S(2)}, u32[]{:S(2)}) async-start(f32[8,256,1024]{2,1,0:T(8,128)} %bitcast.6), calls=%async_computation.1 | async-start | bytes 16777216 | tf_op jit(solution)/shard_map/all_to_all | solution.py:193
  175.8 5.6 collective-permute-start.15
  182.1 100.4 %collective-permute-done.15.refs_2_ = f32[128,512]{1,0:T(8,128)} collective-permute-done((f32[128,512]{1,0:T(8,128)S(1)}, f32[128,512]{1,0:T(8,128)}, u32[]{:S(2)}, u32[]{:S(2)}) %collective-permute-start.15) | collective-permute-done | bytes 262176 | tf_op jit(solution)/shard_map/ppermute | solution.py:66
  286.0 2.1 collective-permute-start.24
  294.7 46.0 %collective-permute-start.4 = (f32[32,512]{1,0:T(8,128)S(1)}, f32[32,512]{1,0:T(8,128)S(1)}, u32[]{:S(2)}, u32[]{:S(2)}) collective-permute-start(f32[32,512]{1,0:T(8,128)S(1)} %slice_select_fusion), channel_id=1, source_target_pairs={{0,16},{1,17},{2,18},{3,19},{32,48},{33,49},{34,50},{35,51},{64,80... | collective-permute-start | bytes 196616 | tf_op jit(solution)/shard_map/ppermute | solution.py:66
  345.0 1.9 collective-permute-start.7
  346.9 4.1 collective-permute-start.6
  351.0 1.9 slice.26
  361.3 1.9 constant_dynamic-update-slice_fusion.refs_9_.refs_10_
  365.0 14.6 %collective-permute-done.12.refs_3_ = f32[4,32,512]{2,1,0:T(8,128)S(1)} collective-permute-done((f32[4,32,512]{2,1,0:T(8,128)S(1)}, f32[4,32,512]{2,1,0:T(8,128)S(1)}, u32[]{:S(2)}, u32[]{:S(2)}) %collective-permute-start.12) | collective-permute-done | bytes 262176 | tf_op jit(solution)/shard_map/ppermute | solution.py:66
  381.9 4.7 collective-permute-done.10.refs_1_
  386.7 58.3 %inverse_factor.1 = (f32[512,512]{1,0:T(8,128)}, f32[512,512]{1,0:T(8,128)}) custom-call(s32[5]{0:T(128)} %stack.62.spot_ref, f32[4,32,512]{2,1,0:T(8,128)} %copy-done.7, f32[4,32,512]{2,1,0:T(8,128)} %collective-permute-done.10.refs_1_, f32[4,32,512]{2,1,0:T(8,128)} %copy-done.13, f32[4,32,512]{2,1,0:T(8,128)} %copy-done.12), custom_call_target="tpu_custom_call" | custom-call | tf_op jit(solution)/shard_map/inverse_factor/pallas_call | solution.py:129
  445.0 4.6 solve.6
  452.8 6.1 place_panels.1.refs_7_
  459.6 7.4 %solve.7 = (f32[512,128]{1,0:T(8,128)}, f32[512,128]{1,0:T(8,128)}, f32[256,128]{1,0:T(8,128)}) custom-call(s32[5]{0:T(128)} %stack.62.spot_ref, f32[3072,128]{1,0:T(8,128)} %refs_0_.11, f32[256,128]{1,0:T(8,128)} %get-tuple-element.27.refs_1_, f32[256,128]{1,0:T(8,128)} %copy-done.23, f32[256,128]{1,0:T(8,128)} %collective-permute-done.18.refs_3_, ...), custom_call_target="tpu_custom_call" | custom-call | tf_op jit(solution)/shard_map/solve/pallas_call | solution.py:397
  469.7 7.7 %solve.8 = (f32[512,128]{1,0:T(8,128)}, f32[512,128]{1,0:T(8,128)}, f32[256,128]{1,0:T(8,128)}) custom-call(s32[5]{0:T(128)} %stack.62.spot_ref, f32[3072,128]{1,0:T(8,128)} %refs_0_.11, f32[256,128]{1,0:T(8,128)} %get-tuple-element.31.refs_1_, f32[256,128]{1,0:T(8,128)} %copy-done.26, f32[256,128]{1,0:T(8,128)} %copy-done.24, f32[256,128]{1,0:T(8,128)} %copy-done.21, ...), custom_call_target="tpu_custom_call" | custom-call | tf_op jit(solution)/shard_map/solve/pallas_call | solution.py:397
  480.2 8.3 %solve.9 = (f32[512,128]{1,0:T(8,128)}, f32[512,128]{1,0:T(8,128)}, f32[256,128]{1,0:T(8,128)}) custom-call(s32[5]{0:T(128)} %stack.62.spot_ref, f32[3072,128]{1,0:T(8,128)} %refs_0_.11, f32[256,128]{1,0:T(8,128)} %get-tuple-element.34.refs_1_, f32[256,128]{1,0:T(8,128)} %copy-done.16, f32[256,128]{1,0:T(8,128)} %copy-done.15, f32[256,128]{1,0:T(8,128)} %copy-done.14, ...), custom_call_target="tpu_custom_call" | custom-call | tf_op jit(solution)/shard_map/solve/pallas_call | solution.py:397
  491.6 8.6 %solve.10 = (f32[512,128]{1,0:T(8,128)}, f32[512,128]{1,0:T(8,128)}, f32[256,128]{1,0:T(8,128)}) custom-call(s32[5]{0:T(128)} %stack.62.spot_ref, f32[3072,128]{1,0:T(8,128)} %refs_0_.11, f32[256,128]{1,0:T(8,128)} %get-tuple-element.37.refs_1_, f32[256,128]{1,0:T(8,128)} %copy-done.20, f32[256,128]{1,0:T(8,128)} %copy-done.19, f32[256,128]{1,0:T(8,128)} %copy-done.17, ...), custom_call_target="tpu_custom_call" | custom-call | tf_op jit(solution)/shard_map/solve/pallas_call | solution.py:397
  504.6 3.2 solve.11
  511.5 62.5 %collective-permute-done.41 = f32[384,128]{1,0:T(8,128)S(1)} collective-permute-done((f32[384,128]{1,0:T(8,128)S(1)}, f32[384,128]{1,0:T(8,128)S(1)}, u32[]{:S(2)}, u32[]{:S(2)}) %collective-permute-start.41) | collective-permute-done | bytes 196640 | tf_op jit(solution)/shard_map/ppermute | solution.py:66
  579.2 2.1 collective-permute-done.43
  584.7 4.6 collective-permute-done.48
  589.9 8.6 %collective-permute-start.49 = (f32[4,384,128]{2,1,0:T(8,128)S(1)}, f32[4,384,128]{2,1,0:T(8,128)S(1)}, u32[]{:S(2)}, u32[]{:S(2)}) collective-permute-start(f32[4,384,128]{2,1,0:T(8,128)S(1)} %pad_maximum_fusion.1.own_ref), channel_id=1, source_target_pairs={{0,1},{1,0},{2,3},{3,2},{4,5},{5,4},{6,7},{7,6},{8,9},{9,8},{10,11... | collective-permute-start | bytes 2359304 | tf_op jit(solution)/shard_map/ppermute | solution.py:66
  598.6 1.9 collective-permute-done.49.other_ref
  601.4 2.6 place_rows.1
  604.0 9.7 %panel_solve.1 = (f32[2048,512]{1,0:T(8,128)}, f32[1024,512]{1,0:T(8,128)}, f32[128,512]{1,0:T(8,128)}) custom-call(s32[5]{0:T(128)} %stack.62.spot_ref, f32[512,512]{1,0:T(8,128)} %get-tuple-element.22.x_ref.refs_1_, f32[2048,512]{1,0:T(8,128)} %all-gather.3.cloned.1.call-done.rows_ref, f32[1024,512]{1,0:T(8,128)} %all-gather.5.cloned.1.call-done.cols_ref), custom_call_target="tpu_custom_call" | custom-call | tf_op jit(solution)/shard_map/panel_solve/pallas_call | solution.py:211
  613.7 8.4 %update.2.refs_0_ = f32[16384,128]{1,0:T(8,128)} custom-call(f32[8,256,1024]{2,1,0:T(8,128)} %all-to-all-done.1.block_ref, f32[2048,512]{1,0:T(8,128)} %get-tuple-element.23.row_ref, f32[1024,512]{1,0:T(8,128)} %get-tuple-element.24.col_ref), custom_call_target="tpu_custom_call" | custom-call | tf_op jit(solution)/shard_map/update/pallas_call | solution.py:259
  622.1 8.7 %update.3 = f32[16384,128]{1,0:T(8,128)} custom-call(f32[8,256,1024]{2,1,0:T(8,128)} %all-to-all-done.1.block_ref, f32[2048,512]{1,0:T(8,128)} %get-tuple-element.23.row_ref, f32[1024,512]{1,0:T(8,128)} %get-tuple-element.24.col_ref, f32[16384,128]{1,0:T(8,128)} %update.2.refs_0_), custom_call_target="tpu_custom_call", output_to_operand_aliasing={{}: (3, {})} | custom-call | tf_op jit(solution)/shard_map/update/pallas_call | solution.py:259
  (175 shorter events, 61.6 us)
Async XLA Ops:
  15.3 129.3 %all-to-all-start = ((f32[16,128,1024]{2,1,0:T(8,128)}), f32[16,128,1024]{2,1,0:T(8,128)}, u32[]{:S(2)}, u32[]{:S(2)}) async-start(f32[16,128,1024]{2,1,0:T(8,128)} %pack_tiles.1), calls=%async_computation | async-start | bytes 16777216 | tf_op jit(solution)/shard_map/all_to_all | solution.py:192
  22.3 581.7 %all-gather.5.cloned.1.call-start = ((), (), s32[]{:S(2)}) async-start(), calls=%async_computation.3 | async-start | bytes 2359296 | tf_op jit(solution)/shard_map/all_gather | solution.py:457
  23.4 119.0 %collective-permute-start.14 = (f32[128,512]{1,0:T(8,128)S(1)}, f32[128,512]{1,0:T(8,128)S(1)}, u32[]{:S(2)}, u32[]{:S(2)}) collective-permute-start(f32[128,512]{1,0:T(8,128)S(1)} %select_add_fusion), channel_id=1, source_target_pairs={{0,0},{1,16},{2,1},{3,17},{4,2},{5,18},{6,3},{7,19},{8,4},{9,20},{... | collective-permute-start | bytes 786440 | tf_op jit(solution)/shard_map/ppermute | solution.py:234
  143.1 460.9 %all-gather.3.cloned.1.call-start = ((), (), s32[]{:S(2)}) async-start(), calls=%async_computation.2 | async-start | bytes 4456448 | tf_op jit(solution)/shard_map/all_gather | solution.py:458
  144.6 469.1 %all-to-all-start.1 = ((f32[8,256,1024]{2,1,0:T(8,128)}), f32[8,256,1024]{2,1,0:T(8,128)}, u32[]{:S(2)}, u32[]{:S(2)}) async-start(f32[8,256,1024]{2,1,0:T(8,128)} %bitcast.6), calls=%async_computation.1 | async-start | bytes 16777216 | tf_op jit(solution)/shard_map/all_to_all | solution.py:193
  175.8 106.6 %collective-permute-start.15 = (f32[128,512]{1,0:T(8,128)S(1)}, f32[128,512]{1,0:T(8,128)}, u32[]{:S(2)}, u32[]{:S(2)}) collective-permute-start(f32[128,512]{1,0:T(8,128)S(1)} %select_add_fusion), channel_id=1, source_target_pairs={{0,16},{1,17},{2,18},{3,19},{4,20},{5,21},{6,22},{7,23}} | collective-permute-start | bytes 786440 | tf_op jit(solution)/shard_map/ppermute | solution.py:66
  181.4 102.1 %collective-permute-start.20 = (f32[128,512]{1,0:T(8,128)S(1)}, f32[128,512]{1,0:T(8,128)S(1)}, u32[]{:S(2)}, u32[]{:S(2)}) collective-permute-start(f32[128,512]{1,0:T(8,128)S(1)} %select_add_fusion), channel_id=1, source_target_pairs={{8,16},{9,17},{10,18},{11,19},{12,20},{13,21},{14,22},{15,23}} | collective-permute-start | bytes 786440 | tf_op jit(solution)/shard_map/ppermute | solution.py:66
  286.0 165.5 %collective-permute-start.24 = (f32[4,256,512]{2,1,0:T(8,128)S(1)}, f32[4,256,512]{2,1,0:T(8,128)}, u32[]{:S(2)}, u32[]{:S(2)}) collective-permute-start(f32[4,256,512]{2,1,0:T(8,128)S(1)} %pad_maximum_fusion.own_ref), channel_id=1, source_target_pairs={{16,17},{17,16},{18,19},{19,18},{20,21},{21,20},{22,23},{23,22}} | collective-permute-start | bytes 6291464 | tf_op jit(solution)/shard_map/ppermute | solution.py:66
  293.4 48.7 %collective-permute-start.5 = (f32[32,512]{1,0:T(8,128)S(1)}, f32[32,512]{1,0:T(8,128)S(1)}, u32[]{:S(2)}, u32[]{:S(2)}) collective-permute-start(f32[32,512]{1,0:T(8,128)S(1)} %slice_select_fusion), channel_id=1, source_target_pairs={{0,24},{1,25},{2,26},{3,27},{32,56},{33,57},{34,58},{35,59},{64,88... | collective-permute-start | bytes 196616 | tf_op jit(solution)/shard_map/ppermute | solution.py:66
  294.7 47.5 %collective-permute-start.4 = (f32[32,512]{1,0:T(8,128)S(1)}, f32[32,512]{1,0:T(8,128)S(1)}, u32[]{:S(2)}, u32[]{:S(2)}) collective-permute-start(f32[32,512]{1,0:T(8,128)S(1)} %slice_select_fusion), channel_id=1, source_target_pairs={{0,16},{1,17},{2,18},{3,19},{32,48},{33,49},{34,50},{35,51},{64,80... | collective-permute-start | bytes 196616 | tf_op jit(solution)/shard_map/ppermute | solution.py:66
  343.7 12.1 %collective-permute-start.8 = (f32[32,512]{1,0:T(8,128)S(1)}, f32[32,512]{1,0:T(8,128)S(1)}, u32[]{:S(2)}, u32[]{:S(2)}) collective-permute-start(f32[32,512]{1,0:T(8,128)S(1)} %add_select_fusion.2), channel_id=1, source_target_pairs={{0,6},{1,7},{2,4},{3,5},{8,14},{9,15},{10,12},{11,13},{16,22},{17,... | collective-permute-start | bytes 196616 | tf_op jit(solution)/shard_map/ppermute | solution.py:66
  345.0 12.6 %collective-permute-start.7 = (f32[32,512]{1,0:T(8,128)S(1)}, f32[32,512]{1,0:T(8,128)}, u32[]{:S(2)}, u32[]{:S(2)}) collective-permute-start(f32[32,512]{1,0:T(8,128)S(1)} %add_select_fusion.2), channel_id=1, source_target_pairs={{0,4},{1,5},{2,6},{3,7},{8,12},{9,13},{10,14},{11,15},{16,20},{17,... | collective-permute-start | bytes 196616 | tf_op jit(solution)/shard_map/ppermute | solution.py:66
  346.9 10.7 %collective-permute-start.6 = (f32[32,512]{1,0:T(8,128)S(1)}, f32[32,512]{1,0:T(8,128)}, u32[]{:S(2)}, u32[]{:S(2)}) collective-permute-start(f32[32,512]{1,0:T(8,128)S(1)} %add_select_fusion.2), channel_id=1, source_target_pairs={{0,2},{1,3},{2,0},{3,1},{8,10},{9,11},{10,8},{11,9},{16,18},{17,19... | collective-permute-start | bytes 196616 | tf_op jit(solution)/shard_map/ppermute | solution.py:66
  352.9 8.5 %collective-permute-start.25 = (f32[128,1024]{1,0:T(8,128)}, f32[128,1024]{1,0:T(8,128)}, u32[]{:S(2)}, u32[]{:S(2)}) collective-permute-start(f32[128,1024]{1,0:T(8,128)} %slice.26), channel_id=1, source_target_pairs={{8,16},{9,17},{10,18},{11,19},{12,20},{13,21},{14,22},{15,23}} | collective-permute-start | bytes 1572872 | tf_op jit(solution)/shard_map/ppermute | solution.py:66
  355.8 123.6 %collective-permute-start.33 = (f32[128,2560]{1,0:T(8,128)S(1)}, f32[128,2560]{1,0:T(8,128)}, u32[]{:S(2)}, u32[]{:S(2)}) collective-permute-start(f32[128,2560]{1,0:T(8,128)S(1)} %slice.27.refs_11_.refs_12_), channel_id=1, source_target_pairs={{16,17},{17,16},{18,19},{19,18},{20,21},{21,20},{22,23},{23,22}} | collective-permute-start | bytes 3932168 | tf_op jit(solution)/shard_map/ppermute | solution.py:66
  358.5 6.3 collective-permute-start.9
  363.2 95.6 %collective-permute-start.26 = (f32[128,1536]{1,0:T(8,128)}, f32[128,1536]{1,0:T(8,128)}, u32[]{:S(2)}, u32[]{:S(2)}) collective-permute-start(f32[128,1536]{1,0:T(8,128)} %constant_dynamic-update-slice_fusion.refs_9_.refs_10_), channel_id=1, source_target_pairs={{16,17},{17,16},{18,19},{19,18},{20,21},{21,20},{22,23},{23,22}} | collective-permute-start | bytes 2359304 | tf_op jit(solution)/shard_map/ppermute | solution.py:66
  364.8 14.8 %collective-permute-start.12 = (f32[4,32,512]{2,1,0:T(8,128)S(1)}, f32[4,32,512]{2,1,0:T(8,128)S(1)}, u32[]{:S(2)}, u32[]{:S(2)}) collective-permute-start(f32[4,32,512]{2,1,0:T(8,128)S(1)} %pad_maximum_fusion.3.refs_0_), channel_id=1, source_target_pairs={{0,96},{1,97},{2,98},{3,99},{4,100},{5,101},{6,102},{7,103},{8,104... | collective-permute-start | bytes 786440 | tf_op jit(solution)/shard_map/ppermute | solution.py:66
  364.9 14.7 %collective-permute-start.11 = (f32[4,32,512]{2,1,0:T(8,128)S(1)}, f32[4,32,512]{2,1,0:T(8,128)S(1)}, u32[]{:S(2)}, u32[]{:S(2)}) collective-permute-start(f32[4,32,512]{2,1,0:T(8,128)S(1)} %pad_maximum_fusion.3.refs_0_), channel_id=1, source_target_pairs={{0,64},{1,65},{2,66},{3,67},{4,68},{5,69},{6,70},{7,71},{8,72},{9,... | collective-permute-start | bytes 786440 | tf_op jit(solution)/shard_map/ppermute | solution.py:66
  379.6 7.1 %collective-permute-start.10 = (f32[4,32,512]{2,1,0:T(8,128)S(1)}, f32[4,32,512]{2,1,0:T(8,128)}, u32[]{:S(2)}, u32[]{:S(2)}) collective-permute-start(f32[4,32,512]{2,1,0:T(8,128)S(1)} %pad_maximum_fusion.3.refs_0_), channel_id=1, source_target_pairs={{0,32},{1,33},{2,34},{3,35},{4,36},{5,37},{6,38},{7,39},{8,40},{9,... | collective-permute-start | bytes 786440 | tf_op jit(solution)/shard_map/ppermute | solution.py:66
  380.3 64.7 %collective-permute-start.16 = (f32[128,512]{1,0:T(8,128)}, f32[128,512]{1,0:T(8,128)}, u32[]{:S(2)}, u32[]{:S(2)}) collective-permute-start(f32[128,512]{1,0:T(8,128)} %collective-permute-done.15.refs_2_), channel_id=1, source_target_pairs={{16,17},{17,16},{18,19},{19,18},{20,21},{21,20},{22,23},{23,22}} | collective-permute-start | bytes 786440 | tf_op jit(solution)/shard_map/ppermute | solution.py:66
  449.6 9.3 %collective-permute-start.19 = (f32[256,128]{1,0:T(8,128)}, f32[256,128]{1,0:T(8,128)S(1)}, u32[]{:S(2)}, u32[]{:S(2)}) collective-permute-start(f32[256,128]{1,0:T(8,128)} %get-tuple-element.27.refs_1_), channel_id=1, source_target_pairs={{16,22},{17,23},{18,20},{19,21},{20,18},{21,19},{22,16},{23,17}} | collective-permute-start | bytes 393224 | tf_op jit(solution)/shard_map/ppermute | solution.py:66
  450.2 8.6 %collective-permute-start.18 = (f32[256,128]{1,0:T(8,128)}, f32[256,128]{1,0:T(8,128)}, u32[]{:S(2)}, u32[]{:S(2)}) collective-permute-start(f32[256,128]{1,0:T(8,128)} %get-tuple-element.27.refs_1_), channel_id=1, source_target_pairs={{16,20},{17,21},{18,22},{19,23},{20,16},{21,17},{22,18},{23,19}} | collective-permute-start | bytes 393224 | tf_op jit(solution)/shard_map/ppermute | solution.py:66
  451.6 7.3 %collective-permute-start.17 = (f32[256,128]{1,0:T(8,128)}, f32[256,128]{1,0:T(8,128)S(1)}, u32[]{:S(2)}, u32[]{:S(2)}) collective-permute-start(f32[256,128]{1,0:T(8,128)} %get-tuple-element.27.refs_1_), channel_id=1, source_target_pairs={{16,18},{17,19},{18,16},{19,17},{20,22},{21,23},{22,20},{23,21}} | collective-permute-start | bytes 393224 | tf_op jit(solution)/shard_map/ppermute | solution.py:66
  509.5 64.5 %collective-permute-start.41 = (f32[384,128]{1,0:T(8,128)S(1)}, f32[384,128]{1,0:T(8,128)S(1)}, u32[]{:S(2)}, u32[]{:S(2)}) collective-permute-start(f32[384,128]{1,0:T(8,128)S(1)} %constant_dynamic-slice_fusion), channel_id=1, source_target_pairs={{16,0},{17,1},{18,2},{19,3},{20,4},{21,5},{22,6},{23,7}} | collective-permute-start | bytes 589832 | tf_op jit(solution)/shard_map/ppermute | solution.py:66
  510.8 63.2 %collective-permute-start.40 = (f32[384,128]{1,0:T(8,128)S(1)}, f32[384,128]{1,0:T(8,128)S(1)}, u32[]{:S(2)}, u32[]{:S(2)}) collective-permute-start(f32[384,128]{1,0:T(8,128)S(1)} %constant_dynamic-slice_fusion), channel_id=1, source_target_pairs={{16,24},{17,25},{18,26},{19,27},{20,28},{21,29},{22,30},{23,31}} | collective-permute-start | bytes 589832 | tf_op jit(solution)/shard_map/ppermute | solution.py:66
  574.0 3.9 collective-permute-start.45
  576.7 4.7 collective-permute-start.43
  581.4 7.9 %collective-permute-start.48 = (f32[384,128]{1,0:T(8,128)S(1)}, f32[384,128]{1,0:T(8,128)S(1)}, u32[]{:S(2)}, u32[]{:S(2)}) collective-permute-start(f32[384,128]{1,0:T(8,128)S(1)} %add_select_fusion), channel_id=1, source_target_pairs={{0,6},{1,7},{2,4},{3,5},{4,2},{5,3},{6,0},{7,1},{8,14},{9,15},{10,... | collective-permute-start | bytes 589832 | tf_op jit(solution)/shard_map/ppermute | solution.py:66
  582.1 7.2 %collective-permute-start.47 = (f32[384,128]{1,0:T(8,128)S(1)}, f32[384,128]{1,0:T(8,128)S(1)}, u32[]{:S(2)}, u32[]{:S(2)}) collective-permute-start(f32[384,128]{1,0:T(8,128)S(1)} %add_select_fusion), channel_id=1, source_target_pairs={{0,4},{1,5},{2,6},{3,7},{4,0},{5,1},{6,2},{7,3},{8,12},{9,13},{10,... | collective-permute-start | bytes 589832 | tf_op jit(solution)/shard_map/ppermute | solution.py:66
  583.1 6.8 %collective-permute-start.46 = (f32[384,128]{1,0:T(8,128)S(1)}, f32[384,128]{1,0:T(8,128)S(1)}, u32[]{:S(2)}, u32[]{:S(2)}) collective-permute-start(f32[384,128]{1,0:T(8,128)S(1)} %add_select_fusion), channel_id=1, source_target_pairs={{0,2},{1,3},{2,0},{3,1},{4,6},{5,7},{6,4},{7,5},{8,10},{9,11},{10,... | collective-permute-start | bytes 589832 | tf_op jit(solution)/shard_map/ppermute | solution.py:66
  589.9 10.5 %collective-permute-start.49 = (f32[4,384,128]{2,1,0:T(8,128)S(1)}, f32[4,384,128]{2,1,0:T(8,128)S(1)}, u32[]{:S(2)}, u32[]{:S(2)}) collective-permute-start(f32[4,384,128]{2,1,0:T(8,128)S(1)} %pad_maximum_fusion.1.own_ref), channel_id=1, source_target_pairs={{0,1},{1,0},{2,3},{3,2},{4,5},{5,4},{6,7},{7,6},{8,9},{9,8},{10,11... | collective-permute-start | bytes 2359304 | tf_op jit(solution)/shard_map/ppermute | solution.py:66
  (51 other events, 293.4 us)
Sparse Core Ops, SparseCore 0:
  143.3 142.3 all-gather.4
  287.3 36.8 all-gather.2

commit v4 on v3

--- a/solution.py
+++ b/solution.py
@@ -282,7 +282,7 @@
     return z == 0 and x == 2
 
 
-def place_panels_kernel(spot_ref, own_ref, other_ref, out_ref):
+def place_panels_kernel(spot_ref, own_ref, other_ref, tie_own_ref, tie_other_ref, out_ref, tie_ref):
     part = own_ref.shape[1] // 2
     y, core = spot_ref[3], spot_ref[4]
     for ref, side in ((own_ref, core), (other_ref, 1 - core)):
@@ -293,111 +293,134 @@
                 out_ref[:, pl.ds(pl.multiple_of(at, part), part)] = ref[
                     m, slot * part : (slot + 1) * part, :
                 ].T
-
-
-def place_panels(spot, own, other):
+    for ref, side in ((tie_own_ref, core), (tie_other_ref, 1 - core)):
+        for c in range(2):
+            at = pl.multiple_of((c * 2 + side) * part, part)
+            for i in range(2):
+                tie_ref[i, pl.ds(at, part), :] = ref[y ^ c, i * part : (i + 1) * part, :]
+
+
+def place_panels(spot, own, other, tie_own, tie_other):
     _, rows, width = own.shape
     return pl.pallas_call(
         place_panels_kernel,
-        out_shape=shape(width, 12 * rows),
-        in_specs=[SMEM, VMEM, VMEM],
-        out_specs=VMEM,
+        out_shape=[shape(width, 12 * rows), shape(2, width, width)],
+        in_specs=[SMEM] + [VMEM] * 4,
+        out_specs=[VMEM, VMEM],
         interpret=INTERPRET,
         name="place_panels",
-    )(spot, own, other)
+    )(spot, own, other, tie_own, tie_other)
 
 
 def dot_e(left, right, dims):
     return dot3(halves(left), halves(right), dims)
 
 
-def solve_kernel(spot_ref, *refs, block, last, panel):
-    refs = list(refs)
+def write_share(spot_ref, grads_ref, share_ref, sources, known, v, slots):
     y, core = spot_ref[3], spot_ref[4]
-    take = lambda: refs.pop(0)
-    grads_ref = take()
-    known = []
-    if block == 0:
-        x = take()[...]
-        solved = dot_e(x, grads_ref[0:panel, :], NN)
-        v = dot_e(x, solved, TN)
-    else:
-        shares = [take()[...] for _ in range(4)]
-        inverse_ref = take()
-        lead = 2 * (block % 2)
-        near = y == lead
-        twin = y == lead + 1
-        far = y == (lead ^ 2)
-        upper = jnp.where(near, shares[0], jnp.where(twin, shares[1], jnp.where(far, shares[2], shares[3])))
-        lower = jnp.where(twin, shares[0], jnp.where(near, shares[1], jnp.where(far, shares[3], shares[2])))
-        right = jnp.concatenate([upper, lower], axis=0)
-        solved = dot_e(inverse_ref[0], right, NN)
-        if last:
-            refs[0][...] = solved
-            return
-        square_ref, panel_ref, v_ref = take(), take(), take()
-        known = [take()[...] for _ in range(block - 1)] + [solved]
-        v = v_ref[...] - dot_e(square_ref[...], dot_e(panel_ref[...], solved, NN), NN)
-    own_ref, other_ref = take(), take()
-    solved_ref, v_out, share_ref = refs
-    tile = panel // 2
-    part = tile // 2
-    slot = (block + 1) // 2
-    rest = []
-    for ref in (own_ref, other_ref):
-        total = dot_e(ref[:, :panel], v, NN)
-        for j, value in enumerate(known):
-            total = total + dot_e(ref[:, (j + 1) * panel : (j + 2) * panel], value, NN)
-        rest.append(total)
-    start = (slot * 4 + y) * tile
-    for value, side in ((rest[0], core), (rest[1], 1 - core)):
+    panel = v.shape[0]
+    part = panel // 4
+    slot = jnp.where(y < 2, slots[0], slots[1])
+    start = (slot * 4 + y) * 2 * part
+    for refs, side in ((sources[0], core), (sources[1], 1 - core)):
+        total = None
+        for j, value in enumerate([v] + known):
+            low, high = j * panel, (j + 1) * panel
+            rows = refs[0][:, low:high]
+            if len(refs) == 2:
+                rows = jnp.where(y < 2, refs[1][:, low:high], rows)
+            term = dot_e(rows, value, NN)
+            total = term if total is None else total + term
         at = pl.multiple_of(side * part, part)
         row = pl.multiple_of(start + at, part)
-        share_ref[pl.ds(at, part), :] = grads_ref[pl.ds(row, part), :] - value
-    solved_ref[...] = solved
+        share_ref[pl.ds(at, part), :] = grads_ref[pl.ds(row, part), :] - total
+
+
+def pick(shares, y, line):
+    near = jnp.where(y == (line ^ 2), shares[2], shares[3])
+    return jnp.where(y == line, shares[0], jnp.where(y == (line ^ 1), shares[1], near))
+
+
+def right_sides(refs, y):
+    shares = [ref[...] for ref in refs]
+    odd = jnp.concatenate([pick(shares, y, 2), pick(shares, y, 3)], axis=0)
+    return odd, shares
+
+
+def solve_first_kernel(spot_ref, grads_ref, x_ref, square_ref, a0, b0, a1, b1, y_ref, v_ref, share_ref):
+    panel = x_ref.shape[0]
+    lead = grads_ref[0:panel, :]
+    v = dot_e(square_ref[...], lead, NN)
+    write_share(spot_ref, grads_ref, share_ref, ((a0, a1), (b0, b1)), [], v, (1, 0))
+    y_ref[...] = dot_e(x_ref[...], lead, NN)
+    v_ref[...] = v
+
+
+def solve_pair_kernel(spot_ref, grads_ref, *refs, pair):
+    shares, refs = refs[:4], list(refs[4:])
+    inverse_a, inverse_b, square_ref, panel_a, panel_b, tie_ref, v_ref = refs[:7]
+    known = [ref[...] for ref in refs[7 : 7 + 2 * pair]]
+    refs = refs[7 + 2 * pair :]
+    y_a_ref, y_b_ref, v_out, share_ref = refs[-4:]
+    sources = refs[:-4]
+    y = spot_ref[3]
+    square = square_ref[...]
+    right, values = right_sides(shares, y)
+    y_a = dot_e(inverse_a[0], right, NN)
+    move = dot_e(square, dot_e(panel_a[...], y_a, NN), NN)
+    right = jnp.concatenate([pick(values, y, 0), pick(values, y, 1)], axis=0)
+    right = right - dot_e(tie_ref[0], y_a, NN) + dot_e(panel_b[...], move, TN)
+    y_b = dot_e(inverse_b[0], right, NN)
+    v = v_ref[...] - move - dot_e(square, dot_e(panel_b[...], y_b, NN), NN)
+    half = len(sources) // 2
+    slots = (2, 1) if pair == 0 else (2, 2)
+    write_share(spot_ref, grads_ref, share_ref, (sources[:half], sources[half:]), known + [y_a, y_b], v, slots)
+    y_a_ref[...] = y_a
+    y_b_ref[...] = y_b
     v_out[...] = v
 
 
-def forward_solve(spot, x, square, grads, inverses, panels, own, other):
+def solve_last_kernel(spot_ref, *refs):
+    right, _ = right_sides(refs[:4], spot_ref[3])
+    refs[5][...] = dot_e(refs[4][0], right, NN)
+
+
+def forward_solve(spot, x, square, grads, inverses, panels, ties, own, other):
     panel = x.shape[0]
     count = grads.shape[1]
-    blocks = grads.shape[0] // panel
-    solved, v, share = [], None, None
-    for block in range(blocks):
-        last = block == blocks - 1
-        operands, specs = [spot, grads], [SMEM, VMEM]
-        if block == 0:
-            operands += [x]
-            specs += [VMEM]
-        else:
-            got = [share] + [swap(share, dy=m, only=on_line) for m in (1, 2, 3)]
-            operands += [*got, inverses]
-            specs += [VMEM] * 4
-            specs += [pl.BlockSpec((1, panel, panel), lambda i, b=block: (b - 1, 0, 0))]
-            if not last:
-                operands += [square, panels, v, *solved[1:]]
-                specs += [VMEM, pl.BlockSpec((panel, panel), lambda i, b=block: (0, b))]
-                specs += [VMEM] * block
-        if not last:
-            slot = (block + 1) // 2
-            operands += [own[slot], other[slot]]
-            specs += [VMEM, VMEM]
-        outs = [shape(panel, count)]
-        if not last:
-            outs += [shape(panel, count), shape(panel // 2, count)]
-        run = pl.pallas_call(
-            functools.partial(solve_kernel, block=block, last=last, panel=panel),
+    full, tile = shape(panel, count), shape(panel // 2, count)
+
+    def run(kernel, operands, specs, outs):
+        return pl.pallas_call(
+            kernel,
             out_shape=outs,
             grid=(1,),
-            in_specs=specs,
+            in_specs=[SMEM] + specs,
             out_specs=[VMEM] * len(outs),
             interpret=INTERPRET,
             name="solve",
-        )
-        result = run(*operands)
-        solved.append(result[0])
-        if not last:
-            v, share = result[1], result[2]
+        )(spot, *operands)
+
+    def exchange(share):
+        return [share] + [swap(share, dy=m, only=on_line) for m in (1, 2, 3)]
+
+    inverse = lambda b: pl.BlockSpec((1, panel, panel), lambda i: (b - 1, 0, 0))
+    leading = lambda b: pl.BlockSpec((panel, panel), lambda i: (0, b))
+    operands = [grads, x, square, own[0], other[0], own[1], other[1]]
+    first, v, share = run(solve_first_kernel, operands, [VMEM] * 7, [full, full, tile])
+    solved = [first]
+    for pair in range(2):
+        a, b = 2 * pair + 1, 2 * pair + 2
+        operands = [grads, *exchange(share), inverses, inverses, square, panels, panels, ties, v]
+        specs = [VMEM] * 5 + [inverse(a), inverse(b), VMEM, leading(a), leading(b)]
+        specs += [pl.BlockSpec((1, panel, panel), lambda i, p=pair: (p, 0, 0)), VMEM]
+        rest = solved[1:] + ([own[1], own[2], other[1], other[2]] if pair == 0 else [own[2], other[2]])
+        outs = [full, full, full, tile]
+        kernel = functools.partial(solve_pair_kernel, pair=pair)
+        y_a, y_b, v, share = run(kernel, operands + rest, specs + [VMEM] * len(rest), outs)
+        solved += [y_a, y_b]
+    operands = [*exchange(share), inverses]
+    solved += run(solve_last_kernel, operands, [VMEM] * 4 + [inverse(5)], [full])
     return solved
 
 
@@ -446,31 +469,37 @@
 
     from_first = lambda zz, xx, yy, cc: zz == 0 and xx == 0
     from_second = lambda zz, xx, yy, cc: zz == 0 and xx == 1
-    lead = [swap(panel, dx=2, only=from_first), swap(panel, dx=3, only=from_second), panel]
+    moved = swap(factor[:, : 2 * panel_width], dx=3, only=from_second)
+    lead = [swap(panel, dx=2, only=from_first), moved[:, :panel_width], panel]
     pieces = spread_corner(panel, z, x, y)
     ends = jnp.where(y < 2, lead[2], lead[0])
     ends = jnp.concatenate([lead[1], ends], axis=0)
     lines = jnp.stack([ends] + [swap(ends, dy=m, only=on_line) for m in (1, 2, 3)])
+    tie = factor[:, 3 * panel_width : 4 * panel_width]
+    tie = jnp.concatenate([moved[:, panel_width:], tie], axis=0)
+    from_low = lambda zz, xx, yy, cc: on_line(zz, xx, yy, cc) and yy < 2
+    ties = jnp.stack([tie] + [swap(tie, dy=m, only=from_low) for m in (1, 2, 3)])
     cols_share = share_cols(panel)
     rows_share = share_rows(panel)
-    second = swap(factor[:, panel_width : 3 * panel_width], dx=3, only=from_second)
+    second = swap(factor[:, 2 * panel_width : 3 * panel_width], dx=3, only=from_second)
     cols_in = lax.all_gather(cols_share, ("z", "xh"), tiled=True)
     rows_in = lax.all_gather(rows_share, ("xl", "y", "core"), tiled=True)
     blocks = send_tiles(spot, factor, damping[None, :])
 
     lower = [
         lead[0],
-        jnp.concatenate([lead[1], second], axis=1),
+        jnp.concatenate([moved, second], axis=1),
         factor[:, : 5 * panel_width],
     ]
     lines_other = swap(lines, dcore=1, only=on_line)
+    ties_other = swap(ties, dcore=1, only=on_line)
     lower_other = [swap(value, dcore=1, only=on_line) for value in lower]
 
     x_inverse, inverse = inverse_factor(spot, pieces)
-    panels = place_panels(spot, lines, lines_other)
+    panels, ties = place_panels(spot, lines, lines_other, ties, ties_other)
     row_factor, col_factor, tiles = panel_solve(spot, x_inverse, rows_in, cols_in)
 
-    solved = forward_solve(spot, x_inverse, inverse, gradients, inverses, panels, lower, lower_other)
+    solved = forward_solve(spot, x_inverse, inverse, gradients, inverses, panels, ties, lower, lower_other)
     solution_rows = spread_solution(spot, solved, z, x, y, core)
 
     out = update(blocks, row_factor, col_factor, None)

time: 644 us -> 640 us (level)
  starting transfers between devices: 151 us -> 189 us
  waiting for transfers between devices: 310 us -> 272 us
    ppermute x48 -> x46, starting transfers between devices: 108 us -> 145 us  [swap(): return lax.ppermute(value, ALL, pairs)]
    ppermute x48 -> x46, waiting for transfers between devices: 196 us -> 158 us  [swap(): return lax.ppermute(value, ALL, pairs)]
    pallas_call x7 -> x5, Pallas kernels: 45.9 us -> 40.9 us  [the longest x4 32.9 us: run(): pl.pallas_call(kernel, out_shape=outs, grid=(1,), in_specs=[SMEM] + specs...]
  transfers between devices with their start and end apart: 54 -> 52, of which waited for: 13 -> 11; matrix products, arithmetic and copies ran while one was open for 2% -> 3% of each run, Pallas kernels for 18% -> 18%
where the time goes in v4:
time: 640 us; the launch traced here: 637 us
  waiting for transfers between devices  272 us (42%)
  starting transfers between devices  189 us (30%)
  Pallas kernels  136 us (21%)
  local copies, waits for them, and re-layouts  17.4 us (3%)
  between operations  14.8 us (2%)
  other arithmetic  8.49 us (1%)
    ppermute x46, waiting for transfers between devices, swap(): return lax.ppermute(value, ALL, pairs)  158 us
    ppermute x46, starting transfers between devices, swap(): return lax.ppermute(value, ALL, pairs)  145 us
    ppermute x1, waiting for transfers between devices, share_cols(): return lax.ppermute(panel, ALL, pairs)  114 us
    pallas_call x1, Pallas kernels, inverse_factor(): pl.pallas_call(corner_kernel, out_shape=[shape(n, n), shape(n, n)], in_sp...  58.3 us
    pallas_call x4, Pallas kernels, run(): pl.pallas_call(kernel, out_shape=outs, grid=(1,), in_specs=[SMEM] + specs...  32.9 us
    all_to_all x1, starting transfers between devices, send_tiles(): lax.all_to_all(packed.reshape(8, 2 * part, cols), ('z', 'xh'), 0, 0, tile...  31.2 us
    pallas_call x2, Pallas kernels, update(): pl.pallas_call(update_kernel, out_shape=shape(count * rows * 8, lanes), g...  17.1 us
  transfers between devices with their start and end apart: 52, of which 11 were waited for; matrix products, arithmetic and copies ran while one was open for 3% of the time, Pallas kernels for 18%

profile of v4, /device:TPU:1, one launch (start us, length us, event | category | flops | bytes accessed | tf_op | source)
XLA Modules:
  0.0 637.4 jit_solution(3242280422330584954)
XLA Ops:
  7.9 7.4 %pack_tiles.1 = f32[16,128,1024]{2,1,0:T(8,128)} custom-call(s32[5]{0:T(128)} %stack.77.spot_ref, f32[128,16384]{1,0:T(8,128)} %factor_ref.1, f32[1,128]{1,0:T(1,128)} %bitcast.35), custom_call_target="tpu_custom_call" | custom-call | tf_op jit(solution)/shard_map/pack_tiles/pallas_call | solution.py:182
  15.3 7.0 %all-to-all-start = ((f32[16,128,1024]{2,1,0:T(8,128)}), f32[16,128,1024]{2,1,0:T(8,128)}, u32[]{:S(2)}, u32[]{:S(2)}) async-start(f32[16,128,1024]{2,1,0:T(8,128)} %pack_tiles.1), calls=%async_computation | async-start | bytes 16777216 | tf_op jit(solution)/shard_map/all_to_all | solution.py:192
  24.2 4.4 collective-permute-start.14
  28.6 113.8 %collective-permute-done.14 = f32[128,512]{1,0:T(8,128)S(1)} collective-permute-done((f32[128,512]{1,0:T(8,128)S(1)}, f32[128,512]{1,0:T(8,128)S(1)}, u32[]{:S(2)}, u32[]{:S(2)}) %collective-permute-start.14) | collective-permute-done | bytes 262176 | tf_op jit(solution)/shard_map/ppermute | solution.py:234
  144.6 31.2 %all-to-all-start.1 = ((f32[8,256,1024]{2,1,0:T(8,128)}), f32[8,256,1024]{2,1,0:T(8,128)}, u32[]{:S(2)}, u32[]{:S(2)}) async-start(f32[8,256,1024]{2,1,0:T(8,128)} %bitcast.6), calls=%async_computation.1 | async-start | bytes 16777216 | tf_op jit(solution)/shard_map/all_to_all | solution.py:193
  177.6 6.2 collective-permute-start.15
  183.8 98.5 %collective-permute-done.15.a0 = f32[128,512]{1,0:T(8,128)} collective-permute-done((f32[128,512]{1,0:T(8,128)S(1)}, f32[128,512]{1,0:T(8,128)}, u32[]{:S(2)}, u32[]{:S(2)}) %collective-permute-start.15) | collective-permute-done | bytes 262176 | tf_op jit(solution)/shard_map/ppermute | solution.py:66
  297.7 44.3 %collective-permute-start.4 = (f32[32,512]{1,0:T(8,128)S(1)}, f32[32,512]{1,0:T(8,128)S(1)}, u32[]{:S(2)}, u32[]{:S(2)}) collective-permute-start(f32[32,512]{1,0:T(8,128)S(1)} %slice_select_fusion), channel_id=1, source_target_pairs={{0,16},{1,17},{2,18},{3,19},{32,48},{33,49},{34,50},{35,51},{64,80... | collective-permute-start | bytes 196616 | tf_op jit(solution)/shard_map/ppermute | solution.py:66
  344.9 2.1 collective-permute-start.26
  346.9 3.0 pad_maximum_fusion.1.tie_own_ref
  349.9 2.0 collective-permute-start.30
  354.6 3.8 collective-permute-start.6
  360.4 2.5 collective-permute-start.9
  366.7 21.6 %collective-permute-start.12 = (f32[4,32,512]{2,1,0:T(8,128)S(1)}, f32[4,32,512]{2,1,0:T(8,128)S(1)}, u32[]{:S(2)}, u32[]{:S(2)}) collective-permute-start(f32[4,32,512]{2,1,0:T(8,128)S(1)} %pad_maximum_fusion.5.refs_0_), channel_id=1, source_target_pairs={{0,96},{1,97},{2,98},{3,99},{4,100},{5,101},{6,102},{7,103},{8,104... | collective-permute-start | bytes 786440 | tf_op jit(solution)/shard_map/ppermute | solution.py:66
  390.3 8.9 %collective-permute-start.11 = (f32[4,32,512]{2,1,0:T(8,128)S(1)}, f32[4,32,512]{2,1,0:T(8,128)S(1)}, u32[]{:S(2)}, u32[]{:S(2)}) collective-permute-start(f32[4,32,512]{2,1,0:T(8,128)S(1)} %pad_maximum_fusion.5.refs_0_), channel_id=1, source_target_pairs={{0,64},{1,65},{2,66},{3,67},{4,68},{5,69},{6,70},{7,71},{8,72},{9,... | collective-permute-start | bytes 786440 | tf_op jit(solution)/shard_map/ppermute | solution.py:66
  401.5 7.2 %collective-permute-done.11.refs_2_ = f32[4,32,512]{2,1,0:T(8,128)S(1)} collective-permute-done((f32[4,32,512]{2,1,0:T(8,128)S(1)}, f32[4,32,512]{2,1,0:T(8,128)S(1)}, u32[]{:S(2)}, u32[]{:S(2)}) %collective-permute-start.11) | collective-permute-done | bytes 262176 | tf_op jit(solution)/shard_map/ppermute | solution.py:66
  408.7 6.8 %collective-permute-start.10 = (f32[4,32,512]{2,1,0:T(8,128)S(1)}, f32[4,32,512]{2,1,0:T(8,128)S(1)}, u32[]{:S(2)}, u32[]{:S(2)}) collective-permute-start(f32[4,32,512]{2,1,0:T(8,128)S(1)} %pad_maximum_fusion.5.refs_0_), channel_id=1, source_target_pairs={{0,32},{1,33},{2,34},{3,35},{4,36},{5,37},{6,38},{7,39},{8,40},{9,... | collective-permute-start | bytes 786440 | tf_op jit(solution)/shard_map/ppermute | solution.py:66
  415.6 7.8 %collective-permute-done.10.refs_1_ = f32[4,32,512]{2,1,0:T(8,128)S(1)} collective-permute-done((f32[4,32,512]{2,1,0:T(8,128)S(1)}, f32[4,32,512]{2,1,0:T(8,128)S(1)}, u32[]{:S(2)}, u32[]{:S(2)}) %collective-permute-start.10) | collective-permute-done | bytes 262176 | tf_op jit(solution)/shard_map/ppermute | solution.py:66
  425.4 58.3 %inverse_factor.1 = (f32[512,512]{1,0:T(8,128)}, f32[512,512]{1,0:T(8,128)}) custom-call(s32[5]{0:T(128)} %stack.77.spot_ref, f32[4,32,512]{2,1,0:T(8,128)} %copy-done.4, f32[4,32,512]{2,1,0:T(8,128)} %copy-done.11, f32[4,32,512]{2,1,0:T(8,128)} %copy-done.10, f32[4,32,512]{2,1,0:T(8,128)} %copy-done.9), custom_call_target="tpu_custom_call" | custom-call | tf_op jit(solution)/shard_map/inverse_factor/pallas_call | solution.py:129
  483.7 5.4 solve.4
  493.0 8.0 %place_panels.1 = (f32[512,3072]{1,0:T(8,128)}, f32[2,512,512]{2,1,0:T(8,128)}) custom-call(s32[5]{0:T(128)} %stack.77.spot_ref, f32[4,256,512]{2,1,0:T(8,128)} %copy-done.1, f32[4,256,512]{2,1,0:T(8,128)} %collective-permute-done.26.other_ref, f32[4,256,512]{2,1,0:T(8,128)} %pad_maximum_fusion.1.tie_own_ref, ...), custom_call_target="tpu_custom_call" | custom-call | tf_op jit(solution)/shard_map/place_panels/pallas_call | solution.py:305
  501.8 12.3 %solve.5 = (f32[512,128]{1,0:T(8,128)}, f32[512,128]{1,0:T(8,128)}, f32[512,128]{1,0:T(8,128)}, f32[256,128]{1,0:T(8,128)}) custom-call(s32[5]{0:T(128)} %stack.77.spot_ref, f32[3072,128]{1,0:T(8,128)} %grads_ref.5, f32[256,128]{1,0:T(8,128)} %get-tuple-element.26.refs_0_, f32[256,128]{1,0:T(8,128)} %copy-done.13, ...), custom_call_target="tpu_custom_call" | custom-call | tf_op jit(solution)/shard_map/solve/pallas_call | solution.py:394
  518.7 12.4 %solve.6 = (f32[512,128]{1,0:T(8,128)}, f32[512,128]{1,0:T(8,128)}, f32[512,128]{1,0:T(8,128)}, f32[256,128]{1,0:T(8,128)}) custom-call(s32[5]{0:T(128)} %stack.77.spot_ref, f32[3072,128]{1,0:T(8,128)} %grads_ref.5, f32[256,128]{1,0:T(8,128)} %get-tuple-element.32.refs_0_, f32[256,128]{1,0:T(8,128)} %copy-done.16, f32[256,128]{1,0:T(8,128)} %copy-done.15, ...), custom_call_target="tpu_custom_call" | custom-call | tf_op jit(solution)/shard_map/solve/pallas_call | solution.py:394
  536.5 2.8 solve.7
  543.2 32.1 %collective-permute-done.39 = f32[384,128]{1,0:T(8,128)S(1)} collective-permute-done((f32[384,128]{1,0:T(8,128)S(1)}, f32[384,128]{1,0:T(8,128)S(1)}, u32[]{:S(2)}, u32[]{:S(2)}) %collective-permute-start.39) | collective-permute-done | bytes 196640 | tf_op jit(solution)/shard_map/ppermute | solution.py:66
  580.6 2.1 collective-permute-done.41
  586.1 4.6 collective-permute-done.46
  591.3 6.9 %collective-permute-start.47 = (f32[4,384,128]{2,1,0:T(8,128)S(1)}, f32[4,384,128]{2,1,0:T(8,128)S(1)}, u32[]{:S(2)}, u32[]{:S(2)}) collective-permute-start(f32[4,384,128]{2,1,0:T(8,128)S(1)} %pad_maximum_fusion.2.own_ref), channel_id=1, source_target_pairs={{0,1},{1,0},{2,3},{3,2},{4,5},{5,4},{6,7},{7,6},{8,9},{9,8},{10,11... | collective-permute-start | bytes 2359304 | tf_op jit(solution)/shard_map/ppermute | solution.py:66
  601.1 2.6 place_rows.1
  603.7 9.7 %panel_solve.1 = (f32[2048,512]{1,0:T(8,128)}, f32[1024,512]{1,0:T(8,128)}, f32[128,512]{1,0:T(8,128)}) custom-call(s32[5]{0:T(128)} %stack.77.spot_ref, f32[512,512]{1,0:T(8,128)} %get-tuple-element.20.x_ref, f32[2048,512]{1,0:T(8,128)} %all-gather.3.cloned.1.call-done.rows_ref, f32[1024,512]{1,0:T(8,128)} %all-gather.5.cloned.1.call-done.cols_ref), custom_call_target="tpu_custom_call" | custom-call | tf_op jit(solution)/shard_map/panel_solve/pallas_call | solution.py:211
  613.4 8.4 %update.2.refs_0_ = f32[16384,128]{1,0:T(8,128)} custom-call(f32[8,256,1024]{2,1,0:T(8,128)} %all-to-all-done.1.block_ref, f32[2048,512]{1,0:T(8,128)} %get-tuple-element.21.row_ref, f32[1024,512]{1,0:T(8,128)} %get-tuple-element.22.col_ref), custom_call_target="tpu_custom_call" | custom-call | tf_op jit(solution)/shard_map/update/pallas_call | solution.py:259
  621.8 8.7 %update.3 = f32[16384,128]{1,0:T(8,128)} custom-call(f32[8,256,1024]{2,1,0:T(8,128)} %all-to-all-done.1.block_ref, f32[2048,512]{1,0:T(8,128)} %get-tuple-element.21.row_ref, f32[1024,512]{1,0:T(8,128)} %get-tuple-element.22.col_ref, f32[16384,128]{1,0:T(8,128)} %update.2.refs_0_), custom_call_target="tpu_custom_call", output_to_operand_aliasing={{}: (3, {})} | custom-call | tf_op jit(solution)/shard_map/update/pallas_call | solution.py:259
  (156 shorter events, 69.6 us)
Async XLA Ops:
  15.3 129.4 %all-to-all-start = ((f32[16,128,1024]{2,1,0:T(8,128)}), f32[16,128,1024]{2,1,0:T(8,128)}, u32[]{:S(2)}, u32[]{:S(2)}) async-start(f32[16,128,1024]{2,1,0:T(8,128)} %pack_tiles.1), calls=%async_computation | async-start | bytes 16777216 | tf_op jit(solution)/shard_map/all_to_all | solution.py:192
  22.3 581.4 %all-gather.5.cloned.1.call-start = ((), (), s32[]{:S(2)}) async-start(), calls=%async_computation.3 | async-start | bytes 2359296 | tf_op jit(solution)/shard_map/all_gather | solution.py:485
  24.2 118.2 %collective-permute-start.14 = (f32[128,512]{1,0:T(8,128)S(1)}, f32[128,512]{1,0:T(8,128)S(1)}, u32[]{:S(2)}, u32[]{:S(2)}) collective-permute-start(f32[128,512]{1,0:T(8,128)S(1)} %get-tuple-element.42), channel_id=1, source_target_pairs={{0,0},{1,16},{2,1},{3,17},{4,2},{5,18},{6,3},{7,19},{8,4},{9,20},{... | collective-permute-start | bytes 786440 | tf_op jit(solution)/shard_map/ppermute | solution.py:234
  143.2 460.6 %all-gather.3.cloned.1.call-start = ((), (), s32[]{:S(2)}) async-start(), calls=%async_computation.2 | async-start | bytes 4456448 | tf_op jit(solution)/shard_map/all_gather | solution.py:486
  144.6 468.8 %all-to-all-start.1 = ((f32[8,256,1024]{2,1,0:T(8,128)}), f32[8,256,1024]{2,1,0:T(8,128)}, u32[]{:S(2)}, u32[]{:S(2)}) async-start(f32[8,256,1024]{2,1,0:T(8,128)} %bitcast.6), calls=%async_computation.1 | async-start | bytes 16777216 | tf_op jit(solution)/shard_map/all_to_all | solution.py:193
  176.9 105.5 %collective-permute-start.17 = (f32[128,1024]{1,0:T(8,128)S(1)}, f32[128,1024]{1,0:T(8,128)S(1)}, u32[]{:S(2)}, u32[]{:S(2)}) collective-permute-start(f32[128,1024]{1,0:T(8,128)S(1)} %slice.38), channel_id=1, source_target_pairs={{8,16},{9,17},{10,18},{11,19},{12,20},{13,21},{14,22},{15,23}} | collective-permute-start | bytes 1572872 | tf_op jit(solution)/shard_map/ppermute | solution.py:66
  177.6 104.7 %collective-permute-start.15 = (f32[128,512]{1,0:T(8,128)S(1)}, f32[128,512]{1,0:T(8,128)}, u32[]{:S(2)}, u32[]{:S(2)}) collective-permute-start(f32[128,512]{1,0:T(8,128)S(1)} %get-tuple-element.42), channel_id=1, source_target_pairs={{0,16},{1,17},{2,18},{3,19},{4,20},{5,21},{6,22},{7,23}} | collective-permute-start | bytes 786440 | tf_op jit(solution)/shard_map/ppermute | solution.py:66
  283.4 11.5 %collective-permute-start.24 = (f32[256,512]{1,0:T(8,128)}, f32[256,512]{1,0:T(8,128)S(1)}, u32[]{:S(2)}, u32[]{:S(2)}) collective-permute-start(f32[256,512]{1,0:T(8,128)} %get-tuple-element.48), channel_id=1, source_target_pairs={{16,20},{17,21},{18,22},{19,23},{20,16},{21,17},{22,18},{23,19}} | collective-permute-start | bytes 1572872 | tf_op jit(solution)/shard_map/ppermute | solution.py:66
  285.4 10.9 %collective-permute-start.23 = (f32[256,512]{1,0:T(8,128)}, f32[256,512]{1,0:T(8,128)}, u32[]{:S(2)}, u32[]{:S(2)}) collective-permute-start(f32[256,512]{1,0:T(8,128)} %get-tuple-element.48), channel_id=1, source_target_pairs={{16,18},{17,19},{18,16},{19,17},{20,22},{21,23},{22,20},{23,21}} | collective-permute-start | bytes 1572872 | tf_op jit(solution)/shard_map/ppermute | solution.py:66
  286.9 10.7 %collective-permute-start.25 = (f32[256,512]{1,0:T(8,128)}, f32[256,512]{1,0:T(8,128)}, u32[]{:S(2)}, u32[]{:S(2)}) collective-permute-start(f32[256,512]{1,0:T(8,128)} %get-tuple-element.48), channel_id=1, source_target_pairs={{16,22},{17,23},{18,20},{19,21},{20,18},{21,19},{22,16},{23,17}} | collective-permute-start | bytes 1572872 | tf_op jit(solution)/shard_map/ppermute | solution.py:66
  291.9 51.6 %collective-permute-start.28 = (f32[256,512]{1,0:T(8,128)}, f32[256,512]{1,0:T(8,128)}, u32[]{:S(2)}, u32[]{:S(2)}) collective-permute-start(f32[256,512]{1,0:T(8,128)} %get-tuple-element.44), channel_id=1, source_target_pairs={{16,20},{17,21},{18,22},{19,23}} | collective-permute-start | bytes 1572872 | tf_op jit(solution)/shard_map/ppermute | solution.py:66
  293.4 51.5 %collective-permute-start.27 = (f32[256,512]{1,0:T(8,128)}, f32[256,512]{1,0:T(8,128)}, u32[]{:S(2)}, u32[]{:S(2)}) collective-permute-start(f32[256,512]{1,0:T(8,128)} %get-tuple-element.44), channel_id=1, source_target_pairs={{16,18},{17,19},{18,16},{19,17}} | collective-permute-start | bytes 1572872 | tf_op jit(solution)/shard_map/ppermute | solution.py:66
  294.9 52.1 %collective-permute-start.29 = (f32[256,512]{1,0:T(8,128)}, f32[256,512]{1,0:T(8,128)}, u32[]{:S(2)}, u32[]{:S(2)}) collective-permute-start(f32[256,512]{1,0:T(8,128)} %get-tuple-element.44), channel_id=1, source_target_pairs={{16,22},{17,23},{18,20},{19,21}} | collective-permute-start | bytes 1572872 | tf_op jit(solution)/shard_map/ppermute | solution.py:66
  296.3 55.6 %collective-permute-start.5 = (f32[32,512]{1,0:T(8,128)S(1)}, f32[32,512]{1,0:T(8,128)S(1)}, u32[]{:S(2)}, u32[]{:S(2)}) collective-permute-start(f32[32,512]{1,0:T(8,128)S(1)} %slice_select_fusion), channel_id=1, source_target_pairs={{0,24},{1,25},{2,26},{3,27},{32,56},{33,57},{34,58},{35,59},{64,88... | collective-permute-start | bytes 196616 | tf_op jit(solution)/shard_map/ppermute | solution.py:66
  297.7 54.3 %collective-permute-start.4 = (f32[32,512]{1,0:T(8,128)S(1)}, f32[32,512]{1,0:T(8,128)S(1)}, u32[]{:S(2)}, u32[]{:S(2)}) collective-permute-start(f32[32,512]{1,0:T(8,128)S(1)} %slice_select_fusion), channel_id=1, source_target_pairs={{0,16},{1,17},{2,18},{3,19},{32,48},{33,49},{34,50},{35,51},{64,80... | collective-permute-start | bytes 196616 | tf_op jit(solution)/shard_map/ppermute | solution.py:66
  343.5 8.4 %collective-permute-start.3 = (f32[32,512]{1,0:T(8,128)S(1)}, f32[32,512]{1,0:T(8,128)S(1)}, u32[]{:S(2)}, u32[]{:S(2)}) collective-permute-start(f32[32,512]{1,0:T(8,128)S(1)} %slice_select_fusion), channel_id=1, source_target_pairs={{0,8},{1,9},{2,10},{3,11},{32,40},{33,41},{34,42},{35,43},{64,72},... | collective-permute-start | bytes 196616 | tf_op jit(solution)/shard_map/ppermute | solution.py:66
  344.9 146.3 %collective-permute-start.26 = (f32[4,256,512]{2,1,0:T(8,128)S(1)}, f32[4,256,512]{2,1,0:T(8,128)}, u32[]{:S(2)}, u32[]{:S(2)}) collective-permute-start(f32[4,256,512]{2,1,0:T(8,128)S(1)} %pad_maximum_fusion.own_ref), channel_id=1, source_target_pairs={{16,17},{17,16},{18,19},{19,18},{20,21},{21,20},{22,23},{23,22}} | collective-permute-start | bytes 6291464 | tf_op jit(solution)/shard_map/ppermute | solution.py:66
  349.9 143.0 %collective-permute-start.30 = (f32[4,256,512]{2,1,0:T(8,128)}, f32[4,256,512]{2,1,0:T(8,128)}, u32[]{:S(2)}, u32[]{:S(2)}) collective-permute-start(f32[4,256,512]{2,1,0:T(8,128)} %pad_maximum_fusion.1.tie_own_ref), channel_id=1, source_target_pairs={{16,17},{17,16},{18,19},{19,18},{20,21},{21,20},{22,23},{23,22}} | collective-permute-start | bytes 6291464 | tf_op jit(solution)/shard_map/ppermute | solution.py:66
  364.3 136.7 %collective-permute-start.31 = (f32[128,2560]{1,0:T(8,128)S(1)}, f32[128,2560]{1,0:T(8,128)}, u32[]{:S(2)}, u32[]{:S(2)}) collective-permute-start(f32[128,2560]{1,0:T(8,128)S(1)} %slice.43.refs_12_.refs_13_), channel_id=1, source_target_pairs={{16,17},{17,16},{18,19},{19,18},{20,21},{21,20},{22,23},{23,22}} | collective-permute-start | bytes 3932168 | tf_op jit(solution)/shard_map/ppermute | solution.py:66
  366.0 24.2 %collective-permute-start.18 = (f32[128,512]{1,0:T(8,128)}, f32[128,512]{1,0:T(8,128)S(1)}, u32[]{:S(2)}, u32[]{:S(2)}) collective-permute-start(f32[128,512]{1,0:T(8,128)} %get-tuple-element.41), channel_id=1, source_target_pairs={{8,16},{9,17},{10,18},{11,19},{12,20},{13,21},{14,22},{15,23}} | collective-permute-start | bytes 786440 | tf_op jit(solution)/shard_map/ppermute | solution.py:66
  366.7 33.1 %collective-permute-start.12 = (f32[4,32,512]{2,1,0:T(8,128)S(1)}, f32[4,32,512]{2,1,0:T(8,128)S(1)}, u32[]{:S(2)}, u32[]{:S(2)}) collective-permute-start(f32[4,32,512]{2,1,0:T(8,128)S(1)} %pad_maximum_fusion.5.refs_0_), channel_id=1, source_target_pairs={{0,96},{1,97},{2,98},{3,99},{4,100},{5,101},{6,102},{7,103},{8,104... | collective-permute-start | bytes 786440 | tf_op jit(solution)/shard_map/ppermute | solution.py:66
  390.3 18.4 %collective-permute-start.11 = (f32[4,32,512]{2,1,0:T(8,128)S(1)}, f32[4,32,512]{2,1,0:T(8,128)S(1)}, u32[]{:S(2)}, u32[]{:S(2)}) collective-permute-start(f32[4,32,512]{2,1,0:T(8,128)S(1)} %pad_maximum_fusion.5.refs_0_), channel_id=1, source_target_pairs={{0,64},{1,65},{2,66},{3,67},{4,68},{5,69},{6,70},{7,71},{8,72},{9,... | collective-permute-start | bytes 786440 | tf_op jit(solution)/shard_map/ppermute | solution.py:66
  399.9 83.8 %collective-permute-start.19 = (f32[128,1536]{1,0:T(8,128)}, f32[128,1536]{1,0:T(8,128)}, u32[]{:S(2)}, u32[]{:S(2)}) collective-permute-start(f32[128,1536]{1,0:T(8,128)} %constant_dynamic-update-slice_fusion.a1.refs_11_), channel_id=1, source_target_pairs={{16,17},{17,16},{18,19},{19,18},{20,21},{21,20},{22,23},{23,22}} | collective-permute-start | bytes 2359304 | tf_op jit(solution)/shard_map/ppermute | solution.py:66
  408.7 14.6 %collective-permute-start.10 = (f32[4,32,512]{2,1,0:T(8,128)S(1)}, f32[4,32,512]{2,1,0:T(8,128)S(1)}, u32[]{:S(2)}, u32[]{:S(2)}) collective-permute-start(f32[4,32,512]{2,1,0:T(8,128)S(1)} %pad_maximum_fusion.5.refs_0_), channel_id=1, source_target_pairs={{0,32},{1,33},{2,34},{3,35},{4,36},{5,37},{6,38},{7,39},{8,40},{9,... | collective-permute-start | bytes 786440 | tf_op jit(solution)/shard_map/ppermute | solution.py:66
  424.0 59.7 %collective-permute-start.16 = (f32[128,512]{1,0:T(8,128)}, f32[128,512]{1,0:T(8,128)}, u32[]{:S(2)}, u32[]{:S(2)}) collective-permute-start(f32[128,512]{1,0:T(8,128)} %collective-permute-done.15.a0), channel_id=1, source_target_pairs={{16,17},{17,16},{18,19},{19,18},{20,21},{21,20},{22,23},{23,22}} | collective-permute-start | bytes 786440 | tf_op jit(solution)/shard_map/ppermute | solution.py:66
  489.1 11.9 %collective-permute-start.22 = (f32[256,128]{1,0:T(8,128)}, f32[256,128]{1,0:T(8,128)S(1)}, u32[]{:S(2)}, u32[]{:S(2)}) collective-permute-start(f32[256,128]{1,0:T(8,128)} %get-tuple-element.26.refs_0_), channel_id=1, source_target_pairs={{16,22},{17,23},{18,20},{19,21},{20,18},{21,19},{22,16},{23,17}} | collective-permute-start | bytes 393224 | tf_op jit(solution)/shard_map/ppermute | solution.py:66
  489.8 11.3 %collective-permute-start.21 = (f32[256,128]{1,0:T(8,128)}, f32[256,128]{1,0:T(8,128)}, u32[]{:S(2)}, u32[]{:S(2)}) collective-permute-start(f32[256,128]{1,0:T(8,128)} %get-tuple-element.26.refs_0_), channel_id=1, source_target_pairs={{16,20},{17,21},{18,22},{19,23},{20,16},{21,17},{22,18},{23,19}} | collective-permute-start | bytes 393224 | tf_op jit(solution)/shard_map/ppermute | solution.py:66
  491.1 10.0 %collective-permute-start.20 = (f32[256,128]{1,0:T(8,128)}, f32[256,128]{1,0:T(8,128)S(1)}, u32[]{:S(2)}, u32[]{:S(2)}) collective-permute-start(f32[256,128]{1,0:T(8,128)} %get-tuple-element.26.refs_0_), channel_id=1, source_target_pairs={{16,18},{17,19},{18,16},{19,17},{20,22},{21,23},{22,20},{23,21}} | collective-permute-start | bytes 393224 | tf_op jit(solution)/shard_map/ppermute | solution.py:66
  541.0 34.4 %collective-permute-start.39 = (f32[384,128]{1,0:T(8,128)S(1)}, f32[384,128]{1,0:T(8,128)S(1)}, u32[]{:S(2)}, u32[]{:S(2)}) collective-permute-start(f32[384,128]{1,0:T(8,128)S(1)} %constant_dynamic-slice_fusion), channel_id=1, source_target_pairs={{16,0},{17,1},{18,2},{19,3},{20,4},{21,5},{22,6},{23,7}} | collective-permute-start | bytes 589832 | tf_op jit(solution)/shard_map/ppermute | solution.py:66
  542.3 33.1 %collective-permute-start.38 = (f32[384,128]{1,0:T(8,128)S(1)}, f32[384,128]{1,0:T(8,128)S(1)}, u32[]{:S(2)}, u32[]{:S(2)}) collective-permute-start(f32[384,128]{1,0:T(8,128)S(1)} %constant_dynamic-slice_fusion), channel_id=1, source_target_pairs={{16,24},{17,25},{18,26},{19,27},{20,28},{21,29},{22,30},{23,31}} | collective-permute-start | bytes 589832 | tf_op jit(solution)/shard_map/ppermute | solution.py:66
  582.7 7.9 %collective-permute-start.46 = (f32[384,128]{1,0:T(8,128)S(1)}, f32[384,128]{1,0:T(8,128)S(1)}, u32[]{:S(2)}, u32[]{:S(2)}) collective-permute-start(f32[384,128]{1,0:T(8,128)S(1)} %add_select_fusion), channel_id=1, source_target_pairs={{0,6},{1,7},{2,4},{3,5},{4,2},{5,3},{6,0},{7,1},{8,14},{9,15},{10,... | collective-permute-start | bytes 589832 | tf_op jit(solution)/shard_map/ppermute | solution.py:66
  591.3 8.9 %collective-permute-start.47 = (f32[4,384,128]{2,1,0:T(8,128)S(1)}, f32[4,384,128]{2,1,0:T(8,128)S(1)}, u32[]{:S(2)}, u32[]{:S(2)}) collective-permute-start(f32[4,384,128]{2,1,0:T(8,128)S(1)} %pad_maximum_fusion.2.own_ref), channel_id=1, source_target_pairs={{0,1},{1,0},{2,3},{3,2},{4,5},{5,4},{6,7},{7,6},{8,9},{9,8},{10,11... | collective-permute-start | bytes 2359304 | tf_op jit(solution)/shard_map/ppermute | solution.py:66
  (41 other events, 377.6 us)
Sparse Core Ops, SparseCore 0:
  143.3 141.9 all-gather.4
  287.0 37.1 all-gather.2

commit v5 on v4

--- a/solution.py
+++ b/solution.py
@@ -179,7 +179,7 @@
     part, order = factor.shape
     rows = part // 4
     cols = order // 16
-    packed = pl.pallas_call(
+    pack = pl.pallas_call(
         pack_kernel,
         out_shape=shape(16, part, cols),
         grid=(4,),
@@ -188,7 +188,8 @@
         scratch_shapes=[pltpu.VMEM((rows, order), F32)],
         interpret=INTERPRET,
         name="pack_tiles",
-    )(spot, factor, damping)
+    )
+    packed = pack(spot, factor, damping)
     packed = lax.all_to_all(packed, ("xl", "y", "core"), 0, 0, tiled=True)
     return lax.all_to_all(packed.reshape(8, 2 * part, cols), ("z", "xh"), 0, 0, tiled=True)
 
@@ -347,11 +348,13 @@
     return odd, shares
 
 
-def solve_first_kernel(spot_ref, grads_ref, x_ref, square_ref, a0, b0, a1, b1, y_ref, v_ref, share_ref):
+def solve_first_kernel(spot_ref, grads_ref, x_ref, square_ref, own_ref, other_ref, y_ref, v_ref, share_ref):
     panel = x_ref.shape[0]
+    part = panel // 4
+    sources = [(ref[0:part, :], ref[part : 2 * part, :]) for ref in (own_ref, other_ref)]
     lead = grads_ref[0:panel, :]
     v = dot_e(square_ref[...], lead, NN)
-    write_share(spot_ref, grads_ref, share_ref, ((a0, a1), (b0, b1)), [], v, (1, 0))
+    write_share(spot_ref, grads_ref, share_ref, sources, [], v, (1, 0))
     y_ref[...] = dot_e(x_ref[...], lead, NN)
     v_ref[...] = v
 
@@ -385,7 +388,7 @@
     refs[5][...] = dot_e(refs[4][0], right, NN)
 
 
-def forward_solve(spot, x, square, grads, inverses, panels, ties, own, other):
+def forward_solve(spot, x, square, grads, inverses, panels, ties, start, own, other):
     panel = x.shape[0]
     count = grads.shape[1]
     full, tile = shape(panel, count), shape(panel // 2, count)
@@ -406,15 +409,15 @@
 
     inverse = lambda b: pl.BlockSpec((1, panel, panel), lambda i: (b - 1, 0, 0))
     leading = lambda b: pl.BlockSpec((panel, panel), lambda i: (0, b))
-    operands = [grads, x, square, own[0], other[0], own[1], other[1]]
-    first, v, share = run(solve_first_kernel, operands, [VMEM] * 7, [full, full, tile])
+    operands = [grads, x, square, *start]
+    first, v, share = run(solve_first_kernel, operands, [VMEM] * 5, [full, full, tile])
     solved = [first]
     for pair in range(2):
         a, b = 2 * pair + 1, 2 * pair + 2
         operands = [grads, *exchange(share), inverses, inverses, square, panels, panels, ties, v]
         specs = [VMEM] * 5 + [inverse(a), inverse(b), VMEM, leading(a), leading(b)]
         specs += [pl.BlockSpec((1, panel, panel), lambda i, p=pair: (p, 0, 0)), VMEM]
-        rest = solved[1:] + ([own[1], own[2], other[1], other[2]] if pair == 0 else [own[2], other[2]])
+        rest = solved[1:] + ([own[0], own[1], other[0], other[1]] if pair == 0 else [own[1], other[1]])
         outs = [full, full, full, tile]
         kernel = functools.partial(solve_pair_kernel, pair=pair)
         y_a, y_b, v, share = run(kernel, operands + rest, specs + [VMEM] * len(rest), outs)
@@ -479,6 +482,8 @@
     tie = jnp.concatenate([moved[:, panel_width:], tie], axis=0)
     from_low = lambda zz, xx, yy, cc: on_line(zz, xx, yy, cc) and yy < 2
     ties = jnp.stack([tie] + [swap(tie, dy=m, only=from_low) for m in (1, 2, 3)])
+    start_own = jnp.concatenate(lead[:2], axis=0)
+    start_other = swap(start_own, dcore=1, only=on_line)
     cols_share = share_cols(panel)
     rows_share = share_rows(panel)
     second = swap(factor[:, 2 * panel_width : 3 * panel_width], dx=3, only=from_second)
@@ -487,19 +492,20 @@
     blocks = send_tiles(spot, factor, damping[None, :])
 
     lower = [
-        lead[0],
+        None,
         jnp.concatenate([moved, second], axis=1),
         factor[:, : 5 * panel_width],
     ]
     lines_other = swap(lines, dcore=1, only=on_line)
     ties_other = swap(ties, dcore=1, only=on_line)
-    lower_other = [swap(value, dcore=1, only=on_line) for value in lower]
+    lower_other = [swap(value, dcore=1, only=on_line) for value in lower[1:]]
 
     x_inverse, inverse = inverse_factor(spot, pieces)
     panels, ties = place_panels(spot, lines, lines_other, ties, ties_other)
     row_factor, col_factor, tiles = panel_solve(spot, x_inverse, rows_in, cols_in)
 
-    solved = forward_solve(spot, x_inverse, inverse, gradients, inverses, panels, ties, lower, lower_other)
+    start = (start_own, start_other)
+    solved = forward_solve(spot, x_inverse, inverse, gradients, inverses, panels, ties, start, lower[1:], lower_other)
     solution_rows = spread_solution(spot, solved, z, x, y, core)
 
     out = update(blocks, row_factor, col_factor, None)

time: 640 us -> 629 us (0.983)
  waiting for transfers between devices: 272 us -> 256 us
    ppermute x46, waiting for transfers between devices: 158 us -> 142 us  [swap(): return lax.ppermute(value, ALL, pairs)]
where the time goes in v5:
time: 629 us; the launch traced here: 627 us
  waiting for transfers between devices  256 us (41%)
  starting transfers between devices  194 us (31%)
  Pallas kernels  136 us (22%)
  local copies, waits for them, and re-layouts  18.2 us (3%)
  between operations  14.8 us (2%)
  other arithmetic  7.83 us (1%)
    ppermute x46, starting transfers between devices, swap(): return lax.ppermute(value, ALL, pairs)  151 us
    ppermute x46, waiting for transfers between devices, swap(): return lax.ppermute(value, ALL, pairs)  142 us
    ppermute x1, waiting for transfers between devices, share_cols(): return lax.ppermute(panel, ALL, pairs)  114 us
    pallas_call x1, Pallas kernels, inverse_factor(): pl.pallas_call(corner_kernel, out_shape=[shape(n, n), shape(n, n)], in_sp...  58.3 us
    pallas_call x4, Pallas kernels, run(): pl.pallas_call(kernel, out_shape=outs, grid=(1,), in_specs=[SMEM] + specs...  32.6 us
    all_to_all x1, starting transfers between devices, send_tiles(): lax.all_to_all(packed.reshape(8, 2 * part, cols), ('z', 'xh'), 0, 0, tile...  31.2 us
    pallas_call x2, Pallas kernels, update(): pl.pallas_call(update_kernel, out_shape=shape(count * rows * 8, lanes), g...  17.1 us
    unnamed x48, local copies, waits for them, and re-layouts  13.3 us
  transfers between devices with their start and end apart: 52, of which 11 were waited for; matrix products, arithmetic and copies ran while one was open for 3% of the time, Pallas kernels for 18%

profile of v5, /device:TPU:1, one launch (start us, length us, event | category | flops | bytes accessed | tf_op | source)
XLA Modules:
  0.0 627.1 jit_solution(12041918502417685821)
XLA Ops:
  7.8 7.4 %pack_tiles.1 = f32[16,128,1024]{2,1,0:T(8,128)} custom-call(s32[5]{0:T(128)} %stack.77.spot_ref, f32[128,16384]{1,0:T(8,128)} %factor_ref.1, f32[1,128]{1,0:T(1,128)} %bitcast.34), custom_call_target="tpu_custom_call" | custom-call | tf_op jit(solution)/shard_map/pack_tiles/pallas_call | solution.py:192
  15.2 7.0 %all-to-all-start = ((f32[16,128,1024]{2,1,0:T(8,128)}), f32[16,128,1024]{2,1,0:T(8,128)}, u32[]{:S(2)}, u32[]{:S(2)}) async-start(f32[16,128,1024]{2,1,0:T(8,128)} %pack_tiles.1), calls=%async_computation | async-start | bytes 16777216 | tf_op jit(solution)/shard_map/all_to_all | solution.py:193
  24.2 4.4 collective-permute-start.14
  28.6 113.8 %collective-permute-done.14 = f32[128,512]{1,0:T(8,128)S(1)} collective-permute-done((f32[128,512]{1,0:T(8,128)S(1)}, f32[128,512]{1,0:T(8,128)S(1)}, u32[]{:S(2)}, u32[]{:S(2)}) %collective-permute-start.14) | collective-permute-done | bytes 262176 | tf_op jit(solution)/shard_map/ppermute | solution.py:235
  144.6 31.2 %all-to-all-start.1 = ((f32[8,256,1024]{2,1,0:T(8,128)}), f32[8,256,1024]{2,1,0:T(8,128)}, u32[]{:S(2)}, u32[]{:S(2)}) async-start(f32[8,256,1024]{2,1,0:T(8,128)} %bitcast.6), calls=%async_computation.1 | async-start | bytes 16777216 | tf_op jit(solution)/shard_map/all_to_all | solution.py:194
  177.6 5.5 collective-permute-start.15
  189.7 92.7 %collective-permute-done.15 = f32[128,512]{1,0:T(8,128)S(1)} collective-permute-done((f32[128,512]{1,0:T(8,128)S(1)}, f32[128,512]{1,0:T(8,128)S(1)}, u32[]{:S(2)}, u32[]{:S(2)}) %collective-permute-start.15) | collective-permute-done | bytes 262176 | tf_op jit(solution)/shard_map/ppermute | solution.py:66
  292.1 52.2 %collective-permute-start.4 = (f32[32,512]{1,0:T(8,128)S(1)}, f32[32,512]{1,0:T(8,128)S(1)}, u32[]{:S(2)}, u32[]{:S(2)}) collective-permute-start(f32[32,512]{1,0:T(8,128)S(1)} %slice_select_fusion), channel_id=1, source_target_pairs={{0,16},{1,17},{2,18},{3,19},{32,48},{33,49},{34,50},{35,51},{64,80... | collective-permute-start | bytes 196616 | tf_op jit(solution)/shard_map/ppermute | solution.py:66
  347.1 2.1 collective-permute-start.28
  349.2 2.9 pad_maximum_fusion.own_ref
  352.1 2.0 collective-permute-start.24
  356.7 2.7 collective-permute-start.6
  359.4 2.3 collective-permute-done.6
  361.8 3.0 collective-permute-start.9
  368.7 19.0 %collective-permute-start.12 = (f32[4,32,512]{2,1,0:T(8,128)S(1)}, f32[4,32,512]{2,1,0:T(8,128)S(1)}, u32[]{:S(2)}, u32[]{:S(2)}) collective-permute-start(f32[4,32,512]{2,1,0:T(8,128)S(1)} %pad_maximum_fusion.6.refs_0_), channel_id=1, source_target_pairs={{0,96},{1,97},{2,98},{3,99},{4,100},{5,101},{6,102},{7,103},{8,104... | collective-permute-start | bytes 786440 | tf_op jit(solution)/shard_map/ppermute | solution.py:66
  387.7 8.9 %collective-permute-start.11 = (f32[4,32,512]{2,1,0:T(8,128)S(1)}, f32[4,32,512]{2,1,0:T(8,128)S(1)}, u32[]{:S(2)}, u32[]{:S(2)}) collective-permute-start(f32[4,32,512]{2,1,0:T(8,128)S(1)} %pad_maximum_fusion.6.refs_0_), channel_id=1, source_target_pairs={{0,64},{1,65},{2,66},{3,67},{4,68},{5,69},{6,70},{7,71},{8,72},{9,... | collective-permute-start | bytes 786440 | tf_op jit(solution)/shard_map/ppermute | solution.py:66
  397.2 8.4 %collective-permute-start.10 = (f32[4,32,512]{2,1,0:T(8,128)S(1)}, f32[4,32,512]{2,1,0:T(8,128)S(1)}, u32[]{:S(2)}, u32[]{:S(2)}) collective-permute-start(f32[4,32,512]{2,1,0:T(8,128)S(1)} %pad_maximum_fusion.6.refs_0_), channel_id=1, source_target_pairs={{0,32},{1,33},{2,34},{3,35},{4,36},{5,37},{6,38},{7,39},{8,40},{9,... | collective-permute-start | bytes 786440 | tf_op jit(solution)/shard_map/ppermute | solution.py:66
  409.8 3.5 collective-permute-done.10.refs_1_
  415.5 58.3 %inverse_factor.1 = (f32[512,512]{1,0:T(8,128)}, f32[512,512]{1,0:T(8,128)}) custom-call(s32[5]{0:T(128)} %stack.77.spot_ref, f32[4,32,512]{2,1,0:T(8,128)} %copy-done.4, f32[4,32,512]{2,1,0:T(8,128)} %copy-done.10, f32[4,32,512]{2,1,0:T(8,128)} %copy-done.9, f32[4,32,512]{2,1,0:T(8,128)} %copy-done.8), custom_call_target="tpu_custom_call" | custom-call | tf_op jit(solution)/shard_map/inverse_factor/pallas_call | solution.py:129
  473.8 5.1 solve.4
  482.1 8.0 %place_panels.1 = (f32[512,3072]{1,0:T(8,128)}, f32[2,512,512]{2,1,0:T(8,128)}) custom-call(s32[5]{0:T(128)} %stack.77.spot_ref, f32[4,256,512]{2,1,0:T(8,128)} %pad_maximum_fusion.own_ref, f32[4,256,512]{2,1,0:T(8,128)} %collective-permute-done.24.other_ref, f32[4,256,512]{2,1,0:T(8,128)} %copy-done.1, f32[4,256,512]{2,1,0:T(8,128)} %collective-permute-done.28.tie_other_ref), custom_call_target="tpu_custom_call" | custom-call | tf_op jit(solution)/shard_map/place_panels/pallas_call | solution.py:306
  491.0 12.3 %solve.5 = (f32[512,128]{1,0:T(8,128)}, f32[512,128]{1,0:T(8,128)}, f32[512,128]{1,0:T(8,128)}, f32[256,128]{1,0:T(8,128)}) custom-call(s32[5]{0:T(128)} %stack.77.spot_ref, f32[3072,128]{1,0:T(8,128)} %grads_ref.5, f32[256,128]{1,0:T(8,128)} %get-tuple-element.26.refs_0_, f32[256,128]{1,0:T(8,128)} %copy-done.13, f32[256,128]{1,0:T(8,128)} %copy-done.12, ...), custom_call_target="tpu_custom_call" | custom-call | tf_op jit(solution)/shard_map/solve/pallas_call | solution.py:397
  508.0 12.4 %solve.6 = (f32[512,128]{1,0:T(8,128)}, f32[512,128]{1,0:T(8,128)}, f32[512,128]{1,0:T(8,128)}, f32[256,128]{1,0:T(8,128)}) custom-call(s32[5]{0:T(128)} %stack.77.spot_ref, f32[3072,128]{1,0:T(8,128)} %grads_ref.5, f32[256,128]{1,0:T(8,128)} %get-tuple-element.32.refs_0_, f32[256,128]{1,0:T(8,128)} %copy-done.16, f32[256,128]{1,0:T(8,128)} %copy-done.15, ...), custom_call_target="tpu_custom_call" | custom-call | tf_op jit(solution)/shard_map/solve/pallas_call | solution.py:397
  525.7 2.8 solve.7
  532.4 32.6 %collective-permute-done.39 = f32[384,128]{1,0:T(8,128)S(1)} collective-permute-done((f32[384,128]{1,0:T(8,128)S(1)}, f32[384,128]{1,0:T(8,128)S(1)}, u32[]{:S(2)}, u32[]{:S(2)}) %collective-permute-start.39) | collective-permute-done | bytes 196640 | tf_op jit(solution)/shard_map/ppermute | solution.py:66
  570.3 2.1 collective-permute-done.41
  575.8 4.6 collective-permute-done.46
  581.1 6.9 %collective-permute-start.47 = (f32[4,384,128]{2,1,0:T(8,128)S(1)}, f32[4,384,128]{2,1,0:T(8,128)S(1)}, u32[]{:S(2)}, u32[]{:S(2)}) collective-permute-start(f32[4,384,128]{2,1,0:T(8,128)S(1)} %pad_maximum_fusion.2.own_ref), channel_id=1, source_target_pairs={{0,1},{1,0},{2,3},{3,2},{4,5},{5,4},{6,7},{7,6},{8,9},{9,8},{10,11... | collective-permute-start | bytes 2359304 | tf_op jit(solution)/shard_map/ppermute | solution.py:66
  590.8 2.6 place_rows.1
  593.4 9.7 %panel_solve.1 = (f32[2048,512]{1,0:T(8,128)}, f32[1024,512]{1,0:T(8,128)}, f32[128,512]{1,0:T(8,128)}) custom-call(s32[5]{0:T(128)} %stack.77.spot_ref, f32[512,512]{1,0:T(8,128)} %get-tuple-element.20.x_ref, f32[2048,512]{1,0:T(8,128)} %all-gather.3.cloned.1.call-done.rows_ref, f32[1024,512]{1,0:T(8,128)} %all-gather.5.cloned.1.call-done.cols_ref), custom_call_target="tpu_custom_call" | custom-call | tf_op jit(solution)/shard_map/panel_solve/pallas_call | solution.py:212
  603.2 8.4 %update.2.refs_0_ = f32[16384,128]{1,0:T(8,128)} custom-call(f32[8,256,1024]{2,1,0:T(8,128)} %all-to-all-done.1.block_ref, f32[2048,512]{1,0:T(8,128)} %get-tuple-element.21.row_ref, f32[1024,512]{1,0:T(8,128)} %get-tuple-element.22.col_ref), custom_call_target="tpu_custom_call" | custom-call | tf_op jit(solution)/shard_map/update/pallas_call | solution.py:260
  611.5 8.7 %update.3 = f32[16384,128]{1,0:T(8,128)} custom-call(f32[8,256,1024]{2,1,0:T(8,128)} %all-to-all-done.1.block_ref, f32[2048,512]{1,0:T(8,128)} %get-tuple-element.21.row_ref, f32[1024,512]{1,0:T(8,128)} %get-tuple-element.22.col_ref, f32[16384,128]{1,0:T(8,128)} %update.2.refs_0_), custom_call_target="tpu_custom_call", output_to_operand_aliasing={{}: (3, {})} | custom-call | tf_op jit(solution)/shard_map/update/pallas_call | solution.py:260
  (156 shorter events, 68.8 us)
Async XLA Ops:
  15.2 129.4 %all-to-all-start = ((f32[16,128,1024]{2,1,0:T(8,128)}), f32[16,128,1024]{2,1,0:T(8,128)}, u32[]{:S(2)}, u32[]{:S(2)}) async-start(f32[16,128,1024]{2,1,0:T(8,128)} %pack_tiles.1), calls=%async_computation | async-start | bytes 16777216 | tf_op jit(solution)/shard_map/all_to_all | solution.py:193
  22.3 571.2 %all-gather.5.cloned.1.call-start = ((), (), s32[]{:S(2)}) async-start(), calls=%async_computation.3 | async-start | bytes 2359296 | tf_op jit(solution)/shard_map/all_gather | solution.py:490
  24.2 118.2 %collective-permute-start.14 = (f32[128,512]{1,0:T(8,128)S(1)}, f32[128,512]{1,0:T(8,128)S(1)}, u32[]{:S(2)}, u32[]{:S(2)}) collective-permute-start(f32[128,512]{1,0:T(8,128)S(1)} %get-tuple-element.42), channel_id=1, source_target_pairs={{0,0},{1,16},{2,1},{3,17},{4,2},{5,18},{6,3},{7,19},{8,4},{9,20},{... | collective-permute-start | bytes 786440 | tf_op jit(solution)/shard_map/ppermute | solution.py:235
  143.1 450.3 %all-gather.3.cloned.1.call-start = ((), (), s32[]{:S(2)}) async-start(), calls=%async_computation.2 | async-start | bytes 4456448 | tf_op jit(solution)/shard_map/all_gather | solution.py:491
  144.6 458.5 %all-to-all-start.1 = ((f32[8,256,1024]{2,1,0:T(8,128)}), f32[8,256,1024]{2,1,0:T(8,128)}, u32[]{:S(2)}, u32[]{:S(2)}) async-start(f32[8,256,1024]{2,1,0:T(8,128)} %bitcast.6), calls=%async_computation.1 | async-start | bytes 16777216 | tf_op jit(solution)/shard_map/all_to_all | solution.py:194
  177.6 104.7 %collective-permute-start.15 = (f32[128,512]{1,0:T(8,128)S(1)}, f32[128,512]{1,0:T(8,128)S(1)}, u32[]{:S(2)}, u32[]{:S(2)}) collective-permute-start(f32[128,512]{1,0:T(8,128)S(1)} %get-tuple-element.42), channel_id=1, source_target_pairs={{0,16},{1,17},{2,18},{3,19},{4,20},{5,21},{6,22},{7,23}} | collective-permute-start | bytes 786440 | tf_op jit(solution)/shard_map/ppermute | solution.py:66
  184.1 105.2 %collective-permute-start.26 = (f32[256,512]{1,0:T(8,128)S(1)}, f32[256,512]{1,0:T(8,128)}, u32[]{:S(2)}, u32[]{:S(2)}) collective-permute-start(f32[256,512]{1,0:T(8,128)S(1)} %get-tuple-element.44), channel_id=1, source_target_pairs={{16,20},{17,21},{18,22},{19,23}} | collective-permute-start | bytes 1572872 | tf_op jit(solution)/shard_map/ppermute | solution.py:66
  185.6 98.3 %collective-permute-start.1 = (f32[32,512]{1,0:T(8,128)S(1)}, f32[32,512]{1,0:T(8,128)S(1)}, u32[]{:S(2)}, u32[]{:S(2)}) collective-permute-start(f32[32,512]{1,0:T(8,128)S(1)} %get-tuple-element.52), channel_id=1, source_target_pairs={{0,64},{1,65},{2,66},{3,67}} | collective-permute-start | bytes 196616 | tf_op jit(solution)/shard_map/ppermute | solution.py:66
  186.9 99.5 %collective-permute-start.2 = (f32[32,512]{1,0:T(8,128)S(1)}, f32[32,512]{1,0:T(8,128)S(1)}, u32[]{:S(2)}, u32[]{:S(2)}) collective-permute-start(f32[32,512]{1,0:T(8,128)S(1)} %get-tuple-element.53), channel_id=1, source_target_pairs={{0,96},{1,97},{2,98},{3,99}} | collective-permute-start | bytes 196616 | tf_op jit(solution)/shard_map/ppermute | solution.py:66
  188.2 102.6 %collective-permute-start.25 = (f32[256,512]{1,0:T(8,128)S(1)}, f32[256,512]{1,0:T(8,128)}, u32[]{:S(2)}, u32[]{:S(2)}) collective-permute-start(f32[256,512]{1,0:T(8,128)S(1)} %get-tuple-element.44), channel_id=1, source_target_pairs={{16,18},{17,19},{18,16},{19,17}} | collective-permute-start | bytes 1572872 | tf_op jit(solution)/shard_map/ppermute | solution.py:66
  282.3 9.7 %collective-permute-start.27 = (f32[256,512]{1,0:T(8,128)S(1)}, f32[256,512]{1,0:T(8,128)}, u32[]{:S(2)}, u32[]{:S(2)}) collective-permute-start(f32[256,512]{1,0:T(8,128)S(1)} %get-tuple-element.44), channel_id=1, source_target_pairs={{16,22},{17,23},{18,20},{19,21}} | collective-permute-start | bytes 1572872 | tf_op jit(solution)/shard_map/ppermute | solution.py:66
  286.3 59.4 %collective-permute-start.22 = (f32[256,512]{1,0:T(8,128)}, f32[256,512]{1,0:T(8,128)}, u32[]{:S(2)}, u32[]{:S(2)}) collective-permute-start(f32[256,512]{1,0:T(8,128)} %get-tuple-element.48), channel_id=1, source_target_pairs={{16,20},{17,21},{18,22},{19,23},{20,16},{21,17},{22,18},{23,19}} | collective-permute-start | bytes 1572872 | tf_op jit(solution)/shard_map/ppermute | solution.py:66
  287.8 59.3 %collective-permute-start.21 = (f32[256,512]{1,0:T(8,128)}, f32[256,512]{1,0:T(8,128)}, u32[]{:S(2)}, u32[]{:S(2)}) collective-permute-start(f32[256,512]{1,0:T(8,128)} %get-tuple-element.48), channel_id=1, source_target_pairs={{16,18},{17,19},{18,16},{19,17},{20,22},{21,23},{22,20},{23,21}} | collective-permute-start | bytes 1572872 | tf_op jit(solution)/shard_map/ppermute | solution.py:66
  289.3 59.9 %collective-permute-start.23 = (f32[256,512]{1,0:T(8,128)}, f32[256,512]{1,0:T(8,128)}, u32[]{:S(2)}, u32[]{:S(2)}) collective-permute-start(f32[256,512]{1,0:T(8,128)} %get-tuple-element.48), channel_id=1, source_target_pairs={{16,22},{17,23},{18,20},{19,21},{20,18},{21,19},{22,16},{23,17}} | collective-permute-start | bytes 1572872 | tf_op jit(solution)/shard_map/ppermute | solution.py:66
  290.8 63.3 %collective-permute-start.5 = (f32[32,512]{1,0:T(8,128)S(1)}, f32[32,512]{1,0:T(8,128)S(1)}, u32[]{:S(2)}, u32[]{:S(2)}) collective-permute-start(f32[32,512]{1,0:T(8,128)S(1)} %slice_select_fusion), channel_id=1, source_target_pairs={{0,24},{1,25},{2,26},{3,27},{32,56},{33,57},{34,58},{35,59},{64,88... | collective-permute-start | bytes 196616 | tf_op jit(solution)/shard_map/ppermute | solution.py:66
  292.1 62.0 %collective-permute-start.4 = (f32[32,512]{1,0:T(8,128)S(1)}, f32[32,512]{1,0:T(8,128)S(1)}, u32[]{:S(2)}, u32[]{:S(2)}) collective-permute-start(f32[32,512]{1,0:T(8,128)S(1)} %slice_select_fusion), channel_id=1, source_target_pairs={{0,16},{1,17},{2,18},{3,19},{32,48},{33,49},{34,50},{35,51},{64,80... | collective-permute-start | bytes 196616 | tf_op jit(solution)/shard_map/ppermute | solution.py:66
  345.8 8.3 %collective-permute-start.3 = (f32[32,512]{1,0:T(8,128)S(1)}, f32[32,512]{1,0:T(8,128)S(1)}, u32[]{:S(2)}, u32[]{:S(2)}) collective-permute-start(f32[32,512]{1,0:T(8,128)S(1)} %slice_select_fusion), channel_id=1, source_target_pairs={{0,8},{1,9},{2,10},{3,11},{32,40},{33,41},{34,42},{35,43},{64,72},... | collective-permute-start | bytes 196616 | tf_op jit(solution)/shard_map/ppermute | solution.py:66
  347.1 132.5 %collective-permute-start.28 = (f32[4,256,512]{2,1,0:T(8,128)S(1)}, f32[4,256,512]{2,1,0:T(8,128)}, u32[]{:S(2)}, u32[]{:S(2)}) collective-permute-start(f32[4,256,512]{2,1,0:T(8,128)S(1)} %pad_maximum_fusion.1.tie_own_ref), channel_id=1, source_target_pairs={{16,17},{17,16},{18,19},{19,18},{20,21},{21,20},{22,23},{23,22}} | collective-permute-start | bytes 6291464 | tf_op jit(solution)/shard_map/ppermute | solution.py:66
  352.1 128.2 %collective-permute-start.24 = (f32[4,256,512]{2,1,0:T(8,128)}, f32[4,256,512]{2,1,0:T(8,128)}, u32[]{:S(2)}, u32[]{:S(2)}) collective-permute-start(f32[4,256,512]{2,1,0:T(8,128)} %pad_maximum_fusion.own_ref), channel_id=1, source_target_pairs={{16,17},{17,16},{18,19},{19,18},{20,21},{21,20},{22,23},{23,22}} | collective-permute-start | bytes 6291464 | tf_op jit(solution)/shard_map/ppermute | solution.py:66
  364.8 22.9 %collective-permute-start.29 = (f32[128,512]{1,0:T(8,128)}, f32[128,512]{1,0:T(8,128)S(1)}, u32[]{:S(2)}, u32[]{:S(2)}) collective-permute-start(f32[128,512]{1,0:T(8,128)} %get-tuple-element.40), channel_id=1, source_target_pairs={{8,16},{9,17},{10,18},{11,19},{12,20},{13,21},{14,22},{15,23}} | collective-permute-start | bytes 786440 | tf_op jit(solution)/shard_map/ppermute | solution.py:66
  366.9 123.3 %collective-permute-start.31 = (f32[128,2560]{1,0:T(8,128)S(1)}, f32[128,2560]{1,0:T(8,128)}, u32[]{:S(2)}, u32[]{:S(2)}) collective-permute-start(f32[128,2560]{1,0:T(8,128)S(1)} %slice.43.refs_12_.refs_13_), channel_id=1, source_target_pairs={{16,17},{17,16},{18,19},{19,18},{20,21},{21,20},{22,23},{23,22}} | collective-permute-start | bytes 3932168 | tf_op jit(solution)/shard_map/ppermute | solution.py:66
  368.7 28.5 %collective-permute-start.12 = (f32[4,32,512]{2,1,0:T(8,128)S(1)}, f32[4,32,512]{2,1,0:T(8,128)S(1)}, u32[]{:S(2)}, u32[]{:S(2)}) collective-permute-start(f32[4,32,512]{2,1,0:T(8,128)S(1)} %pad_maximum_fusion.6.refs_0_), channel_id=1, source_target_pairs={{0,96},{1,97},{2,98},{3,99},{4,100},{5,101},{6,102},{7,103},{8,104... | collective-permute-start | bytes 786440 | tf_op jit(solution)/shard_map/ppermute | solution.py:66
  387.7 20.5 %collective-permute-start.11 = (f32[4,32,512]{2,1,0:T(8,128)S(1)}, f32[4,32,512]{2,1,0:T(8,128)S(1)}, u32[]{:S(2)}, u32[]{:S(2)}) collective-permute-start(f32[4,32,512]{2,1,0:T(8,128)S(1)} %pad_maximum_fusion.6.refs_0_), channel_id=1, source_target_pairs={{0,64},{1,65},{2,66},{3,67},{4,68},{5,69},{6,70},{7,71},{8,72},{9,... | collective-permute-start | bytes 786440 | tf_op jit(solution)/shard_map/ppermute | solution.py:66
  397.2 16.1 %collective-permute-start.10 = (f32[4,32,512]{2,1,0:T(8,128)S(1)}, f32[4,32,512]{2,1,0:T(8,128)S(1)}, u32[]{:S(2)}, u32[]{:S(2)}) collective-permute-start(f32[4,32,512]{2,1,0:T(8,128)S(1)} %pad_maximum_fusion.6.refs_0_), channel_id=1, source_target_pairs={{0,32},{1,33},{2,34},{3,35},{4,36},{5,37},{6,38},{7,39},{8,40},{9,... | collective-permute-start | bytes 786440 | tf_op jit(solution)/shard_map/ppermute | solution.py:66
  408.2 82.0 %collective-permute-start.30 = (f32[128,1536]{1,0:T(8,128)}, f32[128,1536]{1,0:T(8,128)}, u32[]{:S(2)}, u32[]{:S(2)}) collective-permute-start(f32[128,1536]{1,0:T(8,128)} %constant_dynamic-update-slice_fusion.refs_11_), channel_id=1, source_target_pairs={{16,17},{17,16},{18,19},{19,18},{20,21},{21,20},{22,23},{23,22}} | collective-permute-start | bytes 2359304 | tf_op jit(solution)/shard_map/ppermute | solution.py:66
  414.1 59.7 %collective-permute-start.17 = (f32[256,512]{1,0:T(8,128)}, f32[256,512]{1,0:T(8,128)}, u32[]{:S(2)}, u32[]{:S(2)}) collective-permute-start(f32[256,512]{1,0:T(8,128)} %get-tuple-element.49.own_ref), channel_id=1, source_target_pairs={{16,17},{17,16},{18,19},{19,18},{20,21},{21,20},{22,23},{23,22}} | collective-permute-start | bytes 1572872 | tf_op jit(solution)/shard_map/ppermute | solution.py:66
  478.9 11.3 %collective-permute-start.20 = (f32[256,128]{1,0:T(8,128)}, f32[256,128]{1,0:T(8,128)S(1)}, u32[]{:S(2)}, u32[]{:S(2)}) collective-permute-start(f32[256,128]{1,0:T(8,128)} %get-tuple-element.26.refs_0_), channel_id=1, source_target_pairs={{16,22},{17,23},{18,20},{19,21},{20,18},{21,19},{22,16},{23,17}} | collective-permute-start | bytes 393224 | tf_op jit(solution)/shard_map/ppermute | solution.py:66
  479.6 10.6 %collective-permute-start.19 = (f32[256,128]{1,0:T(8,128)}, f32[256,128]{1,0:T(8,128)S(1)}, u32[]{:S(2)}, u32[]{:S(2)}) collective-permute-start(f32[256,128]{1,0:T(8,128)} %get-tuple-element.26.refs_0_), channel_id=1, source_target_pairs={{16,20},{17,21},{18,22},{19,23},{20,16},{21,17},{22,18},{23,19}} | collective-permute-start | bytes 393224 | tf_op jit(solution)/shard_map/ppermute | solution.py:66
  480.3 9.9 %collective-permute-start.18 = (f32[256,128]{1,0:T(8,128)}, f32[256,128]{1,0:T(8,128)S(1)}, u32[]{:S(2)}, u32[]{:S(2)}) collective-permute-start(f32[256,128]{1,0:T(8,128)} %get-tuple-element.26.refs_0_), channel_id=1, source_target_pairs={{16,18},{17,19},{18,16},{19,17},{20,22},{21,23},{22,20},{23,21}} | collective-permute-start | bytes 393224 | tf_op jit(solution)/shard_map/ppermute | solution.py:66
  530.2 34.9 %collective-permute-start.39 = (f32[384,128]{1,0:T(8,128)S(1)}, f32[384,128]{1,0:T(8,128)S(1)}, u32[]{:S(2)}, u32[]{:S(2)}) collective-permute-start(f32[384,128]{1,0:T(8,128)S(1)} %constant_dynamic-slice_fusion), channel_id=1, source_target_pairs={{16,0},{17,1},{18,2},{19,3},{20,4},{21,5},{22,6},{23,7}} | collective-permute-start | bytes 589832 | tf_op jit(solution)/shard_map/ppermute | solution.py:66
  531.5 33.6 %collective-permute-start.38 = (f32[384,128]{1,0:T(8,128)S(1)}, f32[384,128]{1,0:T(8,128)S(1)}, u32[]{:S(2)}, u32[]{:S(2)}) collective-permute-start(f32[384,128]{1,0:T(8,128)S(1)} %constant_dynamic-slice_fusion), channel_id=1, source_target_pairs={{16,24},{17,25},{18,26},{19,27},{20,28},{21,29},{22,30},{23,31}} | collective-permute-start | bytes 589832 | tf_op jit(solution)/shard_map/ppermute | solution.py:66
  581.1 8.9 %collective-permute-start.47 = (f32[4,384,128]{2,1,0:T(8,128)S(1)}, f32[4,384,128]{2,1,0:T(8,128)S(1)}, u32[]{:S(2)}, u32[]{:S(2)}) collective-permute-start(f32[4,384,128]{2,1,0:T(8,128)S(1)} %pad_maximum_fusion.2.own_ref), channel_id=1, source_target_pairs={{0,1},{1,0},{2,3},{3,2},{4,5},{5,4},{6,7},{7,6},{8,9},{9,8},{10,11... | collective-permute-start | bytes 2359304 | tf_op jit(solution)/shard_map/ppermute | solution.py:66
  (41 other events, 282.1 us)
Sparse Core Ops, SparseCore 0:
  143.3 142.0 all-gather.4
  287.0 37.0 all-gather.2
